TPU v7x, 32 devices: a whole 2x2x4 slice. The times are simulated.
32 devices in a mesh: section: 2 (over core), ctx: 4 (over y, x), shard: 4 (over z).
Axes of the slice: x: 2, y: 2, z: 4, core: 2. Of those that a mesh axis runs over, the one named last changes fastest.
Arguments:
- inputs: bfloat16 [2, 1024, 2048], P(None, ('ctx', 'shard')), may hold values from -6 to 6
- cotangent: bfloat16 [2, 1024, 2048], P(None, ('ctx', 'shard')), may hold values from -6 to 6
- doc_lengths: int32 [2, 4], replicated, may hold values from 1 to 512, 1024 in all within a row
- norm_in: float32 [2, 2048], P('section'), may hold values from 0.5 to 1.5
- w_query: bfloat16 [2, 2048, 1024], P('section', None, 'shard'), may hold values from -0.125 to 0.125
- w_keyval: bfloat16 [2, 2048, 2, 256], P('section'), may hold values from -0.125 to 0.125
- w_attn_out: bfloat16 [2, 1024, 2048], P('section', 'shard'), may hold values from -0.75 to 0.75
- w_mixer_in: bfloat16 [2, 2048, 2, 3072], P('section', None, None, 'shard'), may hold values from -0.125 to 0.125
- w_state_io: bfloat16 [2, 2048, 512], P('section'), may hold values from -0.125 to 0.125
- w_step: bfloat16 [2, 2048, 48], P('section', None, 'shard'), may hold values from -0.125 to 0.125
- step_bias: float32 [2, 48], P('section', 'shard'), may hold values from -4 to -1
- decay_rate: float32 [2, 48], P('section', 'shard'), may hold values from 0.001 to 2
- skip_gain: float32 [2, 48], P('section', 'shard'), may hold values from 0.5 to 1.5
- w_mixer_out: bfloat16 [2, 3072, 2048], P('section', 'shard'), may hold values from -0.109375 to 0.109375
- norm_ffn: float32 [2, 2048], P('section'), may hold values from 0.5 to 1.5
- w_gate_up: bfloat16 [2, 2048, 2, 4096], P('section', None, None, 'shard'), may hold values from -0.125 to 0.125
- w_down: bfloat16 [2, 4096, 2048], P('section', 'shard'), may hold values from -0.09375 to 0.09375
Outputs:
- section_out: bfloat16 [2, 2, 1024, 2048], P('section', None, ('ctx', 'shard'))
- input_grad: float32 [2, 2, 1024, 2048], P('section', None, ('ctx', 'shard'))
- grad_norm_in: float32 [2, 2048], P('section', ('ctx', 'shard'))
- grad_query: float32 [2, 2048, 1024], P('section', 'ctx', 'shard')
- grad_keyval: float32 [2, 2048, 2, 256], P('section', ('ctx', 'shard'))
- grad_attn_out: float32 [2, 1024, 2048], P('section', 'shard', 'ctx')
- grad_mixer_in: float32 [2, 2048, 2, 3072], P('section', 'ctx', None, 'shard')
- grad_state_io: float32 [2, 2048, 512], P('section', ('ctx', 'shard'))
- grad_step: float32 [2, 2048, 48], P('section', 'ctx', 'shard')
- grad_step_bias: float32 [2, 48], P('section', 'shard')
- grad_decay: float32 [2, 48], P('section', 'shard')
- grad_skip: float32 [2, 48], P('section', 'shard')
- grad_mixer_out: float32 [2, 3072, 2048], P('section', 'shard', 'ctx')
- grad_norm_ffn: float32 [2, 2048], P('section', ('ctx', 'shard'))
- grad_gate_up: float32 [2, 2048, 2, 4096], P('section', 'ctx', None, 'shard')
- grad_down: float32 [2, 4096, 2048], P('section', 'shard', 'ctx')
Inputs may be any that keep to these rules, and one draw needn't show every extreme that they name: Each row of doc_lengths sums to 1024.
All inputs are finite; a program needn't handle non-finite values.
Results may differ from a plain program's by a relative error of at most 0.025.
Values may be sent and summed in bfloat16 or wider, within the bound.
A program may use at most 320 MiB of HBM per device.

v0:
```python
import functools
import types

import jax
import jax.numpy as jnp
from jax import lax
from jax.experimental import pallas as pl
from jax.experimental.pallas import tpu as pltpu
from jax.sharding import PartitionSpec as P

SECTION, CTX, SHARD = "section", "ctx", "shard"
QH = 8
KVH = 2
HD = 128
HP = 64
CHUNKS = 16
LAG = 3

MESH = pl.DeviceIdType.MESH
eps = 1e-05
bf16 = jnp.bfloat16
f32 = jnp.float32


def line_sum(n, chunks, lag, p_rows, done, sr, sl, rr, rl, srs, sls, rrs, rls, tot, fill=None):
    z = lax.axis_index(SHARD)
    hasr, hasl = z < n - 1, z > 0
    bar = pltpu.get_barrier_semaphore()
    more = 0
    if fill is not None:
        more = fill.greet(bar)

    @pl.when(hasr)
    def _():
        pl.semaphore_signal(bar, inc=1, device_id={SHARD: z + 1}, device_id_type=MESH)

    @pl.when(hasl)
    def _():
        pl.semaphore_signal(bar, inc=1, device_id={SHARD: z - 1}, device_id_type=MESH)

    @pl.when(hasl & hasr)
    def _():
        pl.semaphore_wait(bar, 2 + more)

    @pl.when(jnp.logical_not(hasl & hasr))
    def _():
        pl.semaphore_wait(bar, 1 + more)

    def right(j):
        return pltpu.make_async_remote_copy(
            sr.at[j], rr.at[j], srs.at[j], rrs.at[j], device_id={SHARD: z + 1}, device_id_type=MESH
        )

    def left(j):
        return pltpu.make_async_remote_copy(
            sl.at[j], rl.at[j], sls.at[j], rls.at[j], device_id={SHARD: z - 1}, device_id_type=MESH
        )

    steps = chunks + lag * (n - 1)
    if fill is not None:
        fill.start()

    def one(i, _):
        def go(j, copy, came, goes, inbox, outbox):
            live = (j >= 0) & (j < chunks)

            @pl.when(live & came & goes)
            def _():
                copy(j).wait_recv()
                outbox[j] = (p_rows(j) + inbox[j].astype(f32)).astype(bf16)
                copy(j).start()

            @pl.when(live & jnp.logical_not(came))
            def _():
                outbox[j] = p_rows(j).astype(bf16)
                copy(j).start()

            @pl.when(live & jnp.logical_not(goes))
            def _():
                copy(j).wait_recv()

        go(i - lag * z, right, hasl, hasr, rr, sr)
        go(i - lag * (n - 1 - z), left, hasr, hasl, rl, sl)
        jd = i - lag * jnp.maximum(z, n - 1 - z)

        @pl.when((jd >= 0) & (jd < chunks))
        def _():
            tot[...] = p_rows(jd)

            @pl.when(hasl)
            def _():
                tot[...] += rr[jd].astype(f32)

            @pl.when(hasr)
            def _():
                tot[...] += rl[jd].astype(f32)

            done(jd, tot[...])

        if fill is not None:
            fill.step(i, steps)
        return 0

    lax.fori_loop(0, steps, one, 0)
    if fill is not None:
        fill.finish()

    def drain(j, _):
        @pl.when(hasr)
        def _():
            right(j).wait_send()

        @pl.when(hasl)
        def _():
            left(j).wait_send()

        return 0

    lax.fori_loop(0, chunks, drain, 0)


def row_slice(j, rows):
    return pl.ds(pl.multiple_of(j * rows, rows), rows)


def middle_kernel(n, chunks, lag, p_ref, h_ref, gain_ref, mid_ref, low_ref, *scratch, fill=None):
    rows = p_ref.shape[0] // chunks

    def p_rows(j):
        return p_ref[row_slice(j, rows), :]

    def done(j, total):
        v = h_ref[row_slice(j, rows), :] + total
        r = lax.rsqrt(jnp.mean(v * v, axis=-1, keepdims=True) + eps)
        mid_ref[row_slice(j, rows), :] = v
        low_ref[row_slice(j, rows), :] = (v * r * gain_ref[...]).astype(bf16)

    line_sum(n, chunks, lag, p_rows, done, *scratch, fill=fill)


class Copies:
    parts = 16

    def __init__(self, layers, own, other, out, boxes, came, went):
        self.layers, self.own, self.other, self.out = layers, own, other, out
        self.boxes, self.came, self.went = boxes, came, went

    def greet(self, bar):
        return 0

    def start(self):
        pass

    def rows(self, a, j):
        size = self.boxes[a].shape[1]
        return pl.ds(pl.multiple_of(j * size, size), size)

    def fetch(self, a, j, act):
        section, slot = lax.axis_index(SECTION), lax.rem(j, 2)
        for mine, source in ((True, self.own[a]), (False, self.other[a])):

            @pl.when((section == self.layers[a]) == mine)
            def _():
                part = source.at[self.rows(a, j), :]
                act(
                    pltpu.make_async_copy(
                        part, self.boxes[a].at[slot], self.came.at[2 * a + slot]
                    )
                )

    def store(self, a, j):
        slot = lax.rem(j, 2)
        part = self.out[a].at[self.rows(a, j), :]
        return pltpu.make_async_copy(self.boxes[a].at[slot], part, self.went.at[2 * a + slot])

    def step(self, i, steps):
        @pl.when((i >= 1) & (i <= self.parts))
        def _():
            for a in range(len(self.layers)):
                self.fetch(a, i - 1, lambda copy: copy.wait())
                self.store(a, i - 1).start()

        @pl.when((i >= 2) & (i < self.parts))
        def _():
            for a in range(len(self.layers)):
                self.store(a, i - 2).wait()

        @pl.when(i < self.parts)
        def _():
            for a in range(len(self.layers)):
                self.fetch(a, i, lambda copy: copy.start())

    def finish(self):
        for a in range(len(self.layers)):
            for j in (self.parts - 2, self.parts - 1):
                self.store(a, j).wait()


def copying(kernel, layers, n, chunks, lag, p_ref, h_ref, gain_ref, *refs):
    count = len(layers)
    own, other, refs = refs[:count], refs[count : 2 * count], refs[2 * count :]
    first_ref, low_ref, refs = refs[0], refs[1], refs[2:]
    out, refs = refs[:count], refs[count:]
    copies = Copies(layers, own, other, out, refs[9 : 9 + count], *refs[9 + count :])
    kernel(n, chunks, lag, p_ref, h_ref, gain_ref, first_ref, low_ref, *refs[:9], fill=copies)


def layer_end_kernel(n, chunks, lag, p_ref, h_ref, gain_ref, out_ref, low_ref, *scratch, fill=None):
    rows = p_ref.shape[0] // chunks

    def p_rows(j):
        return p_ref[row_slice(j, rows), :]

    def done(j, total):
        out = (h_ref[row_slice(j, rows), :] + total).astype(bf16)
        out_ref[row_slice(j, rows), :] = out
        v = out.astype(f32)
        r = lax.rsqrt(jnp.mean(v * v, axis=-1, keepdims=True) + eps)
        low_ref[row_slice(j, rows), :] = (v * r * gain_ref[...]).astype(bf16)

    line_sum(n, chunks, lag, p_rows, done, *scratch, fill=fill)


def flipped(place, k, count):
    total, bit = 0, 1
    while bit < count:
        total = total + (place // bit + k // bit) % 2 * bit
        bit *= 2
    return total


def mirrored(k, count):
    total, bit = 0, 1
    while bit < count:
        total = total + k // bit % 2 * (count // (2 * bit))
        bit *= 2
    return total


class Fill:
    first = 6

    def __init__(self, plan, xs, ys, outs, scratch):
        self.plan, self.xs, self.ys, self.outs = plan, xs, ys, outs
        count = len(plan)
        self.other_x, rest = scratch[: len(xs)], scratch[len(xs) :]
        self.own_y, self.other_y = rest[:count], rest[count : 2 * count]
        self.send, self.recv = rest[2 * count :]

    def greet(self, bar):
        other = 1 - lax.axis_index(SECTION)
        pl.semaphore_signal(bar, inc=1, device_id={SECTION: other}, device_id_type=MESH)
        return 1

    def copies(self):
        section = lax.axis_index(SECTION)
        copies = []

        def add(source, target):
            i = len(copies)
            copies.append(
                pltpu.make_async_remote_copy(
                    source,
                    target,
                    self.send.at[i],
                    self.recv.at[i],
                    device_id={SECTION: 1 - section},
                    device_id_type=MESH,
                )
            )

        for x, target in zip(self.xs, self.other_x):
            add(x, target)
        for (_, _, parts), target in zip(self.plan, self.other_y):
            at = 0
            for y, low, high, width in parts:
                start = pl.multiple_of(low + (high - low) * (1 - section), 128)
                add(self.ys[y].at[:, pl.ds(start, width)], target.at[:, at : at + width])
                at += width
        return copies

    def start(self):
        for copy in self.copies():
            copy.start()
        section = lax.axis_index(SECTION)
        for (_, _, parts), own in zip(self.plan, self.own_y):
            at = 0
            for y, low, high, width in parts:
                start = pl.multiple_of(low + (high - low) * section, 128)
                own[:, at : at + width] = self.ys[y][:, pl.ds(start, width)]
                at += width

    def step(self, i, steps):
        place, count = lax.axis_index(CTX), lax.axis_size(CTX)

        @pl.when(i == self.first)
        def _():
            for copy in self.copies():
                copy.wait_recv()

        each = -(-count * len(self.plan) // (steps - self.first))
        begin = (i - self.first) * each

        def piece(t, _):
            at = [0, 0]
            for f, (x, stream, _) in enumerate(self.plan):
                k = t - f * count
                width = self.own_y[f].shape[1]
                where = slice(at[stream], at[stream] + width)
                at[stream] += width
                kept, sent = self.outs[2 * stream : 2 * stream + 2]

                @pl.when((k >= 0) & (k < count))
                def _():
                    block = kept.shape[1]
                    source = flipped(place, mirrored(k, count) if stream else k, count)
                    cols = pl.ds(pl.multiple_of(source * block, block), block)
                    dims = (((0,), (0,)), ((), ()))
                    total = lax.dot_general(
                        self.xs[x][:, cols], self.own_y[f][...], dims, preferred_element_type=f32
                    ) + lax.dot_general(
                        self.other_x[x][:, cols],
                        self.other_y[f][...],
                        dims,
                        preferred_element_type=f32,
                    )
                    low = total.astype(bf16)

                    @pl.when(k < count // 2)
                    def _():
                        kept[k, :, where] = low

                    @pl.when(k >= count // 2)
                    def _():
                        sent[k - count // 2, :, where] = low

            return 0

        @pl.when(i >= self.first)
        def _():
            lax.fori_loop(begin, begin + each, piece, 0)

    def finish(self):
        for copy in self.copies():
            copy.wait_send()


class Scatter:
    def __init__(self, blocks, out, inbox, send, recv):
        self.blocks, self.out, self.inbox, self.send, self.recv = blocks, out, inbox, send, recv
        self.count, self.place = lax.axis_size(CTX), lax.axis_index(CTX)

    def peer(self, k):
        return flipped(self.place, k, self.count)

    def copy(self, k):
        return pltpu.make_async_remote_copy(
            self.blocks.at[k],
            self.inbox.at[k],
            self.send.at[k],
            self.recv.at[k],
            device_id={CTX: self.peer(k)},
            device_id_type=MESH,
        )

    def greet(self, bar):
        for k in range(1, self.count):
            pl.semaphore_signal(bar, inc=1, device_id={CTX: self.peer(k)}, device_id_type=MESH)
        return self.count - 1

    def start(self):
        for k in reversed(range(1, self.count)):
            self.copy(k).start()

    def step(self, i, steps):
        pass

    def finish(self):
        rows = 64

        for k in range(1, self.count):
            self.copy(k).wait_recv()

        def add(j, _):
            part = row_slice(j, rows)
            total = self.blocks[0, part, :].astype(f32)
            for k in range(1, self.count):
                total += self.inbox[k, part, :].astype(f32)
            self.out[part, :] = total.astype(bf16)
            return 0

        lax.fori_loop(0, self.out.shape[0] // rows, add, 0)
        for k in range(1, self.count):
            self.copy(k).wait_send()


class Halving:
    cuts = 2
    turns = (11, 20)

    def __init__(self, streams, outs, scratch):
        self.place, self.count = lax.axis_index(CTX), lax.axis_size(CTX)
        self.streams, self.outs = streams, outs
        self.orders = ctx_orders()
        self.levels = len(self.orders[0])
        self.inbox = [scratch[k * self.levels : (k + 1) * self.levels] for k in range(2)]
        rest = scratch[2 * self.levels :]
        self.sums = [rest[k * (self.levels - 1) : (k + 1) * (self.levels - 1)] for k in range(2)]
        self.send, self.recv = rest[2 * (self.levels - 1) :]

    def greet(self, bar):
        for bit in self.orders[0]:
            peer = flipped(self.place, bit, self.count)
            pl.semaphore_signal(bar, inc=1, device_id={CTX: peer}, device_id_type=MESH)
        return self.levels

    def rows(self, cut):
        size = self.outs[0].shape[0] // self.cuts
        return pl.ds(cut * size, size)

    def copy(self, level, stream, cut):
        rows = self.rows(cut)
        if level == 0:
            source = self.streams[2 * stream + 1].at[:, rows, :]
        else:
            blocks = self.count >> (level + 1)
            source = self.sums[stream][level - 1].at[pl.ds(blocks, blocks), rows, :]
        i = (level * 2 + stream) * self.cuts + cut
        return pltpu.make_async_remote_copy(
            source,
            self.inbox[stream][level].at[:, rows, :],
            self.send.at[i],
            self.recv.at[i],
            device_id={CTX: flipped(self.place, self.orders[stream][level], self.count)},
            device_id_type=MESH,
        )

    def advance(self, level, cut):
        rows, blocks = self.rows(cut), self.count >> (level + 1)
        for stream in range(2):
            self.copy(level, stream, cut).wait_recv()
            kept = self.streams[2 * stream] if level == 0 else self.sums[stream][level - 1]
            for k in range(blocks):
                total = kept[k, rows, :].astype(f32) + self.inbox[stream][level][k, rows, :].astype(
                    f32
                )
                if level + 1 < self.levels:
                    self.sums[stream][level][k, rows, :] = total.astype(bf16)
                else:
                    self.outs[stream][rows, :] = total.astype(bf16)
            if level + 1 < self.levels:
                self.copy(level + 1, stream, cut).start()

    def start(self):
        for cut in range(self.cuts):
            for stream in range(2):
                self.copy(0, stream, cut).start()

    def step(self, i, steps):
        for cut, turn in enumerate(self.turns):

            @pl.when(i == turn)
            def _():
                self.advance(0, cut)

    def finish(self):
        for level in range(1, self.levels):
            for cut in range(self.cuts):
                self.advance(level, cut)
        for level in range(self.levels):
            for stream in range(2):
                for cut in range(self.cuts):
                    self.copy(level, stream, cut).wait_send()


def halving_scratch(streams):
    blocks, rows, width = streams[0].shape
    levels = len(ctx_bits())
    inbox = [pltpu.VMEM((blocks >> k, rows, width), bf16) for k in range(levels)]
    copies = levels * 2 * Halving.cuts
    return [*inbox * 2, *inbox[: levels - 1] * 2, *[pltpu.SemaphoreType.DMA((copies,))] * 2]


class Together:
    def __init__(self, *jobs):
        self.jobs = jobs

    def greet(self, bar):
        return sum(job.greet(bar) for job in self.jobs)

    def start(self):
        for job in self.jobs:
            job.start()

    def step(self, i, steps):
        for job in self.jobs:
            job.step(i, steps)

    def finish(self):
        for job in self.jobs:
            job.finish()


def scatter_kernel(n, chunks, lag, p_ref, q_ref, d_ref, v_ref, gain_ref, blocks, *refs):
    outs, out, scratch = refs[:4], refs[4], refs[5:]
    job = Scatter(blocks, out, *scratch[9:])
    back_rows(n, chunks, lag, p_ref, d_ref, v_ref, gain_ref, *outs[:3], scratch[:9], job, q_ref, outs[3])


def back_kernel(n, chunks, lag, plan, x_count, y_count, beside, ready, p_ref, *refs):
    q_ref = q_out = None
    if beside:
        q_ref, refs = refs[0], refs[1:]
    (d_ref, v_ref, gain_ref), refs = refs[:3], refs[3:]
    xs, refs = refs[:x_count], refs[x_count:]
    ys, refs = refs[:y_count], refs[y_count:]
    streams, refs = refs[:ready], refs[ready:]
    out_ref, low_ref, gg_ref = refs[:3]
    refs = refs[3:]
    if beside:
        q_out, refs = refs[0], refs[1:]
    sums, refs = refs[:4], refs[4:]
    totals, refs = refs[: ready // 2], refs[ready // 2 :]
    cut = len(xs) + 2 * len(plan) + 2
    fill = Fill(plan, xs, ys, sums, refs[9 : 9 + cut])
    if ready:
        fill = Together(fill, Halving(streams, totals, refs[9 + cut :]))
    outs = out_ref, low_ref, gg_ref
    back_rows(n, chunks, lag, p_ref, d_ref, v_ref, gain_ref, *outs, refs[:9], fill, q_ref, q_out)


def back_rows(
    n,
    chunks,
    lag,
    p_ref,
    d_ref,
    v_ref,
    gain_ref,
    out_ref,
    low_ref,
    gg_ref,
    scratch,
    fill,
    q_ref=None,
    q_out=None,
):
    rows, width = p_ref.shape[0] // chunks, p_ref.shape[1]
    gg_ref[...] = jnp.zeros_like(gg_ref)

    def p_rows(j):
        part = row_slice(j, rows)
        if q_ref is None:
            return p_ref[part, :]
        return jnp.concatenate([p_ref[part, :], q_ref[part, :].astype(f32)], axis=1)

    def done(j, total):
        if q_ref is not None:
            q_out[row_slice(j, rows), :] = total[:, width:].astype(bf16)
            total = total[:, :width]
        v = v_ref[row_slice(j, rows), :].astype(f32)
        r = lax.rsqrt(jnp.mean(v * v, axis=-1, keepdims=True) + eps)
        vr = v * r
        dg = total * gain_ref[...]
        inner = jnp.mean(dg * vr, axis=-1, keepdims=True)
        gg_ref[...] += jnp.sum((total * vr).reshape(rows // 8, 8, vr.shape[1]), axis=0)
        out = d_ref[row_slice(j, rows), :].astype(f32) + r * (dg - vr * inner)
        out_ref[row_slice(j, rows), :] = out
        low_ref[row_slice(j, rows), :] = out.astype(bf16)

    line_sum(n, chunks, lag, p_rows, done, *scratch, fill=fill)


def summed(kernel, collective, outs, *operands, extra=(), more=0, far=(0, 0)):
    n = lax.axis_size(SHARD)
    length, width = operands[0].shape[0], operands[0].shape[1] + more
    box = pltpu.VMEM((CHUNKS, length // CHUNKS, width), bf16)
    distant = pl.BlockSpec(memory_space=pl.ANY)
    whole = pl.BlockSpec(memory_space=pltpu.VMEM)
    return pl.pallas_call(
        functools.partial(kernel, n, CHUNKS, LAG),
        out_shape=outs,
        in_specs=[whole] * (len(operands) - far[0]) + [distant] * far[0],
        out_specs=[whole] * (len(outs) - far[1]) + [distant] * far[1],
        scratch_shapes=[box] * 4
        + [pltpu.SemaphoreType.DMA((CHUNKS,))] * 4
        + [pltpu.VMEM((length // CHUNKS, width), f32), *extra],
        compiler_params=pltpu.CompilerParams(
            collective_id=collective, has_side_effects=True, vmem_limit_bytes=58 << 20
        ),
        cost_estimate=pl.CostEstimate(flops=0, bytes_accessed=20 << 20, transcendentals=0),
        name="line_sum"+str(collective),
    )(*operands)


def gather_kernel(n, rows_ref, out_ref, box, send, recv):
    z = lax.axis_index(SHARD)
    part = rows_ref.shape[0]
    bar = pltpu.get_barrier_semaphore()

    def copy(k):
        return pltpu.make_async_remote_copy(
            rows_ref,
            box.at[k],
            send.at[k],
            recv.at[k],
            device_id={SHARD: lax.rem(z + k, n)},
            device_id_type=MESH,
        )

    for k in range(1, n):
        pl.semaphore_signal(bar, inc=1, device_id={SHARD: lax.rem(z + k, n)}, device_id_type=MESH)
    pl.semaphore_wait(bar, n - 1)
    for k in range(1, n):
        copy(k).start()
    out_ref[row_slice(z, part), :] = rows_ref[...]
    for k in range(1, n):
        copy(k).wait_recv()
        out_ref[row_slice(lax.rem(z + n - k, n), part), :] = box[k]
    for k in range(1, n):
        copy(k).wait_send()


def line_gather(rows):
    n = lax.axis_size(SHARD)
    whole = pl.BlockSpec(memory_space=pltpu.VMEM)
    return pl.pallas_call(
        functools.partial(gather_kernel, n),
        out_shape=jax.ShapeDtypeStruct((n * rows.shape[0], rows.shape[1]), rows.dtype),
        in_specs=[whole],
        out_specs=whole,
        scratch_shapes=[pltpu.VMEM((n,) + rows.shape, rows.dtype)]
        + [pltpu.SemaphoreType.DMA((n,))] * 2,
        compiler_params=pltpu.CompilerParams(collective_id=8, has_side_effects=True),
        name="gather",
    )(rows)


def shaped(array, dtype):
    return jax.ShapeDtypeStruct(array.shape, dtype)


def copying_sum(kernel, collective, dtype, p, hidden, gain, wanted):
    layers, own, other = zip(*wanted)
    outs = [shaped(p, dtype), shaped(p, bf16)] + [shaped(a, bf16) for a in own]
    boxes = [pltpu.VMEM((2, a.shape[0] // Copies.parts, a.shape[1]), bf16) for a in own]
    first, low, *chosen = summed(
        functools.partial(copying, kernel, layers),
        collective,
        outs,
        p,
        hidden,
        gain[None],
        *own,
        *other,
        extra=[*boxes, *[pltpu.SemaphoreType.DMA((2 * len(layers),))] * 2],
        far=(2 * len(layers), len(layers)),
    )
    return first, low, chosen


def back_sum(collective, p, d_out, values, gain, plan, xs, ys, beside=(), ready=()):
    count = lax.axis_size(CTX)
    length = p.shape[0]
    outs = [shaped(p, f32), shaped(p, bf16), jax.ShapeDtypeStruct((8, p.shape[1]), f32)]
    outs += [shaped(q, bf16) for q in beside]
    widths = [sum(part[3] for part in parts) for _, _, parts in plan]
    for stream in range(2):
        total = sum(w for (_, at, _), w in zip(plan, widths) if at == stream)
        shape = (count // 2, xs[0].shape[1] // count, total)
        outs += [jax.ShapeDtypeStruct(shape, bf16)] * 2
    extra = [pltpu.VMEM(x.shape, bf16) for x in xs]
    extra += [pltpu.VMEM((length, w), bf16) for w in widths] * 2
    copies = len(xs) + sum(len(parts) for _, _, parts in plan)
    extra += [pltpu.SemaphoreType.DMA((copies,))] * 2
    if ready:
        outs += [jax.ShapeDtypeStruct(a.shape[1:], bf16) for a in ready[::2]]
        extra += halving_scratch(ready)

    def bound(n, chunks, lag, *refs):
        back_kernel(n, chunks, lag, plan, len(xs), len(ys), bool(beside), len(ready), *refs)

    operands = (p, *beside, d_out, values, gain[None], *xs, *ys, *ready)
    more = sum(q.shape[1] for q in beside)
    out, low, gg, *sums = summed(bound, collective, outs, *operands, extra=extra, more=more)
    return out, low, jnp.sum(gg, axis=0), *sums


def back_sum_scatter(collective, p, beside, d_out, values, gain, blocks):
    outs = [shaped(p, f32), shaped(p, bf16), jax.ShapeDtypeStruct((8, p.shape[1]), f32)]
    outs += [shaped(beside, bf16), jax.ShapeDtypeStruct(blocks.shape[1:], bf16)]
    sems = [pltpu.SemaphoreType.DMA((blocks.shape[0],))] * 2
    extra = [pltpu.VMEM(blocks.shape, bf16), *sems]
    operands = (p, beside, d_out, values, gain[None], blocks)
    more = beside.shape[1]
    out, low, gg, whole, total = summed(
        scatter_kernel, collective, outs, *operands, extra=extra, more=more
    )
    return out, low, jnp.sum(gg, axis=0), whole, total


def dot(left, right, dims=((1,), (0,))):
    return lax.dot_general(left, right, (dims, ((), ())), preferred_element_type=f32)


NT = ((1,), (1,))
TN = ((0,), (0,))


def in_three(values):
    high = values.astype(bf16)
    rest = values - high.astype(f32)
    mid = rest.astype(bf16)
    return high, mid, (rest - mid.astype(f32)).astype(bf16)


def running_sum(values, reverse):
    length = values.shape[0]
    row = lax.broadcasted_iota(jnp.int32, (length, length), 0)
    col = lax.broadcasted_iota(jnp.int32, (length, length), 1)
    kept = jnp.where(row <= col if reverse else row >= col, 1.0, 0.0).astype(bf16)
    return sum(dot(kept, part) for part in in_three(values))


def lanes(shape):
    return lax.broadcasted_iota(jnp.int32, shape, 1)


def column(values, head):
    return jnp.sum(jnp.where(lanes(values.shape) == head, values, 0.0), axis=1, keepdims=True)


def in_pair(values, pair):
    low, high = column(values, 2 * pair), column(values, 2 * pair + 1)
    return jnp.where(lanes(values.shape) < HP, low, high)


def from_pair(values, pair):
    lane = lanes(values.shape)
    low = jnp.sum(jnp.where(lane < HP, values, 0.0), axis=1, keepdims=True)
    high = jnp.sum(jnp.where(lane < HP, 0.0, values), axis=1, keepdims=True)
    return jnp.where(lane == 2 * pair, low, 0.0) + jnp.where(lane == 2 * pair + 1, high, 0.0)


def pair_ds(pair, start=0):
    return pl.ds(pl.multiple_of(start + pair * 2 * HP, 2 * HP), 2 * HP)


def steps_of(step_raw, vec_ref, tok_ref, cum, cum_rows, step, enter, fade):
    shifted = step_raw + vec_ref[0:1, :]
    step[...] = jnp.maximum(shifted, 0.0) + jnp.log1p(jnp.exp(-jnp.abs(shifted)))
    cum[...] = running_sum(-step[...] * vec_ref[1:2, :], False)
    total = cum[...]
    cum_rows[...] = total.T
    enter[...] = jnp.exp(total) * tok_ref[:, 1:2]
    fade[...] = jnp.exp(total[-1:, :] - total) * tok_ref[:, 2:3]
    return shifted


def masks_of(tok_ref, key_ref):
    kept = (tok_ref[:, 3:4] >= key_ref[1:2, :]) & (tok_ref[:, 0:1] == key_ref[0:1, :])
    return jnp.where(kept, 0.0, -1e30)


def ctx_barrier(count, place):
    bar = pltpu.get_barrier_semaphore()

    def greet(k, _):
        pl.semaphore_signal(
            bar, inc=1, device_id={CTX: lax.rem(place + k, count)}, device_id_type=MESH
        )
        return 0

    lax.fori_loop(1, count, greet, 0)
    pl.semaphore_wait(bar, count - 1)


def ctx_copy(source, target, send, recv, peer):
    return pltpu.make_async_remote_copy(
        source, target, send, recv, device_id={CTX: peer}, device_id_type=MESH
    )


def mix_forward_kernel(
    count,
    widths,
    heads,
    proj_ref,
    vec_ref,
    skip_ref,
    tok_ref,
    key_ref,
    both_ref,
    mixed_ref,
    state_ref,
    keyval_ref,
    decay_ref,
    cum,
    cum_rows,
    step,
    enter,
    fade,
    mask,
    crossed,
    keyvals,
    fresh,
    decays,
    total_state,
    kv_send,
    kv_recv,
    st_send,
    st_recv,
    dc_send,
    dc_recv,
):
    place = lax.axis_index(CTX)
    length = proj_ref.shape[0]
    inner = (proj_ref.shape[1] - widths[3]) // 2
    pairs = heads // 2
    states = (widths[2] - widths[1]) // 2
    ctx_barrier(count, place)

    keyvals[0] = proj_ref[:, widths[0] : widths[1]].astype(bf16)

    def kv_copy(k):
        peer = lax.rem(place + k, count)
        return ctx_copy(keyvals.at[0], keyvals.at[k], kv_send.at[k], kv_recv.at[k], peer)

    def st_copy(k):
        peer = lax.rem(place + k, count)
        return ctx_copy(fresh.at[0], fresh.at[k], st_send.at[k], st_recv.at[k], peer)

    def dc_copy(k):
        peer = lax.rem(place + k, count)
        return ctx_copy(decays.at[0], decays.at[k], dc_send.at[k], dc_recv.at[k], peer)

    def kv_start(k, _):
        kv_copy(k).start()
        return 0

    lax.fori_loop(1, count, kv_start, 0)
    steps_of(
        proj_ref[:, widths[2] : widths[2] + 128], vec_ref, tok_ref, cum, cum_rows, step, enter, fade
    )
    last = cum_rows[: decays.shape[1], length - 1 :]
    decays[0] = jnp.broadcast_to(jnp.exp(last) * tok_ref[0:1, 4:5], decays.shape[1:])
    b_low = proj_ref[:, widths[1] : widths[1] + states].astype(bf16)
    c_low = proj_ref[:, widths[1] + states : widths[2]].astype(bf16)

    def make_fresh(pair, _):
        x = proj_ref[:, pair_ds(pair, widths[3] + inner)]
        x = x.astype(bf16).astype(f32)
        faded = (x * in_pair(fade[...] * step[...], pair)).astype(bf16)
        fresh[0, pair_ds(pair), :] = dot(faded, b_low, TN).astype(bf16)
        return 0

    lax.fori_loop(0, pairs, make_fresh, 0)

    def st_start(k, _):
        dc_copy(k).start()

        @pl.when(place + k < count)
        def _():
            st_copy(k).start()

        return 0

    lax.fori_loop(1, count, st_start, 0)
    mask[...] = masks_of(tok_ref, key_ref)
    crossed[...] = dot(c_low, b_low, NT) * states ** (-0.5)

    def inside(pair, _):
        x = proj_ref[:, pair_ds(pair, widths[3] + inner)]
        x = x.astype(bf16).astype(f32)
        xdt = (x * in_pair(step[...], pair)).astype(bf16)
        parts = []
        for side in range(2):
            head = 2 * pair + side
            spread = column(cum[...], head) - cum_rows[pl.ds(head, 1), :]
            weight = jnp.exp(spread + mask[:, :length])
            parts.append(dot((weight * crossed[...]).astype(bf16), xdt))
        mixed_ref[:, pair_ds(pair)] = jnp.where(lanes(parts[0].shape) < HP, *parts)
        return 0

    lax.fori_loop(0, pairs, inside, 0)

    def kv_wait(k, _):
        kv_copy(k).wait_recv()
        return 0

    lax.fori_loop(1, count, kv_wait, 0)
    keyval_ref[...] = keyvals[...].reshape(keyval_ref.shape)
    for head in range(widths[0] // HD):
        query = proj_ref[:, head * HD : (head + 1) * HD].astype(bf16)
        scores = dot(query, keyval_ref[:, :HD], NT) * HD ** (-0.5) + mask[...]
        expo = jnp.exp(scores - jnp.max(scores, axis=1, keepdims=True))
        soft = expo * (1.0 / jnp.sum(expo, axis=1, keepdims=True))
        both_ref[:, head * HD : (head + 1) * HD] = dot(
            soft.astype(bf16), keyval_ref[:, HD:]
        ).astype(bf16)

    def dc_wait(k, _):
        dc_copy(k).wait_recv()

        @pl.when(k <= place)
        def _():
            st_copy(k).wait_recv()

        return 0

    lax.fori_loop(1, count, dc_wait, 0)
    total_state[...] = jnp.zeros_like(total_state)
    head_width = inner // heads

    def combine(index, _):
        slot = place - index

        def one_head(head, _):
            rows = pl.ds(pl.multiple_of(head * head_width, head_width), head_width)
            total_state[rows, :] = total_state[rows, :] * decays[slot, pl.ds(head, 1), :] + fresh[
                slot, rows, :
            ].astype(f32)
            return 0

        lax.fori_loop(0, heads, one_head, 0)
        return 0

    lax.fori_loop(0, place, combine, 0)
    state_ref[...] = total_state[...].astype(bf16)
    decay_ref[...] = decays[...]

    def finish(pair, _):
        carried = dot(c_low, state_ref[pair_ds(pair), :], NT)
        mixed = mixed_ref[:, pair_ds(pair)] + carried * in_pair(enter[...], pair)
        mixed_ref[:, pair_ds(pair)] = mixed
        x = proj_ref[:, pair_ds(pair, widths[3] + inner)]
        x = x.astype(bf16).astype(f32)
        gate = proj_ref[:, pair_ds(pair, widths[3])]
        y = mixed + x * skip_ref[0:1, pair_ds(pair)]
        both_ref[:, pair_ds(pair, widths[0])] = (
            y * gate / (1.0 + jnp.exp(-gate))
        ).astype(bf16)
        return 0

    lax.fori_loop(0, pairs, finish, 0)

    def drain(k, _):
        kv_copy(k).wait_send()
        dc_copy(k).wait_send()

        @pl.when(place + k < count)
        def _():
            st_copy(k).wait_send()

        return 0

    lax.fori_loop(1, count, drain, 0)


def mix_backward_kernel(
    count,
    widths,
    heads,
    proj_ref,
    vec_ref,
    skip_ref,
    tok_ref,
    key_ref,
    mixed_ref,
    state_ref,
    keyval_ref,
    decay_ref,
    d_both_ref,
    d_proj_ref,
    d_vec_ref,
    cum,
    cum_rows,
    step,
    enter,
    fade,
    mask,
    crossed,
    d_crossed,
    d_y,
    d_carried,
    d_x,
    d_keyval,
    d_b,
    d_c,
    d_cum,
    d_step,
    d_coeff,
    d_skip,
    d_states,
    total_state,
    kv_out,
    kv_in,
    kv_send,
    kv_recv,
    st_send,
    st_recv,
):
    place = lax.axis_index(CTX)
    length = proj_ref.shape[0]
    inner = (proj_ref.shape[1] - widths[3]) // 2
    pairs = heads // 2
    head_width = inner // heads
    states = (widths[2] - widths[1]) // 2
    ctx_barrier(count, place)

    def back(k):
        return lax.rem(place + count - k, count)

    def kv_copy(k):
        return ctx_copy(kv_out.at[k], kv_in.at[k], kv_send.at[k], kv_recv.at[k], back(k))

    def st_copy(k):
        return ctx_copy(d_states.at[0], d_states.at[k], st_send.at[k], st_recv.at[k], back(k))

    shifted = steps_of(
        proj_ref[:, widths[2] : widths[2] + 128], vec_ref, tok_ref, cum, cum_rows, step, enter, fade
    )
    b_low = proj_ref[:, widths[1] : widths[1] + states].astype(bf16)
    c_low = proj_ref[:, widths[1] + states : widths[2]].astype(bf16)
    d_cum[...] = jnp.zeros_like(d_cum)
    d_step[...] = jnp.zeros_like(d_step)
    d_coeff[...] = jnp.zeros_like(d_coeff)
    d_skip[...] = jnp.zeros_like(d_skip)

    def x_of(pair):
        x = proj_ref[:, pair_ds(pair, widths[3] + inner)]
        return x.astype(bf16).astype(f32)

    def outer(pair, _):
        gate = proj_ref[:, pair_ds(pair, widths[3])]
        d_gated = d_both_ref[:, pair_ds(pair, widths[0])]
        x, mixed, skip = x_of(pair), mixed_ref[:, pair_ds(pair)], skip_ref[0:1, pair_ds(pair)]
        sig = 1.0 / (1.0 + jnp.exp(-gate))
        dy = d_gated * gate * sig
        d_gate = d_gated * (mixed + x * skip) * sig * (1.0 + gate * (1.0 - sig))
        d_proj_ref[:, pair_ds(pair, widths[3])] = d_gate.astype(bf16)
        low = dy.astype(bf16)
        d_y[:, pair_ds(pair)] = low
        d_x[:, pair_ds(pair)] = dy * skip
        d_skip[...] += from_pair(dy * x, pair)
        d_cum[...] += from_pair(low.astype(f32) * mixed, pair)
        carried = (low.astype(f32) * in_pair(enter[...], pair)).astype(bf16)
        d_carried[:, pair_ds(pair)] = carried
        d_states[0, pair_ds(pair), :] = dot(carried, c_low, TN).astype(bf16)
        return 0

    lax.fori_loop(0, pairs, outer, 0)

    def st_start(k, _):
        @pl.when(k <= place)
        def _():
            st_copy(k).start()

        return 0

    lax.fori_loop(1, count, st_start, 0)
    mask[...] = masks_of(tok_ref, key_ref)
    for head in range(widths[0] // HD):
        cols = slice(head * HD, (head + 1) * HD)
        query = proj_ref[:, cols].astype(bf16)
        scores = dot(query, keyval_ref[:, :HD], NT) * HD ** (-0.5) + mask[...]
        expo = jnp.exp(scores - jnp.max(scores, axis=1, keepdims=True))
        soft = expo * (1.0 / jnp.sum(expo, axis=1, keepdims=True))
        grad = d_both_ref[:, cols].astype(bf16)
        d_soft = dot(grad, keyval_ref[:, HD:], NT)
        d_scores = soft * (d_soft - jnp.sum(soft * d_soft, axis=1, keepdims=True))
        d_raw = (d_scores * HD ** (-0.5)).astype(bf16)
        d_proj_ref[:, cols] = dot(d_raw, keyval_ref[:, :HD]).astype(bf16)
        d_keys, d_values = dot(d_raw, query, TN), dot(soft.astype(bf16), grad, TN)
        if head == 0:
            d_keyval[:, :HD] = d_keys
            d_keyval[:, HD:] = d_values
        else:
            d_keyval[:, :HD] += d_keys
            d_keyval[:, HD:] += d_values
    kv_out[...] = d_keyval[...].astype(bf16).reshape(kv_out.shape)

    def kv_start(k, _):
        kv_copy(k).start()
        return 0

    lax.fori_loop(1, count, kv_start, 0)
    crossed[...] = dot(c_low, b_low, NT) * states ** (-0.5)
    d_crossed[...] = jnp.zeros_like(d_crossed)

    def inside(pair, _):
        x = x_of(pair)
        steps = in_pair(step[...], pair)
        xdt = (x * steps).astype(bf16)
        low = d_y[:, pair_ds(pair)]
        lane = lanes(low.shape)
        parts = []
        for side in range(2):
            head = 2 * pair + side
            spread = column(cum[...], head) - cum_rows[pl.ds(head, 1), :]
            weight = jnp.exp(spread + mask[:, :length])
            parts.append(dot((weight * crossed[...]).astype(bf16), low, TN))
            mine = (lane >= HP) if side else (lane < HP)
            alone = jnp.where(mine, low.astype(f32), 0.0).astype(bf16)
            d_crossed[...] += dot(alone, xdt, NT) * weight
        d_xdt = jnp.where(lane < HP, *parts)
        d_x[:, pair_ds(pair)] += d_xdt * steps
        d_step[...] += from_pair(d_xdt * x, pair)
        d_cum[...] -= from_pair(d_xdt * xdt.astype(f32), pair)
        return 0

    lax.fori_loop(0, pairs, inside, 0)
    low_crossed = (d_crossed[...] * states ** (-0.5)).astype(bf16)
    d_c[...] = dot(low_crossed, b_low) + dot(d_carried[...], state_ref[...])
    d_b[...] = dot(low_crossed, c_low, TN)

    def st_wait(k, _):
        @pl.when(place + k < count)
        def _():
            st_copy(k).wait_recv()

        return 0

    lax.fori_loop(1, count, st_wait, 0)
    total_state[...] = jnp.zeros_like(total_state)

    def combine(index, _):
        slot = count - 1 - place - index
        source = lax.rem(count - slot, count)

        def one_head(head, _):
            rows = pl.ds(pl.multiple_of(head * head_width, head_width), head_width)
            total_state[rows, :] = total_state[rows, :] * decay_ref[
                source, pl.ds(head, 1), :
            ] + d_states[slot, rows, :].astype(f32)
            return 0

        lax.fori_loop(0, heads, one_head, 0)
        return 0

    lax.fori_loop(0, count - 1 - place, combine, 0)
    d_vec_ref[...] = jnp.zeros_like(d_vec_ref)

    def from_later(pair, _):
        rows = pair_ds(pair)
        later = total_state[rows, :]
        low = later.astype(bf16)
        x = x_of(pair)
        coeffs = in_pair(fade[...] * step[...], pair)
        back_x = dot(b_low, low, NT)
        d_proj_ref[:, pair_ds(pair, widths[3] + inner)] = (
            d_x[:, rows] + back_x * coeffs
        ).astype(bf16)
        d_coeff[...] += from_pair(back_x * x, pair)
        d_b[...] += dot((x * coeffs).astype(bf16), low)
        product = later * state_ref[rows, :].astype(f32)
        row = lax.broadcasted_iota(jnp.int32, product.shape, 0)
        lane = lanes((1, 128))
        for side in range(2):
            mine = (row >= HP) if side else (row < HP)
            part = jnp.sum(jnp.where(mine, product, 0.0), axis=0, keepdims=True)
            part = jnp.sum(part, axis=1, keepdims=True)
            d_vec_ref[3:4, :] += jnp.where(lane == 2 * pair + side, part, 0.0)
        return 0

    lax.fori_loop(0, pairs, from_later, 0)
    fading = fade[...]
    d_keep = d_coeff[...] * fading * step[...]
    block_decay = jnp.exp(cum[length - 1 :, :]) * tok_ref[0:1, 4:5]
    d_last = jnp.sum(d_keep, axis=0, keepdims=True) + block_decay * d_vec_ref[3:4, :]
    d_log = running_sum(d_cum[...] - d_keep, True) + d_last
    d_size = d_step[...] + d_coeff[...] * fading - vec_ref[1:2, :] * d_log
    d_raw_step = d_size / (1.0 + jnp.exp(-shifted))
    d_proj_ref[:, widths[2] : widths[3]] = jnp.where(
        lanes(d_raw_step.shape) < heads, d_raw_step, 0.0
    ).astype(bf16)
    d_vec_ref[0:1, :] = jnp.sum(d_raw_step, axis=0, keepdims=True)
    d_vec_ref[1:2, :] = -jnp.sum(step[...] * d_log, axis=0, keepdims=True)
    d_vec_ref[2:3, :] = jnp.sum(d_skip[...], axis=0, keepdims=True)
    d_proj_ref[:, widths[1] : widths[1] + states] = d_b[...].astype(bf16)
    d_proj_ref[:, widths[1] + states : widths[2]] = d_c[...].astype(bf16)

    def kv_wait(k, _):
        kv_copy(k).wait_recv()
        d_keyval[:length, :] += kv_in[k].astype(f32)
        return 0

    lax.fori_loop(1, count, kv_wait, 0)
    d_proj_ref[:, widths[0] : widths[1]] = d_keyval[:length, :].astype(bf16)

    def drain(k, _):
        kv_copy(k).wait_send()

        @pl.when(k <= place)
        def _():
            st_copy(k).wait_send()

        return 0

    lax.fori_loop(1, count, drain, 0)


def mixer_call(kernel, collective, outs, scratch, sems, widths, heads, operands):
    count = lax.axis_size(CTX)
    whole = pl.BlockSpec(memory_space=pltpu.VMEM)
    return pl.pallas_call(
        functools.partial(kernel, count, widths, heads),
        out_shape=outs,
        in_specs=[whole] * len(operands),
        out_specs=[whole] * len(outs),
        scratch_shapes=[pltpu.VMEM(*s) for s in scratch]
        + [pltpu.SemaphoreType.DMA((count,))] * sems,
        compiler_params=pltpu.CompilerParams(
            collective_id=collective, has_side_effects=True, vmem_limit_bytes=56 << 20
        ),
        cost_estimate=pl.CostEstimate(flops=0, bytes_accessed=20 << 20, transcendentals=0),
        name="mixer"+str(collective),
    )(*operands)


def mix_forward(weights, proj, layout):
    count = lax.axis_size(CTX)
    widths, heads = weights.widths, weights.heads
    length, inner = proj.shape[0], (proj.shape[1] - widths[3]) // 2
    states = (widths[2] - widths[1]) // 2
    kv = widths[1] - widths[0]
    shape = jax.ShapeDtypeStruct
    head_rows = -(-heads // 8) * 8
    outs = [
        shape((length, widths[0] + inner), bf16),
        shape((length, inner), f32),
        shape((inner, states), bf16),
        shape((count * length, kv), bf16),
        shape((count, head_rows, states), f32),
    ]
    per_head = ((length, 128), f32)
    scratch = [
        per_head,
        ((128, length), f32),
        per_head,
        per_head,
        per_head,
        ((length, count * length), f32),
        ((length, length), f32),
        ((count, length, kv), bf16),
        ((count, inner, states), bf16),
        ((count, head_rows, states), f32),
        ((inner, states), f32),
    ]
    operands = (proj, weights.head_rows, weights.skip_row, *layout)
    return mixer_call(mix_forward_kernel, 5, outs, scratch, 6, widths, heads, operands)


def mix_backward(weights, saved, d_both, layout):
    count = lax.axis_size(CTX)
    widths, heads = weights.widths, weights.heads
    proj = saved.proj
    length, inner = proj.shape[0], (proj.shape[1] - widths[3]) // 2
    states = (widths[2] - widths[1]) // 2
    kv = widths[1] - widths[0]
    shape = jax.ShapeDtypeStruct
    outs = [shape(proj.shape, bf16), shape((8, 128), f32)]
    per_head = ((length, 128), f32)
    square = ((length, length), f32)
    scratch = [
        per_head,
        ((128, length), f32),
        per_head,
        per_head,
        per_head,
        ((length, count * length), f32),
        square,
        square,
        ((length, inner), bf16),
        ((length, inner), bf16),
        ((length, inner), f32),
        ((count * length, kv), f32),
        ((length, states), f32),
        ((length, states), f32),
        per_head,
        per_head,
        per_head,
        per_head,
        ((count, inner, states), bf16),
        ((inner, states), f32),
        ((count, length, kv), bf16),
        ((count, length, kv), bf16),
    ]
    operands = (
        proj,
        weights.head_rows,
        weights.skip_row,
        *layout,
        saved.mixed,
        saved.state_in,
        saved.keyval_all,
        saved.decays,
        d_both,
    )
    return mixer_call(mix_backward_kernel, 6, outs, scratch, 4, widths, heads, operands)


def norm_apply(values, gain):
    return values * lax.rsqrt(jnp.mean(values * values, axis=-1, keepdims=True) + eps) * gain


def matmul(left, right):
    return jnp.dot(left, right, preferred_element_type=f32)


def matmul_nt(left, right):
    return lax.dot_general(left, right, (((1,), (1,)), ((), ())), preferred_element_type=f32)


def matmul_tn(left, right):
    return lax.dot_general(left, right, (((0,), (0,)), ((), ())), preferred_element_type=f32)


def swap(values):
    return lax.ppermute(values, SECTION, [(0, 1), (1, 0)])


def block_layout(doc_lengths, length):
    count, place = lax.axis_size(CTX), lax.axis_index(CTX)
    start = place * length
    bounds = jnp.cumsum(doc_lengths)[:-1]

    def segment_of(positions):
        return jnp.sum((positions[:, None] >= bounds[None, :]).astype(jnp.int32), axis=1)

    order = lax.rem(place + count - jnp.arange(count, dtype=jnp.int32), count)
    inside = jnp.arange(length, dtype=jnp.int32)
    keys = (order[:, None] * length + inside[None, :]).reshape(-1)
    positions = start + inside
    segments = segment_of(positions)
    before = jnp.where(place > 0, segment_of(start[None] - 1)[0], -1)
    goes_on = jnp.broadcast_to(segments[-1] == before, segments.shape)
    columns = [segments, segments == before, segments == segments[-1], positions, goes_on]
    tokens = jnp.stack([c.astype(f32) for c in columns], axis=1)
    return jnp.pad(tokens, ((0, 0), (0, 3))), jnp.stack(
        [segment_of(keys).astype(f32), keys.astype(f32)]
    )


def layer_forward(weights, normed, layout):
    proj = matmul(normed, weights.proj)
    both, mixed, state_in, keyval_all, decays = mix_forward(weights, proj, layout)
    saved = types.SimpleNamespace(
        normed=normed,
        proj=proj,
        both=both,
        mixed=mixed,
        state_in=state_in,
        keyval_all=keyval_all,
        decays=decays,
    )
    return matmul(both, weights.out), saved


def ffn_forward(weights, ffn_in):
    gate_up = matmul(ffn_in, weights.gate_up)
    width = gate_up.shape[1] // 2
    gate_pre, upward = gate_up[:, :width], gate_up[:, width:]
    product = (jax.nn.silu(gate_pre) * upward).astype(bf16)
    return matmul(product, weights.down), gate_pre, upward, product


def ctx_bits():
    return [1 << i for i in reversed(range((lax.axis_size(CTX) - 1).bit_length()))]


def flip(values, bit):
    return lax.ppermute(values, CTX, [(i, i ^ bit) for i in range(lax.axis_size(CTX))])


def own_half(values):
    half = values.shape[1] // 2
    section = lax.axis_index(SECTION)
    return (
        lax.dynamic_slice_in_dim(values, section * half, half, 1),
        lax.dynamic_slice_in_dim(values, (1 - section) * half, half, 1),
    )


def both_batches(kept, sent):
    return jnp.concatenate([kept, swap(sent)], axis=0)


def ctx_orders():
    bits = ctx_bits()
    return bits, bits[::-1]


def relative_order(bits):
    order = [0]
    for bit in reversed(bits):
        order = order + [k ^ bit for k in order]
    return order


def weight_sums(columns, *rows):
    kept, sent = zip(*(own_half(r) for r in rows))
    halves = both_batches(jnp.concatenate(kept, axis=1), jnp.concatenate(sent, axis=1))
    return matmul_tn(both_batches(columns, columns), halves).astype(bf16)


def shared_sums(normed, d_shared):
    place, count = lax.axis_index(CTX), lax.axis_size(CTX)
    shards = lax.axis_size(SHARD)
    block = normed.shape[1] // (count * shards)
    columns = jnp.concatenate(
        [
            lax.dynamic_slice_in_dim(
                normed, ((place ^ k) * shards + lax.axis_index(SHARD)) * block, block, 1
            )
            for k in range(count)
        ],
        axis=1,
    )
    total = weight_sums(columns, d_shared)
    rows = total[:block].astype(f32)
    for k in range(1, count):
        rows = rows + flip(total[k * block : (k + 1) * block], k).astype(f32)
    return rows.astype(bf16)


def blocks_of(total):
    place, count = lax.axis_index(CTX), lax.axis_size(CTX)
    block = total.shape[0] // count
    return jnp.stack(
        [lax.dynamic_slice_in_dim(total, (place ^ k) * block, block, 0) for k in range(count)]
    )


def streams_of(total):
    place, count = lax.axis_index(CTX), lax.axis_size(CTX)
    block, half = total.shape[0] // count, total.shape[1] // 2
    streams = []
    for stream, bits in enumerate(ctx_orders()):
        parts = [
            lax.dynamic_slice(total, ((place ^ k) * block, stream * half), (block, half))
            for k in relative_order(bits)
        ]
        streams += [jnp.stack(parts[: count // 2]), jnp.stack(parts[count // 2 :])]
    return streams


def weight_scatter(streams):
    totals = []
    for i, bits in enumerate(ctx_orders()):
        kept, sent = (a.reshape(-1, a.shape[-1]) for a in streams[2 * i : 2 * i + 2])
        totals.append(scatter_relative(kept, sent, bits))
    return totals


def scatter_relative(kept, sent, bits):
    for i, bit in enumerate(bits):
        got = flip(sent, bit)
        if i + 1 < len(bits):
            rows = kept.shape[0] // 2
            sent = (kept[rows:].astype(f32) + got[rows:].astype(f32)).astype(bf16)
            kept = (kept[:rows].astype(f32) + got[:rows].astype(f32)).astype(bf16)
        else:
            kept = (kept.astype(f32) + got.astype(f32)).astype(bf16)
    return kept


def after(first, *later):
    first, later = lax.optimization_barrier((first, later))
    return first, later


def layer_backward(weights, saved, d_out, d_low, values_in, layout, last, before):
    grads = types.SimpleNamespace()
    d_product = matmul_nt(d_low, weights.down)
    gate_pre, upward = saved.gate_pre, saved.upward
    gate_sig = jax.nn.sigmoid(gate_pre)
    d_gate = d_product * upward * gate_sig * (1.0 + gate_pre * (1.0 - gate_sig))
    d_upward = d_product * gate_pre * gate_sig
    d_gate_up = jnp.concatenate([d_gate, d_upward], axis=1).astype(bf16)
    d_ffn_in = matmul_nt(d_gate_up, weights.gate_up)
    width = d_product.shape[1]
    up, down = width // 2, width // 4
    plan = tuple(
        (x, stream, ((x, stream * part, 2 * part + stream * part, part),))
        for stream in range(2)
        for x, part in ((0, up), (1, down))
    )
    d_middle, d_mixed, grads.gain_ffn, *sums = back_sum(
        10 if last else 3,
        d_ffn_in,
        d_out,
        saved.middle,
        weights.gain_ffn,
        plan,
        (saved.ffn_in, d_low),
        (d_gate_up, saved.product),
        (),
        before.sums_mix if last else (),
    )
    if last:
        sums, before.mix = sums[:4], sums[4:]
        grads.ffn = weight_scatter(sums)
    else:
        sums_ffn = sums
    d_both = matmul_nt(d_mixed, weights.out)
    if not last:
        (d_both,), (before.tail,) = after((d_both,), before.tail)
    if last:
        sums_out = weight_sums(d_mixed, saved.both)
        (sums_out,), (d_both,) = after((streams_of(sums_out),), d_both)
        grads.out = weight_scatter(sums_out)
    d_proj, d_vec = mix_backward(weights, saved, d_both, layout)
    if last:
        (grads.out,), (d_proj,) = after((grads.out,), d_proj)
    heads, widths = weights.heads, weights.widths
    grads.step_bias, grads.decay, grads.skip = (d_vec[i, :heads] for i in range(3))
    d_normed = matmul_nt(d_proj, weights.proj)
    placed = [
        jnp.where(weights.kv_owner == owner, d_proj[:, start : start + HD], 0)
        for start in (widths[0], widths[0] + HD)
        for owner in range(KVH)
    ]
    d_shared = jnp.concatenate([d_proj[:, widths[1] : widths[2]], *placed], axis=1)
    normed = saved.normed
    if last:
        d_step, d_zx = d_proj[:, widths[2] : widths[3]], d_proj[:, widths[3] :]
        sums_proj = weight_sums(
            normed, d_proj[:, : widths[0]], d_zx, jnp.concatenate([d_step, d_step], axis=1)
        )
        blocks = blocks_of(sums_proj)
        (blocks,), (d_normed,) = after((blocks,), d_normed)
        d_hidden, d_hidden_low, grads.gain_in, d_shared, grads.proj = back_sum_scatter(
            7, d_normed, d_shared, d_middle, values_in, weights.gain_in, blocks
        )
    else:
        query, inner = widths[0] // 2, (d_proj.shape[1] - widths[3]) // 2
        step, zx = widths[3] - widths[2], widths[3]
        both, most = saved.both.shape[1] // 4, inner // 2
        plan = (
            (0, 0, ((0, 0, query, query), (0, zx, zx + inner, most))),
            (1, 0, ((1, 0, 2 * both, both),)),
            (0, 1, ((0, zx + most, zx + inner + most, most), (0, widths[2], widths[2], step))),
            (1, 1, ((1, both, 3 * both, both),)),
        )
        d_hidden, d_hidden_low, grads.gain_in, d_shared, *sums = back_sum(
            4,
            d_normed,
            d_middle,
            values_in,
            weights.gain_in,
            plan,
            (normed, d_mixed),
            (d_proj, saved.both),
            (d_shared,),
            sums_ffn,
        )
        sums, grads.ffn = sums[:4], sums[4:]
        grads.sums_mix = sums
    grads.shared = shared_sums(normed, d_shared)
    return d_hidden, d_hidden_low, grads


def body(
    inputs,
    cotangent,
    doc_lengths,
    norm_in,
    w_query,
    w_keyval,
    w_attn_out,
    w_mixer_in,
    w_state_io,
    w_step,
    step_bias,
    decay_rate,
    skip_gain,
    w_mixer_out,
    norm_ffn,
    w_gate_up,
    w_down,
):
    section = lax.axis_index(SECTION)
    leading = section == 0
    shard = lax.axis_index(SHARD)
    width = w_query.shape[1]
    query_width = w_query.shape[2]
    head_count = w_step.shape[2]
    kv_owner = shard * (query_width // HD) // (QH // KVH)
    rows_in = lax.dynamic_index_in_dim(inputs, section, 0, False)
    own_keyval = lax.dynamic_slice_in_dim(w_keyval[0], kv_owner * HD, HD, 2).reshape(width, 2 * HD)
    io_end = query_width + 2 * HD + w_state_io.shape[2]
    widths = (query_width, query_width + 2 * HD, io_end, io_end - (-head_count // 128) * 128)
    proj = jnp.concatenate(
        [
            w_query[0],
            own_keyval,
            w_state_io[0],
            jnp.pad(w_step[0], ((0, 0), (0, -head_count % 128))),
            w_mixer_in[0].reshape(width, -1),
        ],
        axis=1,
    )
    vectors = jnp.concatenate([norm_in[0], norm_ffn[0], step_bias[0], decay_rate[0], skip_gain[0]])
    (proj, vectors), (rows_in,) = after((proj, vectors), rows_in)
    block_in = line_gather(rows_in)
    (block_in,), (w_gate_up, w_attn_out) = after((block_in,), w_gate_up, w_attn_out)
    own = (
        proj,
        jnp.concatenate([w_attn_out[0], w_mixer_out[0]], axis=0),
        w_gate_up[0].reshape(width, -1),
        w_down[0],
        vectors,
    )
    other = tuple(swap(array) for array in own)

    def layer_weights(layer):
        weights = types.SimpleNamespace()
        chosen = [jnp.where(section == layer, a, b) for a, b in zip(own, other)]
        weights.proj, weights.out, weights.gate_up, weights.down, vectors = chosen
        heads = vectors[2 * width :]
        weights.gain_in = vectors[:width]
        weights.gain_ffn = vectors[width : 2 * width]
        skip = heads[2 * head_count :]
        rows = heads[: 2 * head_count].reshape(2, head_count)
        weights.head_rows = jnp.pad(rows, ((0, 6), (0, -head_count % 128)))
        weights.skip_row = jnp.repeat(skip, HP)[None]
        weights.heads = head_count
        weights.widths = widths
        weights.kv_owner = kv_owner
        return weights

    layers = [layer_weights(0), layer_weights(1)]
    rows_cot = lax.dynamic_index_in_dim(cotangent, section, 0, False)
    length = block_in.shape[0]
    part = rows_in.shape[0]
    layout = block_layout(lax.dynamic_index_in_dim(doc_lengths, section, 0, False), length)

    def own_rows(values):
        return lax.dynamic_slice_in_dim(values, shard * part, part, 0)

    hidden = block_in.astype(f32)
    normed = norm_apply(hidden, layers[0].gain_in).astype(bf16)
    hiddens, outs, saves = [], [], []
    for layer in range(2):
        weights = layers[layer]
        hiddens.append(hidden)
        if layer == 1:
            (normed,), (rows_cot,) = after((normed,), rows_cot)
            block_cot = lax.all_gather(rows_cot, SHARD, axis=0, tiled=True)
        partial, saved = layer_forward(weights, normed, layout)
        first, second = layers
        wanted = (2, 3) if layer == 0 else (0, 1)
        wanted = [(0, own[i], other[i]) for i in wanted]
        if layer == 0:
            wanted.append((1, own[0], other[0]))
        saved.middle, saved.ffn_in, chosen = copying_sum(
            middle_kernel, 1 + 8 * layer, f32, partial, hidden, weights.gain_ffn, wanted
        )
        if layer == 0:
            first.gate_up, first.down, second.proj = chosen
        else:
            first.proj, first.out = chosen
        partial, saved.gate_pre, saved.upward, saved.product = ffn_forward(
            weights, saved.ffn_in
        )
        saves.append(saved)
        if layer == 0:
            wanted = [(1, own[i], other[i]) for i in (1, 2, 3)]
            out_low, normed, chosen = copying_sum(
                layer_end_kernel, 2, bf16, partial, saved.middle, second.gain_in, wanted
            )
            second.out, second.gate_up, second.down = chosen
            outs.append(own_rows(out_low))
            hidden = out_low.astype(f32)
        else:
            held = types.SimpleNamespace(tail=partial.astype(bf16))

    d_out = d_low = block_cot
    d_hiddens, grads = [None, None], [None, None]
    for layer in (1, 0):
        d_hidden, d_low, grads[layer] = layer_backward(
            layers[layer], saves[layer], d_out, d_low, hiddens[layer], layout, layer == 0, grads[1] if layer == 0 else held
        )
        d_hiddens[layer] = d_hidden
        d_out = d_low

    def by_layer(first, second):
        kept = jnp.where(leading, first, second)
        came = swap(jnp.where(leading, second, first))
        return jnp.where(leading, kept, came), jnp.where(leading, came, kept)

    total = lax.psum_scatter(held.tail, SHARD, scatter_dimension=0, tiled=True)
    outs.append((own_rows(saves[1].middle) + total.astype(f32)).astype(bf16))
    section_out = jnp.stack(by_layer(*outs))[None]
    input_grad = jnp.stack(by_layer(own_rows(d_hiddens[0]), own_rows(d_hiddens[1])))[None]

    def columns_of(first, second):
        return jnp.concatenate(by_layer(first, second), axis=1).astype(f32)

    def rows_of(first, second):
        return jnp.concatenate([first.T, second.T], axis=0).astype(f32)

    first, second = grads
    tiny = [
        jnp.concatenate([g.gain_in, g.gain_ffn, g.step_bias, g.decay, g.skip]) for g in grads
    ]
    tiny = sum(by_layer(*tiny))
    for bit in ctx_bits():
        tiny = tiny + flip(tiny, bit)
    place = lax.axis_index(CTX) * lax.axis_size(SHARD) + shard
    slot = width // (lax.axis_size(CTX) * lax.axis_size(SHARD))
    grad_in = lax.dynamic_slice_in_dim(tiny, place * slot, slot, 0)
    grad_ffn = lax.dynamic_slice_in_dim(tiny, width + place * slot, slot, 0)
    heads = tiny[2 * width :]

    inner = w_mixer_in.shape[3]
    query, most, both = query_width // 2, inner // 2, (query_width + inner) // 4
    left, right = second.mix
    parts = [
        (left[:, :query], left[:, query : query + most], left[:, query + most :]),
        (right[:, :most], right[:, most : most + head_count], right[:, right.shape[1] - both :]),
    ]
    proj = jnp.concatenate([*parts[0][:2], *parts[1][:2]], axis=1)
    proj_low, proj_high = by_layer(first.proj[:, : proj.shape[1]], proj)
    out_low, out_high = by_layer(
        jnp.concatenate(first.out, axis=1), jnp.concatenate([p[2] for p in parts], axis=1)
    )
    ffn_low, ffn_high = by_layer(
        jnp.concatenate(first.ffn, axis=1), jnp.concatenate(second.ffn, axis=1)
    )
    step_at = query + inner
    shared = columns_of(first.shared, second.shared)
    io_width = w_state_io.shape[2]
    out = rows_of(out_low, out_high)
    ff = w_gate_up.shape[3] // 2

    def ffn_parts(total):
        edge = total.shape[1] // 2
        up = jnp.concatenate([total[:, :ff], total[:, edge : edge + ff]], axis=1)
        return up, jnp.concatenate([total[:, ff:edge], total[:, edge + ff :]], axis=1)

    (up_low, down_low), (up_high, down_high) = ffn_parts(ffn_low), ffn_parts(ffn_high)
    gate_up = jnp.stack([up_low, up_high], axis=1)
    return (
        section_out,
        input_grad,
        grad_in[None],
        jnp.concatenate([proj_low[:, :query], proj_high[:, :query]], axis=1).astype(f32)[None],
        shared[:, io_width:].reshape(-1, 2, KVH * HD)[None],
        out[:query_width][None],
        jnp.stack([p[:, query:step_at] for p in (proj_low, proj_high)], axis=1).astype(f32)[None],
        shared[:, :io_width][None],
        proj_low[:, step_at : step_at + head_count].astype(f32)[None],
        heads[:head_count][None],
        heads[head_count : 2 * head_count][None],
        heads[2 * head_count :][None],
        out[query_width:][None],
        grad_ffn[None],
        gate_up.astype(f32)[None],
        rows_of(down_low, down_high)[None],
    )


def solution(mesh):
    return jax.shard_map(
        body,
        mesh=mesh,
        in_specs=(
            P(None, (CTX, SHARD), None),
            P(None, (CTX, SHARD), None),
            P(),
            P(SECTION, None),
            P(SECTION, None, SHARD),
            P(SECTION, None, None, None),
            P(SECTION, SHARD, None),
            P(SECTION, None, None, SHARD),
            P(SECTION, None, None),
            P(SECTION, None, SHARD),
            P(SECTION, SHARD),
            P(SECTION, SHARD),
            P(SECTION, SHARD),
            P(SECTION, SHARD, None),
            P(SECTION, None),
            P(SECTION, None, None, SHARD),
            P(SECTION, SHARD, None),
        ),
        out_specs=(
            P(SECTION, None, (CTX, SHARD), None),
            P(SECTION, None, (CTX, SHARD), None),
            P(SECTION, (CTX, SHARD)),
            P(SECTION, CTX, SHARD),
            P(SECTION, (CTX, SHARD), None, None),
            P(SECTION, SHARD, CTX),
            P(SECTION, CTX, None, SHARD),
            P(SECTION, (CTX, SHARD), None),
            P(SECTION, CTX, SHARD),
            P(SECTION, SHARD),
            P(SECTION, SHARD),
            P(SECTION, SHARD),
            P(SECTION, SHARD, CTX),
            P(SECTION, (CTX, SHARD)),
            P(SECTION, CTX, None, SHARD),
            P(SECTION, SHARD, CTX),
        ),
        check_vma=False,
    )
```

profile of v0, /device:TPU:0, one launch (start us, length us, event | category | flops | bytes accessed | tf_op | source)
XLA Modules:
  0.0 819.5 jit_solution(17159304775649489507)
XLA Ops:
  10.0 6.8 copy.81
  21.8 3.2 constant_dynamic-update-slice_fusion.refs_2_.refs_0_
  26.2 25.1 %gather.1 = bf16[256,2048]{1,0:T(8,128)(2,1)} custom-call(bf16[64,2048]{1,0:T(8,128)(2,1)} %dynamic-slice_bitcast_fusion.13.rows_ref), custom_call_target="tpu_custom_call" | custom-call | tf_op jit(solution)/shard_map/gather/pallas_call | solution.py:627
  51.3 10.5 %copy.84 = bf16[256,8,2,1024]{3,1,2,0:T(8,128)(2,1)} copy(bf16[256,8,2,1024]{3,2,1,0:T(2,128)(2,1)} %bitcast.201) | data formatting | bytes 16777216
  79.7 9.3 %fusion.proj_ref = f32[256,2688]{1,0:T(8,128)} fusion(bf16[256,2048]{1,0:T(8,128)(2,1)} %multiply_convert_fusion, bf16[2048,2688]{1,0:T(8,128)(2,1)} %constant_dynamic-update-slice_fusion.refs_2_.refs_0_, bf16[2048,2688]{1,0:T(8,128)(2,1)} %collective-permute-done.1.refs_5_.refs_2_, pred[]{:T(512)S(6)} %eq.52), kind=kOutput, calls=%fused_computation | convolution fusion | flops 2824077312 | bytes 25821184 | tf_op jit(solution)/shard_map/dot_general | solution.py:1308
  89.0 29.8 %mixer5.2 = (bf16[256,1024]{1,0:T(8,128)(2,1)}, f32[256,768]{1,0:T(8,128)}, bf16[768,256]{1,0:T(8,128)(2,1)}, bf16[1024,256]{1,0:T(8,128)(2,1)}, f32[4,16,256]{2,1,0:T(8,128)}) custom-call(f32[256,2688]{1,0:T(8,128)} %fusion.proj_ref, f32[8,128]{1,0:T(8,128)} %pad.16.vec_ref, f32[1,768]{1,0:T(1,128)} %broadcast_in_dim_reshape.10.skip_ref, ...), custom_call_target="tpu_custom_call" | custom-call | bytes 20971520 | tf_op jit(solution)/shard_map/mixer5/pallas_call | solution.py:1206
  118.8 3.7 fusion.3.p_ref
  122.5 46.2 %line_sum1.1 = (f32[256,2048]{1,0:T(8,128)}, bf16[256,2048]{1,0:T(8,128)(2,1)}, bf16[2048,2048]{1,0:T(8,128)(2,1)}, bf16[1024,2048]{1,0:T(8,128)(2,1)}, bf16[2048,2688]{1,0:T(8,128)(2,1)}) custom-call(f32[256,2048]{1,0:T(8,128)} %fusion.3.p_ref, f32[256,2048]{1,0:T(8,128)} %convert_element_type.360.h_ref.v_ref, f32[1,2048]{1,0:T(1,128)} %bitcast.216, ...), custom_call_target="tpu_custom_call" | custom-call | bytes 20971520 | tf_op jit(solution)/shard_map/line_sum1/pallas_call | solution.py:580
  168.8 6.2 fusion.76
  177.9 37.0 %line_sum2.1 = (bf16[256,2048]{1,0:T(8,128)(2,1)}, bf16[256,2048]{1,0:T(8,128)(2,1)}, bf16[1024,2048]{1,0:T(8,128)(2,1)}, bf16[2048,2048]{1,0:T(8,128)(2,1)}, bf16[1024,2048]{1,0:T(8,128)(2,1)}) custom-call(f32[256,2048]{1,0:T(8,128)} %fusion.77.p_ref, f32[256,2048]{1,0:T(8,128)} %get-tuple-element.104.h_ref.refs_2_, f32[1,2048]{1,0:T(1,128)} %bitcast.212, ...), custom_call_target="tpu_custom_call" | custom-call | bytes 20971520 | tf_op jit(solution)/shard_map/line_sum2/pallas_call | solution.py:580
  218.8 9.0 %fusion.78.proj_ref = f32[256,2688]{1,0:T(8,128)} fusion(bf16[256,2048]{1,0:T(8,128)(2,1)S(1)} %copy-done.26, bf16[2048,2688]{1,0:T(8,128)(2,1)} %get-tuple-element.108), kind=kOutput, calls=%fused_computation.252 | convolution fusion | flops 2818572288 | bytes 14811136 | tf_op jit(solution)/shard_map/dot_general | solution.py:1308
  227.8 32.4 %mixer5.3 = (bf16[256,1024]{1,0:T(8,128)(2,1)}, f32[256,768]{1,0:T(8,128)}, bf16[768,256]{1,0:T(8,128)(2,1)}, bf16[1024,256]{1,0:T(8,128)(2,1)}, f32[4,16,256]{2,1,0:T(8,128)}) custom-call(f32[256,2688]{1,0:T(8,128)} %fusion.78.proj_ref, f32[8,128]{1,0:T(8,128)} %pad.18.vec_ref, f32[1,768]{1,0:T(1,128)} %broadcast_in_dim_reshape.11.skip_ref, ...), custom_call_target="tpu_custom_call" | custom-call | bytes 20971520 | tf_op jit(solution)/shard_map/mixer5/pallas_call | solution.py:1206
  260.2 3.6 fusion.79.p_ref
  263.8 37.8 %line_sum9.1 = (f32[256,2048]{1,0:T(8,128)}, bf16[256,2048]{1,0:T(8,128)(2,1)}, bf16[2048,2688]{1,0:T(8,128)(2,1)}, bf16[1024,2048]{1,0:T(8,128)(2,1)}) custom-call(f32[256,2048]{1,0:T(8,128)} %fusion.79.p_ref, f32[256,2048]{1,0:T(8,128)} %convert_element_type.378.h_ref.refs_3_, f32[1,2048]{1,0:T(1,128)} %bitcast.214, ...), custom_call_target="tpu_custom_call" | custom-call | bytes 20971520 | tf_op jit(solution)/shard_map/line_sum9/pallas_call | solution.py:580
  301.7 7.4 fusion.80
  309.1 4.9 multiply_convert_fusion.5
  315.2 3.7 fusion.67.refs_0_
  321.1 41.0 %line_sum3.1 = (f32[256,2048]{1,0:T(8,128)}, bf16[256,2048]{1,0:T(8,128)(2,1)}, f32[8,2048]{1,0:T(8,128)}, bf16[2,512,768]{2,1,0:T(8,128)(2,1)}, bf16[2,512,768]...) custom-call(f32[256,2048]{1,0:T(8,128)} %fusion.67.refs_0_, ...), custom_call_target="tpu_custom_call" | custom-call | bytes 20971520 | tf_op jit(solution)/shard_map/line_sum3/pallas_call | solution.py:580
  362.1 4.8 fusion.81.d_both_ref
  366.9 35.8 %mixer6.2 = (bf16[256,2688]{1,0:T(8,128)(2,1)}, f32[8,128]{1,0:T(8,128)}) custom-call(f32[256,2688]{1,0:T(8,128)} %fusion.78.proj_ref, f32[8,128]{1,0:T(8,128)} %pad.18.vec_ref, f32[1,768]{1,0:T(1,128)} %broadcast_in_dim_reshape.11.skip_ref, f32[256,8]{1,0:T(8,128)} %pad.17.tok_ref, f32[2,1024]{1,0:T(2,128)} %pad_maximum_fusion.15.key_ref, ...), custom_call_target="tpu_custom_call" | custom-call | bytes 20971520 | tf_op jit(solution)/shard_map/mixer6/pallas_call | solution.py:1206
  403.7 9.1 %fusion.82.refs_0_ = f32[256,2048]{1,0:T(8,128)} fusion(bf16[256,2688]{1,0:T(8,128)(2,1)} %get-tuple-element.123.refs_7_, bf16[2048,2688]{1,0:T(8,128)(2,1)} %get-tuple-element.108), kind=kOutput, calls=%fused_computation.256 | convolution fusion | flops 2818572288 | bytes 14483456 | tf_op jit(solution)/shard_map/dot_general | solution.py:1312
  417.1 64.9 %line_sum4.1 = (f32[256,2048]{1,0:T(8,128)}, bf16[256,2048]{1,0:T(8,128)(2,1)}, f32[8,2048]{1,0:T(8,128)}, bf16[256,1024]{1,0:T(8,128)(2,1)}, bf16[2,512,768]{2,...) custom-call(f32[256,2048]{1,0:T(8,128)} %fusion.82.refs_0_, ...), custom_call_target="tpu_custom_call" | custom-call | bytes 20971520 | tf_op jit(solution)/shard_map/line_sum4/pallas_call | solution.py:580
  482.0 4.2 multiply_convert_fusion.2
  487.3 3.7 fusion.66.refs_0_
  491.0 63.3 %line_sum10.1 = (f32[256,2048]{1,0:T(8,128)}, bf16[256,2048]{1,0:T(8,128)(2,1)}, f32[8,2048]{1,0:T(8,128)}, bf16[2,512,768]{2,1,0:T(8,128)(2,1)}, bf16[2,512,768...) custom-call(f32[256,2048]{1,0:T(8,128)} %fusion.66.refs_0_, ...), custom_call_target="tpu_custom_call" | custom-call | bytes 20971520 | tf_op jit(solution)/shard_map/line_sum10/pallas_call | solution.py:580
  560.9 4.8 fusion.83.d_both_ref
  575.9 62.5 %mixer6.3 = (bf16[256,2688]{1,0:T(8,128)(2,1)}, f32[8,128]{1,0:T(8,128)}) custom-call(f32[256,2688]{1,0:T(8,128)} %fusion.proj_ref, f32[8,128]{1,0:T(8,128)} %pad.16.vec_ref, f32[1,768]{1,0:T(1,128)} %broadcast_in_dim_reshape.10.skip_ref, f32[256,8]{1,0:T(8,128)} %pad.17.tok_ref, f32[2,1024]{1,0:T(2,128)} %pad_maximum_fusion.15.key_ref, ...), custom_call_target="tpu_custom_call" | custom-call | bytes 20971520 | tf_op jit(solution)/shard_map/mixer6/pallas_call | solution.py:1206
  653.7 8.6 %fusion.84.p_ref = f32[256,2048]{1,0:T(8,128)} fusion(bf16[256,2688]{1,0:T(8,128)(2,1)S(1)} %copy-done.25, bf16[2048,2688]{1,0:T(8,128)(2,1)} %get-tuple-element.147), kind=kOutput, calls=%fused_computation.258 | convolution fusion | flops 2818572288 | bytes 14483456 | tf_op jit(solution)/shard_map/dot_general | solution.py:1312
  670.2 4.2 convolution_convert_fusion
  677.1 59.7 %line_sum7.1 = (f32[256,2048]{1,0:T(8,128)}, bf16[256,2048]{1,0:T(8,128)(2,1)}, f32[8,2048]{1,0:T(8,128)}, bf16[256,1024]{1,0:T(8,128)(2,1)}, bf16[512,1024]{1,0:T(8,128)(2,1)}) custom-call(f32[256,2048]{1,0:T(8,128)} %fusion.84.p_ref, bf16[256,1024]{1,0:T(8,128)(2,1)} %copy-done.30, f32[256,2048]{1,0:T(8,128)} %get-tuple-element.149.d_ref, ...), custom_call_target="tpu_custom_call" | custom-call | bytes 20971520 | tf_op jit(solution)/shard_map/line_sum7/pallas_call | solution.py:580
  791.9 4.1 copy.74
  806.9 5.2 copy.78
  (406 shorter events, 149.9 us)
Async XLA Ops:
  7.2 301.9 %all-gather.2.cloned.1.call-start = ((), (), s32[]{:S(2)}) async-start(), calls=%async_computation.1 | async-start | bytes 1310720 | tf_op jit(solution)/shard_map/all_gather | solution.py:1650
  25.8 53.9 %collective-permute-start.1 = (bf16[2048,2688]{1,0:T(8,128)(2,1)}, bf16[2048,2688]{1,0:T(8,128)(2,1)}, u32[]{:S(2)}, u32[]{:S(2)}) collective-permute-start(bf16[2048,2688]{1,0:T(8,128)(2,1)} %constant_dynamic-update-slice_fusion.refs_2_.refs_0_), channel_id=1, source_target_pairs={{0,16},{16,0},{1,17},{17,1},{2,18},{18,2},{3,19},{19,3},{4,20},{20... | collective-permute-start | bytes 33030152 | tf_op jit(solution)/shard_map/ppermute | solution.py:1320
  61.8 60.7 %collective-permute-start.3 = (bf16[2048,2048]{1,0:T(8,128)(2,1)}, bf16[2048,2048]{1,0:T(8,128)(2,1)}, u32[]{:S(2)}, u32[]{:S(2)}) collective-permute-start(bf16[2048,2048]{1,0:T(8,128)(2,1)} %bitcast.197), channel_id=1, source_target_pairs={{0,16},{16,0},{1,17},{17,1},{2,18},{18,2},{3,19},{19,3},{4,20},{20... | collective-permute-start | bytes 25165832 | tf_op jit(solution)/shard_map/ppermute | solution.py:1320
  61.8 11.2 %collective-permute-start = (f32[4132]{0:T(1024)S(1)}, f32[4132]{0:T(1024)S(1)}, u32[]{:S(2)}, u32[]{:S(2)}) collective-permute-start(f32[4132]{0:T(1024)S(1)} %concatenate.145), channel_id=1, source_target_pairs={{0,16},{16,0},{1,17},{17,1},{2,18},{18,2},{3,19},{19,3},{4,20},{20... | collective-permute-start | bytes 49592 | tf_op jit(solution)/shard_map/ppermute | solution.py:1320
  64.7 54.1 %collective-permute-start.2 = (bf16[1024,2048]{1,0:T(8,128)(2,1)}, bf16[1024,2048]{1,0:T(8,128)(2,1)}, u32[]{:S(2)}, u32[]{:S(2)}) collective-permute-start(bf16[1024,2048]{1,0:T(8,128)(2,1)} %pad_maximum_fusion.refs_0_.refs_1_), channel_id=1, source_target_pairs={{0,16},{16,0},{1,17},{17,1},{2,18},{18,2},{3,19},{19,3},{4,20},{20... | collective-permute-start | bytes 12582920 | tf_op jit(solution)/shard_map/ppermute | solution.py:1320
  64.8 57.7 %collective-permute-start.4 = (bf16[1024,2048]{1,0:T(8,128)(2,1)}, bf16[1024,2048]{1,0:T(8,128)(2,1)}, u32[]{:S(2)}, u32[]{:S(2)}) collective-permute-start(bf16[1024,2048]{1,0:T(8,128)(2,1)} %bitcast.19.refs_1_.refs_2_), channel_id=1, source_target_pairs={{0,16},{16,0},{1,17},{17,1},{2,18},{18,2},{3,19},{19,3},{4,20},{20... | collective-permute-start | bytes 12582920 | tf_op jit(solution)/shard_map/ppermute | solution.py:1320
  77.9 589.2 %collective-permute-start.6 = (bf16[256,2048]{1,0:T(8,128)(2,1)}, bf16[256,2048]{1,0:T(8,128)(2,1)}, u32[]{:S(2)}, u32[]{:S(2)}) collective-permute-start(bf16[256,2048]{1,0:T(8,128)(2,1)} %multiply_convert_fusion), channel_id=1, source_target_pairs={{0,16},{16,0},{1,17},{17,1},{2,18},{18,2},{3,19},{19,3},{4,20},{20... | collective-permute-start | bytes 3145736 | tf_op jit(solution)/shard_map/ppermute | solution.py:1320
  217.9 447.1 %reduce-scatter.2.cloned.1.call-start = ((), (), s32[]{:S(2)}) async-start(), calls=%async_computation.2 | async-start | bytes 1310720 | tf_op jit(solution)/shard_map/reduce_scatter | solution.py:1693
  218.8 348.1 %collective-permute-start.8 = (bf16[256,512]{1,0:T(8,128)(2,1)}, bf16[256,512]{1,0:T(8,128)(2,1)}, u32[]{:S(2)}, u32[]{:S(2)}) collective-permute-start(bf16[256,512]{1,0:T(8,128)(2,1)} %get-tuple-element.301), channel_id=1, source_target_pairs={{0,16},{16,0},{1,17},{17,1},{2,18},{18,2},{3,19},{19,3},{4,20},{20... | collective-permute-start | bytes 786440 | tf_op jit(solution)/shard_map/ppermute | solution.py:1320
  554.3 13.3 %collective-permute-start.7 = (bf16[256,2048]{1,0:T(8,128)(2,1)}, bf16[256,2048]{1,0:T(8,128)(2,1)}, u32[]{:S(2)}, u32[]{:S(2)}) collective-permute-start(bf16[256,2048]{1,0:T(8,128)(2,1)} %get-tuple-element.134), channel_id=1, source_target_pairs={{0,16},{16,0},{1,17},{17,1},{2,18},{18,2},{3,19},{19,3},{4,20},{20... | collective-permute-start | bytes 3145736 | tf_op jit(solution)/shard_map/ppermute | solution.py:1320
  555.2 16.3 %collective-permute-start.24 = (bf16[256,512]{1,0:T(8,128)(2,1)}, bf16[256,512]{1,0:T(8,128)(2,1)}, u32[]{:S(2)}, u32[]{:S(2)}) collective-permute-start(bf16[256,512]{1,0:T(8,128)(2,1)} %pad_maximum_fusion.14), channel_id=1, source_target_pairs={{0,16},{16,0},{1,17},{17,1},{2,18},{18,2},{3,19},{19,3},{4,20},{20... | collective-permute-start | bytes 786440 | tf_op jit(solution)/shard_map/ppermute | solution.py:1320
  557.9 82.1 %collective-permute-start.31 = (bf16[1024,768]{1,0:T(8,128)(2,1)}, bf16[1024,768]{1,0:T(8,128)(2,1)}, u32[]{:S(2)}, u32[]{:S(2)}) collective-permute-start(bf16[1024,768]{1,0:T(8,128)(2,1)} %bitcast.71), channel_id=1, source_target_pairs={{0,8},{4,12},{8,0},{12,4},{1,9},{5,13},{9,1},{13,5},{2,10},{6,14},... | collective-permute-start | bytes 4718600 | tf_op jit(solution)/shard_map/ppermute | solution.py:1373
  566.9 75.7 %collective-permute-start.33 = (bf16[1024,768]{1,0:T(8,128)(2,1)}, bf16[1024,768]{1,0:T(8,128)(2,1)}, u32[]{:S(2)}, u32[]{:S(2)}) collective-permute-start(bf16[1024,768]{1,0:T(8,128)(2,1)} %bitcast.74), channel_id=1, source_target_pairs={{0,4},{4,0},{8,12},{12,8},{1,5},{5,1},{9,13},{13,9},{2,6},{6,2},{1... | collective-permute-start | bytes 4718600 | tf_op jit(solution)/shard_map/ppermute | solution.py:1373
  571.5 68.3 %collective-permute-start.11 = (bf16[1024,256]{1,0:T(8,128)(2,1)}, bf16[1024,256]{1,0:T(8,128)(2,1)S(1)}, u32[]{:S(2)}, u32[]{:S(2)}) collective-permute-start(bf16[1024,256]{1,0:T(8,128)(2,1)} %bitcast.38), channel_id=1, source_target_pairs={{0,4},{4,0},{8,12},{12,8},{1,5},{5,1},{9,13},{13,9},{2,6},{6,2},{1... | collective-permute-start | bytes 1572872 | tf_op jit(solution)/shard_map/ppermute | solution.py:1373
  574.3 65.6 %collective-permute-start.9 = (bf16[1024,256]{1,0:T(8,128)(2,1)S(1)}, bf16[1024,256]{1,0:T(8,128)(2,1)S(1)}, u32[]{:S(2)}, u32[]{:S(2)}) collective-permute-start(bf16[1024,256]{1,0:T(8,128)(2,1)S(1)} %bitcast.210), channel_id=1, source_target_pairs={{0,8},{4,12},{8,0},{12,4},{1,9},{5,13},{9,1},{13,5},{2,10},{6,14},... | collective-permute-start | bytes 1572872 | tf_op jit(solution)/shard_map/ppermute | solution.py:1373
  639.8 124.7 %collective-permute-start.19 = (bf16[256,512]{1,0:T(8,128)(2,1)}, bf16[256,512]{1,0:T(8,128)(2,1)}, u32[]{:S(2)}, u32[]{:S(2)}) collective-permute-start(bf16[256,512]{1,0:T(8,128)(2,1)} %pad_maximum_fusion.13), channel_id=1, source_target_pairs={{0,16},{16,0},{1,17},{17,1},{2,18},{18,2},{3,19},{19,3},{4,20},{20... | collective-permute-start | bytes 786440 | tf_op jit(solution)/shard_map/ppermute | solution.py:1320
  639.9 128.6 %collective-permute-start.26 = (bf16[128,512]{0,1:T(8,128)(2,1)}, bf16[128,512]{0,1:T(8,128)(2,1)}, u32[]{:S(2)}, u32[]{:S(2)}) collective-permute-start(bf16[128,512]{0,1:T(8,128)(2,1)} %get-tuple-element.290), channel_id=1, source_target_pairs={{0,4},{4,0},{8,12},{12,8},{1,5},{5,1},{9,13},{13,9},{2,6},{6,2},{1... | collective-permute-start | bytes 393224 | tf_op jit(solution)/shard_map/ppermute | solution.py:1373
  640.0 8.8 %collective-permute-start.12 = (bf16[512,256]{1,0:T(8,128)(2,1)S(1)}, bf16[512,256]{1,0:T(8,128)(2,1)S(1)}, u32[]{:S(2)}, u32[]{:S(2)}) collective-permute-start(bf16[512,256]{1,0:T(8,128)(2,1)S(1)} %fusion.50), channel_id=1, source_target_pairs={{0,8},{4,12},{8,0},{12,4},{1,9},{5,13},{9,1},{13,5},{2,10},{6,14},... | collective-permute-start | bytes 786440 | tf_op jit(solution)/shard_map/ppermute | solution.py:1373
  642.6 9.0 %collective-permute-start.10 = (bf16[512,256]{1,0:T(8,128)(2,1)S(1)}, bf16[512,256]{1,0:T(8,128)(2,1)S(1)}, u32[]{:S(2)}, u32[]{:S(2)}) collective-permute-start(bf16[512,256]{1,0:T(8,128)(2,1)S(1)} %fusion.52), channel_id=1, source_target_pairs={{0,4},{4,0},{8,12},{12,8},{1,5},{5,1},{9,13},{13,9},{2,6},{6,2},{1... | collective-permute-start | bytes 786440 | tf_op jit(solution)/shard_map/ppermute | solution.py:1373
  648.8 123.3 %collective-permute-start.27 = (bf16[128,512]{0,1:T(8,128)(2,1)}, bf16[128,512]{0,1:T(8,128)(2,1)}, u32[]{:S(2)}, u32[]{:S(2)}) collective-permute-start(bf16[128,512]{0,1:T(8,128)(2,1)} %get-tuple-element.292), channel_id=1, source_target_pairs={{0,8},{4,12},{8,0},{12,4},{1,9},{5,13},{9,1},{13,5},{2,10},{6,14},... | collective-permute-start | bytes 393224 | tf_op jit(solution)/shard_map/ppermute | solution.py:1373
  667.1 76.2 %collective-permute-start.32 = (bf16[512,768]{1,0:T(8,128)(2,1)}, bf16[512,768]{1,0:T(8,128)(2,1)S(1)}, u32[]{:S(2)}, u32[]{:S(2)}) collective-permute-start(bf16[512,768]{1,0:T(8,128)(2,1)} %fusion.14), channel_id=1, source_target_pairs={{0,4},{4,0},{8,12},{12,8},{1,5},{5,1},{9,13},{13,9},{2,6},{6,2},{1... | collective-permute-start | bytes 2359304 | tf_op jit(solution)/shard_map/ppermute | solution.py:1373
  668.5 77.4 %collective-permute-start.34 = (bf16[512,768]{1,0:T(8,128)(2,1)}, bf16[512,768]{1,0:T(8,128)(2,1)}, u32[]{:S(2)}, u32[]{:S(2)}) collective-permute-start(bf16[512,768]{1,0:T(8,128)(2,1)} %fusion.12), channel_id=1, source_target_pairs={{0,8},{4,12},{8,0},{12,4},{1,9},{5,13},{9,1},{13,5},{2,10},{6,14},... | collective-permute-start | bytes 2359304 | tf_op jit(solution)/shard_map/ppermute | solution.py:1373
  744.2 5.5 collective-permute-start.30
  749.7 16.2 %collective-permute-start.20 = (bf16[256,512]{1,0:T(8,128)(2,1)}, bf16[256,512]{1,0:T(8,128)(2,1)}, u32[]{:S(2)}, u32[]{:S(2)}) collective-permute-start(bf16[256,512]{1,0:T(8,128)(2,1)} %get-tuple-element.299), channel_id=1, source_target_pairs={{0,16},{16,0},{1,17},{17,1},{2,18},{18,2},{3,19},{19,3},{4,20},{20... | collective-permute-start | bytes 786440 | tf_op jit(solution)/shard_map/ppermute | solution.py:1320
  754.4 8.9 %collective-permute-start.16 = (f32[4132]{0:T(1024)}, f32[4132]{0:T(1024)}, u32[]{:S(2)}, u32[]{:S(2)}) collective-permute-start(f32[4132]{0:T(1024)} %select_add_fusion), channel_id=1, source_target_pairs={{0,8},{4,12},{8,0},{12,4},{1,9},{5,13},{9,1},{13,5},{2,10},{6,14},... | collective-permute-start | bytes 49592 | tf_op jit(solution)/shard_map/ppermute | solution.py:1373
  763.3 8.9 %collective-permute-start.28 = (bf16[128,512]{0,1:T(8,128)(2,1)}, bf16[128,512]{0,1:T(8,128)(2,1)S(1)}, u32[]{:S(2)}, u32[]{:S(2)}) collective-permute-start(bf16[128,512]{0,1:T(8,128)(2,1)} %get-tuple-element.291), channel_id=1, source_target_pairs={{0,12},{4,8},{8,4},{12,0},{1,13},{5,9},{9,5},{13,1},{2,14},{6,10},... | collective-permute-start | bytes 393224 | tf_op jit(solution)/shard_map/ppermute | solution.py:1373
  767.7 5.9 collective-permute-start.21
  768.4 6.7 collective-permute-start.22
  769.9 6.7 collective-permute-start.23
  772.1 27.2 %collective-permute-start.35 = (bf16[512,1536]{1,0:T(8,128)(2,1)}, bf16[512,1536]{1,0:T(8,128)(2,1)}, u32[]{:S(2)}, u32[]{:S(2)}) collective-permute-start(bf16[512,1536]{1,0:T(8,128)(2,1)} %broadcast_select_fusion.2), channel_id=1, source_target_pairs={{0,16},{16,0},{1,17},{17,1},{2,18},{18,2},{3,19},{19,3},{4,20},{20... | collective-permute-start | bytes 4718600 | tf_op jit(solution)/shard_map/ppermute | solution.py:1320
  772.2 14.0 %collective-permute-start.18 = (bf16[512,908]{0,1:T(8,128)(2,1)}, bf16[512,908]{0,1:T(8,128)(2,1)}, u32[]{:S(2)}, u32[]{:S(2)}) collective-permute-start(bf16[512,908]{0,1:T(8,128)(2,1)} %copy.69), channel_id=1, source_target_pairs={{0,16},{16,0},{1,17},{17,1},{2,18},{18,2},{3,19},{19,3},{4,20},{20... | collective-permute-start | bytes 2789384 | tf_op jit(solution)/shard_map/ppermute | solution.py:1320
  773.6 10.0 %collective-permute-start.14 = (f32[64,2048]{1,0:T(8,128)}, f32[64,2048]{1,0:T(8,128)}, u32[]{:S(2)}, u32[]{:S(2)}) collective-permute-start(f32[64,2048]{1,0:T(8,128)} %dynamic-slice_select_fusion), channel_id=1, source_target_pairs={{0,16},{16,0},{1,17},{17,1},{2,18},{18,2},{3,19},{19,3},{4,20},{20... | collective-permute-start | bytes 1572872 | tf_op jit(solution)/shard_map/ppermute | solution.py:1320
  (88 other events, 1457.9 us)
Sparse Core Ops, SparseCore 0:
  218.0 30.5 all-gather.1
  559.5 25.9 reduce-scatter.1
where the time goes:
time: 832 us; the launch traced here: 819 us
  Pallas kernels  536 us (64%)
  matrix products  97.6 us (12%)
  local copies, waits for them, and re-layouts  83.2 us (10%)
  other arithmetic  56.7 us (7%)
  starting transfers between devices  20.7 us (2%)
  between operations  17.2 us (2%)
  waiting for transfers between devices  8.44 us (1%)
    pallas_call x7, Pallas kernels, summed(): pl.pallas_call(functools.partial(kernel, n, CHUNKS, LAG), out_shape=outs,...  350 us
    pallas_call x4, Pallas kernels, mixer_call(): pl.pallas_call(functools.partial(kernel, count, widths, heads), out_shape...  160 us
    unnamed x185, local copies, waits for them, and re-layouts  51.8 us
    dot_general x8, matrix products, matmul(): return jnp.dot(left, right, preferred_element_type=f32)  44 us
    dot_general x8, matrix products, matmul_nt(): lax.dot_general(left, right, (((1,), (1,)), ((), ())), preferred_element_...  43.8 us
    pallas_call x1, Pallas kernels, line_gather(): pl.pallas_call(functools.partial(gather_kernel, n), out_shape=jax.ShapeDt...  25.1 us
    ppermute x16, starting transfers between devices, flip(): lax.ppermute(values, CTX, [(i, i ^ bit) for i in range(lax.axis_size(CTX))])  17 us
  transfers between devices with their start and end apart: 38, of which 6 were waited for; matrix products, arithmetic and copies ran while one was open for 24% of the time, Pallas kernels for 65%

commit v1 on v0

--- a/solution.py
+++ b/solution.py
@@ -593,47 +593,15 @@
     )(*operands)
 
 
-def gather_kernel(n, rows_ref, out_ref, box, send, recv):
-    z = lax.axis_index(SHARD)
-    part = rows_ref.shape[0]
-    bar = pltpu.get_barrier_semaphore()
-
-    def copy(k):
-        return pltpu.make_async_remote_copy(
-            rows_ref,
-            box.at[k],
-            send.at[k],
-            recv.at[k],
-            device_id={SHARD: lax.rem(z + k, n)},
-            device_id_type=MESH,
-        )
-
-    for k in range(1, n):
-        pl.semaphore_signal(bar, inc=1, device_id={SHARD: lax.rem(z + k, n)}, device_id_type=MESH)
-    pl.semaphore_wait(bar, n - 1)
-    for k in range(1, n):
-        copy(k).start()
-    out_ref[row_slice(z, part), :] = rows_ref[...]
-    for k in range(1, n):
-        copy(k).wait_recv()
-        out_ref[row_slice(lax.rem(z + n - k, n), part), :] = box[k]
-    for k in range(1, n):
-        copy(k).wait_send()
-
-
 def line_gather(rows):
-    n = lax.axis_size(SHARD)
-    whole = pl.BlockSpec(memory_space=pltpu.VMEM)
-    return pl.pallas_call(
-        functools.partial(gather_kernel, n),
-        out_shape=jax.ShapeDtypeStruct((n * rows.shape[0], rows.shape[1]), rows.dtype),
-        in_specs=[whole],
-        out_specs=whole,
-        scratch_shapes=[pltpu.VMEM((n,) + rows.shape, rows.dtype)]
-        + [pltpu.SemaphoreType.DMA((n,))] * 2,
-        compiler_params=pltpu.CompilerParams(collective_id=8, has_side_effects=True),
-        name="gather",
-    )(rows)
+    count, place = lax.axis_size(SHARD), lax.axis_index(SHARD)
+    part = rows.shape[0]
+    block = jnp.zeros((count * part, rows.shape[1]), rows.dtype)
+    block = lax.dynamic_update_slice_in_dim(block, rows, place * part, 0)
+    for k in reversed(range(1, count)):
+        got = lax.ppermute(rows, SHARD, [(i, i ^ k) for i in range(count)])
+        block = lax.dynamic_update_slice_in_dim(block, got, (place ^ k) * part, 0)
+    return block
 
 
 def shaped(array, dtype):
@@ -1300,6 +1268,284 @@
     return mixer_call(mix_backward_kernel, 6, outs, scratch, 4, widths, heads, operands)
 
 
+def finish_kernel(
+    count,
+    places,
+    widths,
+    *refs,
+):
+    arrays, refs = refs[: len(places[2])], refs[len(places[2]) :]
+    (
+        rows0,
+        rows1,
+        grad0,
+        grad1,
+        tiny0,
+        tiny1,
+        wide0,
+        wide1,
+        columns0,
+        columns1,
+        *refs,
+    ) = refs
+    (
+        query_out,
+        zx_out,
+        up_out,
+        down_out,
+        out_out,
+        rows_out,
+        grad_out,
+        shared_out,
+        tiny_out,
+        *refs,
+    ) = refs
+    boxes, refs = refs[: len(widths)], refs[len(widths) :]
+    (
+        rows_box,
+        grad_box,
+        tiny_box,
+        tiny_sum,
+        tiny_all,
+        wide_boxes,
+        columns_boxes,
+        blocks,
+        blocks_box,
+        shared,
+        shared_box,
+        send,
+        recv,
+        ctx_send,
+        ctx_recv,
+    ) = refs
+    section, place = lax.axis_index(SECTION), lax.axis_index(CTX)
+    bar = pltpu.get_barrier_semaphore()
+    pl.semaphore_signal(bar, inc=1, device_id={SECTION: 1 - section}, device_id_type=MESH)
+    for k in range(1, count):
+        peer = flipped(place, k, count)
+        pl.semaphore_signal(bar, inc=1, device_id={CTX: peer}, device_id_type=MESH)
+    pl.semaphore_wait(bar, count)
+    half = wide0.shape[1] // 2
+    own_half = pl.ds(pl.multiple_of(section * half, half), half)
+    other_half = pl.ds(pl.multiple_of((1 - section) * half, half), half)
+
+    def over(i, source, target):
+        return pltpu.make_async_remote_copy(
+            source,
+            target,
+            send.at[i],
+            recv.at[i],
+            device_id={SECTION: 1 - section},
+            device_id_type=MESH,
+        )
+
+    def across(i, k, source, target):
+        return pltpu.make_async_remote_copy(
+            source,
+            target,
+            ctx_send.at[i],
+            ctx_recv.at[i],
+            device_id={CTX: flipped(place, k, count)},
+            device_id_type=MESH,
+        )
+
+    def part(layer, i):
+        array, start, width = places[layer][i]
+        return arrays[array].at[:, start : start + width]
+
+    def by_section(act, first, second):
+        @pl.when(section == 1)
+        def _():
+            act(first)
+
+        @pl.when(section == 0)
+        def _():
+            act(second)
+
+    block = blocks.shape[2]
+    wides, columns = (wide0, wide1), (columns0, columns1)
+    early = [over(l, wides[l].at[:, other_half], wide_boxes.at[l]) for l in range(2)]
+    early += [over(2 + l, columns[l], columns_boxes.at[l]) for l in range(2)]
+    for copy in early:
+        copy.start()
+    pairs = [(tiny0, tiny1, tiny_box)]
+    pairs += [(part(0, i), part(1, i), box) for i, box in enumerate(boxes)]
+    pairs += [(rows0, rows1, rows_box), (grad0, grad1, grad_box)]
+    copies = [
+        (over(4 + i, first, box), over(4 + i, second, box))
+        for i, (first, second, box) in enumerate(pairs)
+    ]
+
+    def each(act, which):
+        for first, second in which:
+            by_section(act, first, second)
+
+    each(lambda copy: copy.start(), copies)
+    for copy in early:
+        copy.wait_recv()
+    dims = (((0,), (0,)), ((), ()))
+
+    def block_copy(l, k):
+        return across(2 * k + l, k, blocks.at[l, k], blocks_box.at[l, k])
+
+    for l in range(2):
+        total = lax.dot_general(
+            columns[l][...], wides[l][:, own_half], dims, preferred_element_type=f32
+        ) + lax.dot_general(columns_boxes[l], wide_boxes[l], dims, preferred_element_type=f32)
+        for k in range(count):
+            blocks[l, k] = total[k * block : (k + 1) * block, :].astype(bf16)
+        for k in range(1, count):
+            block_copy(l, k).start()
+    each(lambda copy: copy.wait_recv(), copies[:1])
+
+    def first_tiny(mine):
+        tiny_sum[...] = mine[...] + tiny_box[...]
+
+    by_section(first_tiny, tiny1, tiny0)
+    for k in range(1, count):
+        across(2 * count + k, k, tiny_sum, tiny_all.at[k]).start()
+
+    def place_pieces(low_core, take):
+        query, zx_a, zx_b, up_a, up_b, down_a, down_b, out_a, out_b = (
+            functools.partial(take, i) for i in range(9)
+        )
+        width = query_out.shape[1] // 2
+        query_out[:, pl.ds(pl.multiple_of(low_core * width, width), width)] = query()
+        edge = zx_out.shape[2] // 2
+        zx_out[low_core, :, :edge] = zx_a().astype(f32)
+        zx_out[low_core, :, edge:] = zx_b().astype(f32)
+        edge = up_out.shape[2] // 2
+        up_out[low_core, :, :edge] = up_a().astype(f32)
+        up_out[low_core, :, edge:] = up_b().astype(f32)
+        for target, pieces in ((down_out, (down_a, down_b)), (out_out, (out_a, out_b))):
+            for i, piece in enumerate(pieces):
+                height = target.shape[0] // 4
+                start = low_core * 2 * height + i * height
+                target[pl.ds(pl.multiple_of(start, height), height), :] = piece().T
+
+    def own(layer):
+        def take(i):
+            return part(layer, i)[...]
+
+        place_pieces(section, take)
+
+    by_section(own, 1, 0)
+    each(lambda copy: copy.wait_recv(), copies[1:])
+    place_pieces(1 - section, lambda i: boxes[i][...])
+
+    def rows_done(mine):
+        rows_out[section] = mine[0][...]
+        grad_out[section] = mine[1][...]
+
+    by_section(rows_done, (rows1, grad1), (rows0, grad0))
+    rows_out[1 - section] = rows_box[...]
+    grad_out[1 - section] = grad_box[...]
+    for l in range(2):
+        rows = blocks[l, 0].astype(f32)
+        for k in range(1, count):
+            block_copy(l, k).wait_recv()
+            rows += blocks_box[l, k].astype(f32)
+        shared[l] = rows.astype(bf16)
+    shared_copy = over(len(pairs) + 4, shared.at[1 - section], shared_box)
+    shared_copy.start()
+    everything = tiny_sum[...]
+    for k in range(1, count):
+        across(2 * count + k, k, tiny_sum, tiny_all.at[k]).wait_recv()
+        everything += tiny_all[k]
+    tiny_out[...] = everything
+
+    shared_out[:, own_half] = shared[section]
+    shared_copy.wait_recv()
+    shared_out[:, other_half] = shared_box[...]
+    for copy in early:
+        copy.wait_send()
+    each(lambda copy: copy.wait_send(), copies)
+    shared_copy.wait_send()
+    for k in range(1, count):
+        for l in range(2):
+            block_copy(l, k).wait_send()
+        across(2 * count + k, k, tiny_sum, tiny_all.at[k]).wait_send()
+
+
+def finish(first, second, rows, d_rows, tinies, wides, columns):
+    count = lax.axis_size(CTX)
+    arrays = (*first.ffn, first.proj, *first.out, *second.ffn, *second.mix)
+    up, down = first.ffn[0].shape[1] // 3 * 2, first.ffn[0].shape[1] // 3
+    out = first.out[0].shape[1]
+    step = 128
+    query = (first.proj.shape[1] - step) - 2 * (second.mix[1].shape[1] - step - out)
+    most = second.mix[1].shape[1] - step - out
+
+    def ffn(a):
+        return (a, 0, up), (a + 1, 0, up), (a, up, down), (a + 1, up, down)
+
+    places = (
+        (
+            (2, 0, query),
+            (2, query, most),
+            (2, query + most, most),
+            *ffn(0),
+            (3, 0, out),
+            (4, 0, out),
+        ),
+        (
+            (7, 0, query),
+            (7, query, most),
+            (8, 0, most),
+            *ffn(5),
+            (7, query + most, out),
+            (8, most + step, out),
+        ),
+        arrays,
+    )
+    length, part = first.proj.shape[0], rows[0].shape[0]
+    widths = [piece[2] for piece in places[0]]
+    half, block = wides[0].shape[1] // 2, columns[0].shape[1] // count
+    shape = jax.ShapeDtypeStruct
+    outs = [
+        shape((length, 2 * query), bf16),
+        shape((2, length, 2 * most), f32),
+        shape((2, length, 2 * up), f32),
+        shape((4 * down, length), bf16),
+        shape((4 * out, length), bf16),
+        shape((2,) + rows[0].shape, bf16),
+        shape((2,) + d_rows[0].shape, f32),
+        shape((block, 2 * half), bf16),
+        shape(tinies[0].shape, f32),
+    ]
+    tokens = columns[0].shape[0]
+    scratch = [pltpu.VMEM((length, w), bf16) for w in widths]
+    scratch += [
+        pltpu.VMEM(rows[0].shape, bf16),
+        pltpu.VMEM(d_rows[0].shape, f32),
+        pltpu.VMEM(tinies[0].shape, f32),
+        pltpu.VMEM(tinies[0].shape, f32),
+        pltpu.VMEM((count,) + tinies[0].shape, f32),
+        pltpu.VMEM((2, tokens, half), bf16),
+        pltpu.VMEM((2, tokens, count * block), bf16),
+        pltpu.VMEM((2, count, block, half), bf16),
+        pltpu.VMEM((2, count, block, half), bf16),
+        pltpu.VMEM((2, block, half), bf16),
+        pltpu.VMEM((block, half), bf16),
+    ]
+    over = len(widths) + 8
+    scratch += [pltpu.SemaphoreType.DMA((n,)) for n in (over, over, 3 * count, 3 * count)]
+    whole = pl.BlockSpec(memory_space=pltpu.VMEM)
+    operands = (*arrays, *rows, *d_rows, *tinies, *wides, *columns)
+    return pl.pallas_call(
+        functools.partial(finish_kernel, count, places, widths),
+        out_shape=outs,
+        in_specs=[whole] * len(operands),
+        out_specs=[whole] * len(outs),
+        scratch_shapes=scratch,
+        compiler_params=pltpu.CompilerParams(
+            collective_id=11, has_side_effects=True, vmem_limit_bytes=56 << 20
+        ),
+        cost_estimate=pl.CostEstimate(flops=0, bytes_accessed=20 << 20, transcendentals=0),
+        name="finish",
+    )(*operands)
+
+
 def norm_apply(values, gain):
     return values * lax.rsqrt(jnp.mean(values * values, axis=-1, keepdims=True) + eps) * gain
 
@@ -1404,11 +1650,11 @@
     return matmul_tn(both_batches(columns, columns), halves).astype(bf16)
 
 
-def shared_sums(normed, d_shared):
+def shared_columns(normed):
     place, count = lax.axis_index(CTX), lax.axis_size(CTX)
     shards = lax.axis_size(SHARD)
     block = normed.shape[1] // (count * shards)
-    columns = jnp.concatenate(
+    return jnp.concatenate(
         [
             lax.dynamic_slice_in_dim(
                 normed, ((place ^ k) * shards + lax.axis_index(SHARD)) * block, block, 1
@@ -1417,11 +1663,6 @@
         ],
         axis=1,
     )
-    total = weight_sums(columns, d_shared)
-    rows = total[:block].astype(f32)
-    for k in range(1, count):
-        rows = rows + flip(total[k * block : (k + 1) * block], k).astype(f32)
-    return rows.astype(bf16)
 
 
 def blocks_of(total):
@@ -1511,8 +1752,6 @@
         (sums_out,), (d_both,) = after((streams_of(sums_out),), d_both)
         grads.out = weight_scatter(sums_out)
     d_proj, d_vec = mix_backward(weights, saved, d_both, layout)
-    if last:
-        (grads.out,), (d_proj,) = after((grads.out,), d_proj)
     heads, widths = weights.heads, weights.widths
     grads.step_bias, grads.decay, grads.skip = (d_vec[i, :heads] for i in range(3))
     d_normed = matmul_nt(d_proj, weights.proj)
@@ -1557,7 +1796,7 @@
         )
         sums, grads.ffn = sums[:4], sums[4:]
         grads.sums_mix = sums
-    grads.shared = shared_sums(normed, d_shared)
+    grads.wide = d_shared
     return d_hidden, d_hidden_low, grads
 
 
@@ -1602,9 +1841,8 @@
         axis=1,
     )
     vectors = jnp.concatenate([norm_in[0], norm_ffn[0], step_bias[0], decay_rate[0], skip_gain[0]])
-    (proj, vectors), (rows_in,) = after((proj, vectors), rows_in)
     block_in = line_gather(rows_in)
-    (block_in,), (w_gate_up, w_attn_out) = after((block_in,), w_gate_up, w_attn_out)
+    (block_in,), (proj,) = after((block_in,), proj)
     own = (
         proj,
         jnp.concatenate([w_attn_out[0], w_mixer_out[0]], axis=0),
@@ -1650,27 +1888,21 @@
             block_cot = lax.all_gather(rows_cot, SHARD, axis=0, tiled=True)
         partial, saved = layer_forward(weights, normed, layout)
         first, second = layers
-        wanted = (2, 3) if layer == 0 else (0, 1)
-        wanted = [(0, own[i], other[i]) for i in wanted]
-        if layer == 0:
-            wanted.append((1, own[0], other[0]))
+        wanted = [(layer, own[i], other[i]) for i in (2, 3)]
         saved.middle, saved.ffn_in, chosen = copying_sum(
             middle_kernel, 1 + 8 * layer, f32, partial, hidden, weights.gain_ffn, wanted
         )
-        if layer == 0:
-            first.gate_up, first.down, second.proj = chosen
-        else:
-            first.proj, first.out = chosen
+        weights.gate_up, weights.down = chosen
         partial, saved.gate_pre, saved.upward, saved.product = ffn_forward(
             weights, saved.ffn_in
         )
         saves.append(saved)
         if layer == 0:
-            wanted = [(1, own[i], other[i]) for i in (1, 2, 3)]
+            wanted = [(1, own[i], other[i]) for i in (0, 1)]
             out_low, normed, chosen = copying_sum(
                 layer_end_kernel, 2, bf16, partial, saved.middle, second.gain_in, wanted
             )
-            second.out, second.gate_up, second.down = chosen
+            second.proj, second.out = chosen
             outs.append(own_rows(out_low))
             hidden = out_low.astype(f32)
         else:
@@ -1685,80 +1917,52 @@
         d_hiddens[layer] = d_hidden
         d_out = d_low
 
-    def by_layer(first, second):
-        kept = jnp.where(leading, first, second)
-        came = swap(jnp.where(leading, second, first))
-        return jnp.where(leading, kept, came), jnp.where(leading, came, kept)
-
     total = lax.psum_scatter(held.tail, SHARD, scatter_dimension=0, tiled=True)
     outs.append((own_rows(saves[1].middle) + total.astype(f32)).astype(bf16))
-    section_out = jnp.stack(by_layer(*outs))[None]
-    input_grad = jnp.stack(by_layer(own_rows(d_hiddens[0]), own_rows(d_hiddens[1])))[None]
-
-    def columns_of(first, second):
-        return jnp.concatenate(by_layer(first, second), axis=1).astype(f32)
-
-    def rows_of(first, second):
-        return jnp.concatenate([first.T, second.T], axis=0).astype(f32)
-
     first, second = grads
-    tiny = [
-        jnp.concatenate([g.gain_in, g.gain_ffn, g.step_bias, g.decay, g.skip]) for g in grads
-    ]
-    tiny = sum(by_layer(*tiny))
-    for bit in ctx_bits():
-        tiny = tiny + flip(tiny, bit)
+    tinies = []
+    for g in grads:
+        vector = jnp.concatenate([g.gain_in, g.gain_ffn, g.step_bias, g.decay, g.skip])
+        size = -(-vector.shape[0] // 1024) * 8
+        tinies.append(jnp.pad(vector, (0, size * 128 - vector.shape[0])).reshape(size, 128))
+    query, zx, up, down, out, out_rows, grad_rows, shared, tiny = finish(
+        first,
+        second,
+        outs,
+        [own_rows(d) for d in d_hiddens],
+        tinies,
+        [first.wide, second.wide],
+        [shared_columns(saved.normed) for saved in saves],
+    )
+    tiny = tiny.reshape(-1)
     place = lax.axis_index(CTX) * lax.axis_size(SHARD) + shard
     slot = width // (lax.axis_size(CTX) * lax.axis_size(SHARD))
     grad_in = lax.dynamic_slice_in_dim(tiny, place * slot, slot, 0)
     grad_ffn = lax.dynamic_slice_in_dim(tiny, width + place * slot, slot, 0)
     heads = tiny[2 * width :]
-
-    inner = w_mixer_in.shape[3]
-    query, most, both = query_width // 2, inner // 2, (query_width + inner) // 4
-    left, right = second.mix
-    parts = [
-        (left[:, :query], left[:, query : query + most], left[:, query + most :]),
-        (right[:, :most], right[:, most : most + head_count], right[:, right.shape[1] - both :]),
-    ]
-    proj = jnp.concatenate([*parts[0][:2], *parts[1][:2]], axis=1)
-    proj_low, proj_high = by_layer(first.proj[:, : proj.shape[1]], proj)
-    out_low, out_high = by_layer(
-        jnp.concatenate(first.out, axis=1), jnp.concatenate([p[2] for p in parts], axis=1)
+    step = jnp.where(
+        leading,
+        first.proj[:, first.proj.shape[1] - 128 :],
+        second.mix[1][:, zx.shape[2] // 2 : zx.shape[2] // 2 + 128],
     )
-    ffn_low, ffn_high = by_layer(
-        jnp.concatenate(first.ffn, axis=1), jnp.concatenate(second.ffn, axis=1)
-    )
-    step_at = query + inner
-    shared = columns_of(first.shared, second.shared)
     io_width = w_state_io.shape[2]
-    out = rows_of(out_low, out_high)
-    ff = w_gate_up.shape[3] // 2
-
-    def ffn_parts(total):
-        edge = total.shape[1] // 2
-        up = jnp.concatenate([total[:, :ff], total[:, edge : edge + ff]], axis=1)
-        return up, jnp.concatenate([total[:, ff:edge], total[:, edge + ff :]], axis=1)
-
-    (up_low, down_low), (up_high, down_high) = ffn_parts(ffn_low), ffn_parts(ffn_high)
-    gate_up = jnp.stack([up_low, up_high], axis=1)
     return (
-        section_out,
-        input_grad,
+        out_rows[None],
+        grad_rows[None],
         grad_in[None],
-        jnp.concatenate([proj_low[:, :query], proj_high[:, :query]], axis=1).astype(f32)[None],
-        shared[:, io_width:].reshape(-1, 2, KVH * HD)[None],
-        out[:query_width][None],
-        jnp.stack([p[:, query:step_at] for p in (proj_low, proj_high)], axis=1).astype(f32)[None],
-        shared[:, :io_width][None],
-        proj_low[:, step_at : step_at + head_count].astype(f32)[None],
+        query.astype(f32)[None],
+        shared[:, io_width:].astype(f32).reshape(-1, 2, KVH * HD)[None],
+        out[:query_width].astype(f32)[None],
+        jnp.swapaxes(zx, 0, 1)[None],
+        shared[:, :io_width].astype(f32)[None],
+        step[:, :head_count].astype(f32)[None],
         heads[:head_count][None],
         heads[head_count : 2 * head_count][None],
-        heads[2 * head_count :][None],
-        out[query_width:][None],
+        heads[2 * head_count : 3 * head_count][None],
+        out[query_width:].astype(f32)[None],
         grad_ffn[None],
-        gate_up.astype(f32)[None],
-        rows_of(down_low, down_high)[None],
+        jnp.swapaxes(up, 0, 1)[None],
+        down.astype(f32)[None],
     )
 
 

time: 832 us -> 795 us (0.956)
  Pallas kernels: 536 us -> 520 us
  local copies, waits for them, and re-layouts: 83.2 us -> 74.8 us
    pallas_call x4, Pallas kernels: 160 us -> 144 us  [mixer_call(): pl.pallas_call(functools.partial(kernel, count, widths, heads), out_shape...]
    select_n x10 -> x0, other arithmetic: 13.8 us -> none  [the longest x7 9.25 us: by_layer(): came = swap(jnp.where(leading, second, first))]
    unnamed x185 -> x108, local copies, waits for them, and re-layouts: 51.8 us -> 41.7 us
    ppermute x16 -> x8, starting transfers between devices: 17 us -> 7.94 us  [flip(): lax.ppermute(values, CTX, [(i, i ^ bit) for i in range(lax.axis_size(CTX))])]
  transfers between devices with their start and end apart: 38 -> 22, of which waited for: 6 -> 1; matrix products, arithmetic and copies ran while one was open for 24% -> 25% of each run, Pallas kernels for 65% -> 63%
where the time goes in v1:
time: 795 us; the launch traced here: 782 us
  Pallas kernels  520 us (65%)
  matrix products  101 us (13%)
  local copies, waits for them, and re-layouts  74.8 us (9%)
  other arithmetic  50.6 us (6%)
  between operations  16.6 us (2%)
  starting transfers between devices  15.3 us (2%)
    pallas_call x7, Pallas kernels, summed(): pl.pallas_call(functools.partial(kernel, n, CHUNKS, LAG), out_shape=outs,...  349 us
    pallas_call x4, Pallas kernels, mixer_call(): pl.pallas_call(functools.partial(kernel, count, widths, heads), out_shape...  144 us
    dot_general x8, matrix products, matmul_nt(): lax.dot_general(left, right, (((1,), (1,)), ((), ())), preferred_element_...  50.7 us
    dot_general x8, matrix products, matmul(): return jnp.dot(left, right, preferred_element_type=f32)  44 us
    unnamed x108, local copies, waits for them, and re-layouts  41.7 us
    pallas_call x1, Pallas kernels, finish(): pl.pallas_call(functools.partial(finish_kernel, count, places, widths), o...  28.2 us
  transfers between devices with their start and end apart: 22, of which 1 were waited for; matrix products, arithmetic and copies ran while one was open for 25% of the time, Pallas kernels for 63%

profile of v1, /device:TPU:0, one launch (start us, length us, event | category | flops | bytes accessed | tf_op | source)
XLA Modules:
  0.0 781.9 jit_solution(10147589343443074933)
XLA Ops:
  9.1 5.0 collective-permute-start
  18.0 6.8 copy.55
  37.9 10.2 %copy.58 = bf16[256,8,2,1024]{3,1,2,0:T(8,128)(2,1)} copy(bf16[256,8,2,1024]{3,2,1,0:T(2,128)(2,1)} %bitcast.187) | data formatting | bytes 16777216
  48.8 4.5 pad_maximum_fusion.refs_1_
  68.7 9.3 %fusion.1.proj_ref = f32[256,2688]{1,0:T(8,128)} fusion(bf16[256,2048]{1,0:T(8,128)(2,1)} %multiply_convert_fusion, bf16[2048,2688]{1,0:T(8,128)(2,1)} %constant_dynamic-update-slice_fusion.refs_0_, bf16[2048,2688]{1,0:T(8,128)(2,1)} %collective-permute-done.4.refs_2_, pred[]{:T(512)S(6)} %eq.52), kind=kOutput, calls=%fused_computation.2 | convolution fusion | flops 2824077312 | bytes 25821184 | tf_op jit(solution)/shard_map/dot_general | solution.py:1554
  78.0 29.4 %mixer5.2 = (bf16[256,1024]{1,0:T(8,128)(2,1)}, f32[256,768]{1,0:T(8,128)}, bf16[768,256]{1,0:T(8,128)(2,1)}, bf16[1024,256]{1,0:T(8,128)(2,1)}, f32[4,16,256]{2,1,0:T(8,128)}) custom-call(f32[256,2688]{1,0:T(8,128)} %fusion.1.proj_ref, f32[8,128]{1,0:T(8,128)} %pad.23.vec_ref, f32[1,768]{1,0:T(1,128)} %broadcast_in_dim_reshape.13.skip_ref, ...), custom_call_target="tpu_custom_call" | custom-call | bytes 20971520 | tf_op jit(solution)/shard_map/mixer5/pallas_call | solution.py:1174
  107.4 3.7 fusion.9.p_ref
  111.1 37.6 %line_sum1.1 = (f32[256,2048]{1,0:T(8,128)}, bf16[256,2048]{1,0:T(8,128)(2,1)}, bf16[2048,2048]{1,0:T(8,128)(2,1)}, bf16[1024,2048]{1,0:T(8,128)(2,1)}) custom-call(f32[256,2048]{1,0:T(8,128)} %fusion.9.p_ref, f32[256,2048]{1,0:T(8,128)} %convert_element_type.287.h_ref.v_ref, f32[1,2048]{1,0:T(1,128)} %bitcast.206, bf16[2048,2048]{1,0:T(8,128)(2,1)} %bitcast.184, ...), custom_call_target="tpu_custom_call" | custom-call | bytes 20971520 | tf_op jit(solution)/shard_map/line_sum1/pallas_call | solution.py:580
  148.7 6.2 fusion.43
  157.9 37.4 %line_sum2.1 = (bf16[256,2048]{1,0:T(8,128)(2,1)}, bf16[256,2048]{1,0:T(8,128)(2,1)}, bf16[2048,2688]{1,0:T(8,128)(2,1)}, bf16[1024,2048]{1,0:T(8,128)(2,1)}) custom-call(f32[256,2048]{1,0:T(8,128)} %fusion.44.p_ref, f32[256,2048]{1,0:T(8,128)} %get-tuple-element.100.h_ref.refs_2_, f32[1,2048]{1,0:T(1,128)} %bitcast.204, ...), custom_call_target="tpu_custom_call" | custom-call | bytes 20971520 | tf_op jit(solution)/shard_map/line_sum2/pallas_call | solution.py:580
  199.2 9.0 %fusion.45.proj_ref = f32[256,2688]{1,0:T(8,128)} fusion(bf16[256,2048]{1,0:T(8,128)(2,1)S(1)} %copy-done.11, bf16[2048,2688]{1,0:T(8,128)(2,1)} %get-tuple-element.103), kind=kOutput, calls=%fused_computation.177 | convolution fusion | flops 2818572288 | bytes 14811136 | tf_op jit(solution)/shard_map/dot_general | solution.py:1554
  208.2 32.4 %mixer5.3 = (bf16[256,1024]{1,0:T(8,128)(2,1)}, f32[256,768]{1,0:T(8,128)}, bf16[768,256]{1,0:T(8,128)(2,1)}, bf16[1024,256]{1,0:T(8,128)(2,1)}, f32[4,16,256]{2,1,0:T(8,128)}) custom-call(f32[256,2688]{1,0:T(8,128)} %fusion.45.proj_ref, f32[8,128]{1,0:T(8,128)} %pad.25.vec_ref, f32[1,768]{1,0:T(1,128)} %broadcast_in_dim_reshape.14.skip_ref, ...), custom_call_target="tpu_custom_call" | custom-call | bytes 20971520 | tf_op jit(solution)/shard_map/mixer5/pallas_call | solution.py:1174
  244.2 37.1 %line_sum9.1 = (f32[256,2048]{1,0:T(8,128)}, bf16[256,2048]{1,0:T(8,128)(2,1)}, bf16[2048,2048]{1,0:T(8,128)(2,1)}, bf16[1024,2048]{1,0:T(8,128)(2,1)}) custom-call(f32[256,2048]{1,0:T(8,128)} %fusion.46.p_ref, f32[256,2048]{1,0:T(8,128)} %convert_element_type.305.h_ref.refs_3_, f32[1,2048]{1,0:T(1,128)} %bitcast.208, bf16[2048,2048]{1,0:T(8,128)(2,1)} %bitcast.185, ...), custom_call_target="tpu_custom_call" | custom-call | bytes 20971520 | tf_op jit(solution)/shard_map/line_sum9/pallas_call | solution.py:580
  283.8 7.3 fusion.47
  291.2 4.8 multiply_convert_fusion.5
  296.0 7.4 fusion.40.refs_0_
  306.7 41.0 %line_sum3.1 = (f32[256,2048]{1,0:T(8,128)}, bf16[256,2048]{1,0:T(8,128)(2,1)}, f32[8,2048]{1,0:T(8,128)}, bf16[2,512,768]{2,1,0:T(8,128)(2,1)}, bf16[2,512,768]...) custom-call(f32[256,2048]{1,0:T(8,128)} %fusion.40.refs_0_, ...), custom_call_target="tpu_custom_call" | custom-call | bytes 20971520 | tf_op jit(solution)/shard_map/line_sum3/pallas_call | solution.py:580
  347.7 4.8 fusion.48.d_both_ref
  352.4 35.5 %mixer6.2 = (bf16[256,2688]{1,0:T(8,128)(2,1)}, f32[8,128]{1,0:T(8,128)}) custom-call(f32[256,2688]{1,0:T(8,128)} %fusion.45.proj_ref, f32[8,128]{1,0:T(8,128)} %pad.25.vec_ref, f32[1,768]{1,0:T(1,128)} %broadcast_in_dim_reshape.14.skip_ref, f32[256,8]{1,0:T(8,128)} %pad.24.tok_ref, f32[2,1024]{1,0:T(2,128)} %pad_maximum_fusion.11.key_ref, ...), custom_call_target="tpu_custom_call" | custom-call | bytes 20971520 | tf_op jit(solution)/shard_map/mixer6/pallas_call | solution.py:1174
  388.0 9.0 %fusion.49.refs_0_ = f32[256,2048]{1,0:T(8,128)} fusion(bf16[256,2688]{1,0:T(8,128)(2,1)} %get-tuple-element.118.refs_7_, bf16[2048,2688]{1,0:T(8,128)(2,1)} %get-tuple-element.103), kind=kOutput, calls=%fused_computation.181 | convolution fusion | flops 2818572288 | bytes 14483456 | tf_op jit(solution)/shard_map/dot_general | solution.py:1558
  402.3 64.9 %line_sum4.1 = (f32[256,2048]{1,0:T(8,128)}, bf16[256,2048]{1,0:T(8,128)(2,1)}, f32[8,2048]{1,0:T(8,128)}, bf16[256,1024]{1,0:T(8,128)(2,1)}, bf16[2,512,768]{2,...) custom-call(f32[256,2048]{1,0:T(8,128)} %fusion.49.refs_0_, ...), custom_call_target="tpu_custom_call" | custom-call | bytes 20971520 | tf_op jit(solution)/shard_map/line_sum4/pallas_call | solution.py:580
  467.2 4.1 multiply_convert_fusion.2
  471.3 7.1 fusion.39.refs_0_
  479.4 63.7 %line_sum10.1 = (f32[256,2048]{1,0:T(8,128)}, bf16[256,2048]{1,0:T(8,128)(2,1)}, f32[8,2048]{1,0:T(8,128)}, bf16[2,512,768]{2,1,0:T(8,128)(2,1)}, bf16[2,512,768...) custom-call(f32[256,2048]{1,0:T(8,128)} %fusion.39.refs_0_, ...), custom_call_target="tpu_custom_call" | custom-call | bytes 20971520 | tf_op jit(solution)/shard_map/line_sum10/pallas_call | solution.py:580
  546.1 4.6 fusion.8.d_both_ref
  557.1 46.3 %mixer6.3 = (bf16[256,2688]{1,0:T(8,128)(2,1)}, f32[8,128]{1,0:T(8,128)}) custom-call(f32[256,2688]{1,0:T(8,128)} %fusion.1.proj_ref, f32[8,128]{1,0:T(8,128)} %pad.23.vec_ref, f32[1,768]{1,0:T(1,128)} %broadcast_in_dim_reshape.13.skip_ref, f32[256,8]{1,0:T(8,128)} %pad.24.tok_ref, f32[2,1024]{1,0:T(2,128)} %pad_maximum_fusion.11.key_ref, ...), custom_call_target="tpu_custom_call" | custom-call | bytes 20971520 | tf_op jit(solution)/shard_map/mixer6/pallas_call | solution.py:1174
  610.4 9.0 %fusion.p_ref = f32[256,2048]{1,0:T(8,128)} fusion(bf16[256,2688]{1,0:T(8,128)(2,1)S(1)} %copy-done.10, bf16[2048,2688]{1,0:T(8,128)(2,1)} %constant_dynamic-update-slice_fusion.refs_0_, bf16[2048,2688]{1,0:T(8,128)(2,1)} %collective-permute-done.4.refs_2_, pred[]{:T(512)S(6)} %eq.52), kind=kOutput, calls=%fused_computation.1 | convolution fusion | flops 2824077312 | bytes 25493504 | tf_op jit(solution)/shard_map/dot_general | solution.py:1558
  629.1 4.1 convolution_convert_fusion
  639.0 67.0 %line_sum7.1 = (f32[256,2048]{1,0:T(8,128)}, bf16[256,2048]{1,0:T(8,128)(2,1)}, f32[8,2048]{1,0:T(8,128)}, bf16[256,1024]{1,0:T(8,128)(2,1)}, bf16[512,1024]{1,0:T(8,128)(2,1)}) custom-call(f32[256,2048]{1,0:T(8,128)} %fusion.p_ref, bf16[256,1024]{1,0:T(8,128)(2,1)} %copy-done.15, f32[256,2048]{1,0:T(8,128)} %get-tuple-element.141.d_ref, ...), custom_call_target="tpu_custom_call" | custom-call | bytes 20971520 | tf_op jit(solution)/shard_map/line_sum7/pallas_call | solution.py:580
  722.0 28.2 %finish.1 = (bf16[512,256]{1,0:T(8,128)(2,1)}, f32[2,512,768]{2,1,0:T(8,128)}, f32[2,512,1024]{2,1,0:T(8,128)}, bf16[1024,512]{1,0:T(8,128)(2,1)}, bf16[1024,512...) custom-call(bf16[512,768]{1,0:T(8,128)(2,1)} %add_convert_fusion.1.r, ...), custom_call_target="tpu_custom_call" | custom-call | bytes 20971520 | tf_op jit(solution)/shard_map/finish/pallas_call | solution.py:1535
  757.0 6.1 copy.51
  764.4 5.2 copy.53
  (262 shorter events, 116.6 us)
Async XLA Ops:
  7.2 17.6 %copy-start = (bf16[1,2048,2,256]{3,2,1,0:T(2,128)(2,1)S(1)}, bf16[1,2048,2,256]{3,2,1,0:T(2,128)(2,1)}, u32[]{:S(2)}) copy-start(bf16[1,2048,2,256]{3,2,1,0:T(2,128)(2,1)} %param.22) | copy-start | bytes 6291460
  7.2 284.0 %all-gather.2.cloned.1.call-start = ((), (), s32[]{:S(2)}) async-start(), calls=%async_computation.1 | async-start | bytes 1310720 | tf_op jit(solution)/shard_map/all_gather | solution.py:1888
  9.1 24.0 %collective-permute-start = (bf16[64,2048]{1,0:T(8,128)(2,1)}, bf16[64,2048]{1,0:T(8,128)(2,1)}, u32[]{:S(2)}, u32[]{:S(2)}) collective-permute-start(bf16[64,2048]{1,0:T(8,128)(2,1)} %get-tuple-element.237), channel_id=1, source_target_pairs={{0,3},{1,2},{2,1},{3,0},{4,7},{5,6},{6,5},{7,4},{8,11},{9,10},{10,... | collective-permute-start | bytes 786440 | tf_op jit(solution)/shard_map/ppermute | solution.py:602
  14.1 22.6 %collective-permute-start.1 = (bf16[64,2048]{1,0:T(8,128)(2,1)}, bf16[64,2048]{1,0:T(8,128)(2,1)}, u32[]{:S(2)}, u32[]{:S(2)}) collective-permute-start(bf16[64,2048]{1,0:T(8,128)(2,1)} %get-tuple-element.237), channel_id=1, source_target_pairs={{0,2},{1,3},{2,0},{3,1},{4,6},{5,7},{6,4},{7,5},{8,10},{9,11},{10,... | collective-permute-start | bytes 786440 | tf_op jit(solution)/shard_map/ppermute | solution.py:602
  14.1 23.6 %collective-permute-start.2 = (bf16[64,2048]{1,0:T(8,128)(2,1)}, bf16[64,2048]{1,0:T(8,128)(2,1)S(1)}, u32[]{:S(2)}, u32[]{:S(2)}) collective-permute-start(bf16[64,2048]{1,0:T(8,128)(2,1)} %get-tuple-element.237), channel_id=1, source_target_pairs={{0,1},{1,0},{2,3},{3,2},{4,5},{5,4},{6,7},{7,6},{8,9},{9,8},{10,11... | collective-permute-start | bytes 786440 | tf_op jit(solution)/shard_map/ppermute | solution.py:602
  37.8 30.9 %collective-permute-start.4 = (bf16[2048,2688]{1,0:T(8,128)(2,1)}, bf16[2048,2688]{1,0:T(8,128)(2,1)}, u32[]{:S(2)}, u32[]{:S(2)}) collective-permute-start(bf16[2048,2688]{1,0:T(8,128)(2,1)} %constant_dynamic-update-slice_fusion.refs_0_), channel_id=1, source_target_pairs={{0,16},{16,0},{1,17},{17,1},{2,18},{18,2},{3,19},{19,3},{4,20},{20... | collective-permute-start | bytes 33030152 | tf_op jit(solution)/shard_map/ppermute | solution.py:1566
  48.2 62.9 %collective-permute-start.6 = (bf16[2048,2048]{1,0:T(8,128)(2,1)}, bf16[2048,2048]{1,0:T(8,128)(2,1)}, u32[]{:S(2)}, u32[]{:S(2)}) collective-permute-start(bf16[2048,2048]{1,0:T(8,128)(2,1)} %bitcast.183), channel_id=1, source_target_pairs={{0,16},{16,0},{1,17},{17,1},{2,18},{18,2},{3,19},{19,3},{4,20},{20... | collective-permute-start | bytes 25165832 | tf_op jit(solution)/shard_map/ppermute | solution.py:1566
  48.7 11.0 %collective-permute-start.3 = (f32[4132]{0:T(1024)S(1)}, f32[4132]{0:T(1024)S(1)}, u32[]{:S(2)}, u32[]{:S(2)}) collective-permute-start(f32[4132]{0:T(1024)S(1)} %concatenate.57), channel_id=1, source_target_pairs={{0,16},{16,0},{1,17},{17,1},{2,18},{18,2},{3,19},{19,3},{4,20},{20... | collective-permute-start | bytes 49592 | tf_op jit(solution)/shard_map/ppermute | solution.py:1566
  53.4 54.1 %collective-permute-start.5 = (bf16[1024,2048]{1,0:T(8,128)(2,1)}, bf16[1024,2048]{1,0:T(8,128)(2,1)}, u32[]{:S(2)}, u32[]{:S(2)}) collective-permute-start(bf16[1024,2048]{1,0:T(8,128)(2,1)} %pad_maximum_fusion.refs_1_), channel_id=1, source_target_pairs={{0,16},{16,0},{1,17},{17,1},{2,18},{18,2},{3,19},{19,3},{4,20},{20... | collective-permute-start | bytes 12582920 | tf_op jit(solution)/shard_map/ppermute | solution.py:1566
  53.8 57.3 %collective-permute-start.7 = (bf16[1024,2048]{1,0:T(8,128)(2,1)}, bf16[1024,2048]{1,0:T(8,128)(2,1)}, u32[]{:S(2)}, u32[]{:S(2)}) collective-permute-start(bf16[1024,2048]{1,0:T(8,128)(2,1)} %bitcast.19.refs_1_), channel_id=1, source_target_pairs={{0,16},{16,0},{1,17},{17,1},{2,18},{18,2},{3,19},{19,3},{4,20},{20... | collective-permute-start | bytes 12582920 | tf_op jit(solution)/shard_map/ppermute | solution.py:1566
  66.5 560.7 %collective-permute-start.12 = (bf16[256,2048]{1,0:T(8,128)(2,1)}, bf16[256,2048]{1,0:T(8,128)(2,1)}, u32[]{:S(2)}, u32[]{:S(2)}) collective-permute-start(bf16[256,2048]{1,0:T(8,128)(2,1)} %multiply_convert_fusion), channel_id=1, source_target_pairs={{0,16},{16,0},{1,17},{17,1},{2,18},{18,2},{3,19},{19,3},{4,20},{20... | collective-permute-start | bytes 3145736 | tf_op jit(solution)/shard_map/ppermute | solution.py:1566
  68.7 38.7 %copy-start.4 = (bf16[1,768,2048]{2,1,0:T(8,128)(2,1)S(1)}, bf16[1,768,2048]{2,1,0:T(8,128)(2,1)}, u32[]{:S(2)}) copy-start(bf16[1,768,2048]{2,1,0:T(8,128)(2,1)} %param.30) | copy-start | bytes 9437188
  198.4 516.4 %reduce-scatter.2.cloned.1.call-start = ((), (), s32[]{:S(2)}) async-start(), calls=%async_computation.2 | async-start | bytes 1310720 | tf_op jit(solution)/shard_map/reduce_scatter | solution.py:1920
  199.2 354.9 %collective-permute-start.14 = (bf16[256,512]{1,0:T(8,128)(2,1)}, bf16[256,512]{1,0:T(8,128)(2,1)}, u32[]{:S(2)}, u32[]{:S(2)}) collective-permute-start(bf16[256,512]{1,0:T(8,128)(2,1)} %get-tuple-element.268), channel_id=1, source_target_pairs={{0,16},{16,0},{1,17},{17,1},{2,18},{18,2},{3,19},{19,3},{4,20},{20... | collective-permute-start | bytes 786440 | tf_op jit(solution)/shard_map/ppermute | solution.py:1566
  199.2 41.3 %copy-start.42 = (bf16[1024,2048]{1,0:T(8,128)(2,1)S(1)}, bf16[1024,2048]{1,0:T(8,128)(2,1)}, u32[]{:S(2)}) copy-start(bf16[1024,2048]{1,0:T(8,128)(2,1)} %get-tuple-element.110) | copy-start | bytes 12582916
  402.3 64.9 %copy-start.7 = (f32[256,2048]{1,0:T(8,128)S(1)}, f32[256,2048]{1,0:T(8,128)}, u32[]{:S(2)}) copy-start(f32[256,2048]{1,0:T(8,128)} %copy-done.6) | copy-start | bytes 6291460
  479.4 66.5 %copy-start.33 = (f32[8,2048]{1,0:T(8,128)S(1)}, f32[8,2048]{1,0:T(8,128)}, u32[]{:S(2)}) copy-start(f32[8,2048]{1,0:T(8,128)} %get-tuple-element.158) | copy-start | bytes 196612
  479.4 66.5 %copy-start.32 = (f32[8,2048]{1,0:T(8,128)S(1)}, f32[8,2048]{1,0:T(8,128)}, u32[]{:S(2)}) copy-start(f32[8,2048]{1,0:T(8,128)} %get-tuple-element.159) | copy-start | bytes 196612
  479.4 66.6 %copy-start.20 = (bf16[1,256,2048]{2,1,0:T(8,128)(2,1)S(1)}, bf16[1,256,2048]{2,1,0:T(8,128)(2,1)}, u32[]{:S(2)}) copy-start(bf16[1,256,2048]{2,1,0:T(8,128)(2,1)} %param.23) | copy-start | bytes 3145732
  543.1 77.6 %collective-permute-start.8 = (bf16[1024,768]{1,0:T(8,128)(2,1)}, bf16[1024,768]{1,0:T(8,128)(2,1)}, u32[]{:S(2)}, u32[]{:S(2)}) collective-permute-start(bf16[1024,768]{1,0:T(8,128)(2,1)} %bitcast.223), channel_id=1, source_target_pairs={{0,8},{4,12},{8,0},{12,4},{1,9},{5,13},{9,1},{13,5},{2,10},{6,14},... | collective-permute-start | bytes 4718600 | tf_op jit(solution)/shard_map/ppermute | solution.py:1619
  544.2 80.4 %collective-permute-start.10 = (bf16[1024,768]{1,0:T(8,128)(2,1)}, bf16[1024,768]{1,0:T(8,128)(2,1)}, u32[]{:S(2)}, u32[]{:S(2)}) collective-permute-start(bf16[1024,768]{1,0:T(8,128)(2,1)} %bitcast.222), channel_id=1, source_target_pairs={{0,4},{4,0},{8,12},{12,8},{1,5},{5,1},{9,13},{13,9},{2,6},{6,2},{1... | collective-permute-start | bytes 4718600 | tf_op jit(solution)/shard_map/ppermute | solution.py:1619
  545.1 9.0 %collective-permute-start.13 = (bf16[256,2048]{1,0:T(8,128)(2,1)}, bf16[256,2048]{1,0:T(8,128)(2,1)}, u32[]{:S(2)}, u32[]{:S(2)}) collective-permute-start(bf16[256,2048]{1,0:T(8,128)(2,1)} %get-tuple-element.137), channel_id=1, source_target_pairs={{0,16},{16,0},{1,17},{17,1},{2,18},{18,2},{3,19},{19,3},{4,20},{20... | collective-permute-start | bytes 3145736 | tf_op jit(solution)/shard_map/ppermute | solution.py:1566
  610.3 18.9 %collective-permute-start.15 = (bf16[256,1024]{1,0:T(8,128)(2,1)S(1)}, bf16[256,1024]{1,0:T(8,128)(2,1)}, u32[]{:S(2)}, u32[]{:S(2)}) collective-permute-start(bf16[256,1024]{1,0:T(8,128)(2,1)S(1)} %pad_maximum_fusion.8), channel_id=1, source_target_pairs={{0,16},{16,0},{1,17},{17,1},{2,18},{18,2},{3,19},{19,3},{4,20},{20... | collective-permute-start | bytes 1572872 | tf_op jit(solution)/shard_map/ppermute | solution.py:1566
  610.3 12.1 %copy-start.14 = (bf16[2,512,768]{2,1,0:T(8,128)(2,1)S(1)}, bf16[2,512,768]{2,1,0:T(8,128)(2,1)}, u32[]{:S(2)}) copy-start(bf16[2,512,768]{2,1,0:T(8,128)(2,1)} %get-tuple-element.129) | copy-start | bytes 4718596
  610.4 25.6 %collective-permute-start.16 = (bf16[1024,256]{1,0:T(8,128)(2,1)S(1)}, bf16[1024,256]{1,0:T(8,128)(2,1)}, u32[]{:S(2)}, u32[]{:S(2)}) collective-permute-start(bf16[1024,256]{1,0:T(8,128)(2,1)S(1)} %bitcast.201), channel_id=1, source_target_pairs={{0,8},{4,12},{8,0},{12,4},{1,9},{5,13},{9,1},{13,5},{2,10},{6,14},... | collective-permute-start | bytes 1572872 | tf_op jit(solution)/shard_map/ppermute | solution.py:1619
  620.7 18.0 %collective-permute-start.18 = (bf16[1024,256]{1,0:T(8,128)(2,1)S(1)}, bf16[1024,256]{1,0:T(8,128)(2,1)S(1)}, u32[]{:S(2)}, u32[]{:S(2)}) collective-permute-start(bf16[1024,256]{1,0:T(8,128)(2,1)S(1)} %bitcast.200), channel_id=1, source_target_pairs={{0,4},{4,0},{8,12},{12,8},{1,5},{5,1},{9,13},{13,9},{2,6},{6,2},{1... | collective-permute-start | bytes 1572872 | tf_op jit(solution)/shard_map/ppermute | solution.py:1619
  624.7 92.0 %collective-permute-start.9 = (bf16[512,768]{1,0:T(8,128)(2,1)}, bf16[512,768]{1,0:T(8,128)(2,1)}, u32[]{:S(2)}, u32[]{:S(2)}) collective-permute-start(bf16[512,768]{1,0:T(8,128)(2,1)} %fusion.12), channel_id=1, source_target_pairs={{0,4},{4,0},{8,12},{12,8},{1,5},{5,1},{9,13},{13,9},{2,6},{6,2},{1... | collective-permute-start | bytes 2359304 | tf_op jit(solution)/shard_map/ppermute | solution.py:1619
  627.2 92.3 %collective-permute-start.11 = (bf16[512,768]{1,0:T(8,128)(2,1)}, bf16[512,768]{1,0:T(8,128)(2,1)}, u32[]{:S(2)}, u32[]{:S(2)}) collective-permute-start(bf16[512,768]{1,0:T(8,128)(2,1)} %fusion.10), channel_id=1, source_target_pairs={{0,8},{4,12},{8,0},{12,4},{1,9},{5,13},{9,1},{13,5},{2,10},{6,14},... | collective-permute-start | bytes 2359304 | tf_op jit(solution)/shard_map/ppermute | solution.py:1619
  637.0 74.2 %collective-permute-start.17 = (bf16[512,256]{1,0:T(8,128)(2,1)S(1)}, bf16[512,256]{1,0:T(8,128)(2,1)S(1)}, u32[]{:S(2)}, u32[]{:S(2)}) collective-permute-start(bf16[512,256]{1,0:T(8,128)(2,1)S(1)} %fusion.26), channel_id=1, source_target_pairs={{0,4},{4,0},{8,12},{12,8},{1,5},{5,1},{9,13},{13,9},{2,6},{6,2},{1... | collective-permute-start | bytes 786440 | tf_op jit(solution)/shard_map/ppermute | solution.py:1619
  638.7 67.3 %copy-start.23 = (bf16[1024,256]{1,0:T(8,128)(2,1)}, bf16[1024,256]{1,0:T(8,128)(2,1)S(1)}, u32[]{:S(2)}) copy-start(bf16[1024,256]{1,0:T(8,128)(2,1)S(1)} %collective-permute-done.18) | copy-start | bytes 1572868
  638.8 74.2 %collective-permute-start.19 = (bf16[512,256]{1,0:T(8,128)(2,1)S(1)}, bf16[512,256]{1,0:T(8,128)(2,1)}, u32[]{:S(2)}, u32[]{:S(2)}) collective-permute-start(bf16[512,256]{1,0:T(8,128)(2,1)S(1)} %fusion.24), channel_id=1, source_target_pairs={{0,8},{4,12},{8,0},{12,4},{1,9},{5,13},{9,1},{13,5},{2,10},{6,14},... | collective-permute-start | bytes 786440 | tf_op jit(solution)/shard_map/ppermute | solution.py:1619
  639.0 68.9 %copy-start.37 = (f32[12]{0:T(128)S(1)}, f32[12]{0:T(128)}, u32[]{:S(2)}) copy-start(f32[12]{0:T(128)} %get-tuple-element.291) | copy-start | bytes 148
  (36 other events, 229.8 us)
Sparse Core Ops, SparseCore 0:
  198.6 30.1 all-gather.1
  545.2 25.1 reduce-scatter.1

commit v2 on v1

--- a/solution.py
+++ b/solution.py
@@ -345,60 +345,11 @@
             copy.wait_send()
 
 
-class Scatter:
-    def __init__(self, blocks, out, inbox, send, recv):
-        self.blocks, self.out, self.inbox, self.send, self.recv = blocks, out, inbox, send, recv
-        self.count, self.place = lax.axis_size(CTX), lax.axis_index(CTX)
-
-    def peer(self, k):
-        return flipped(self.place, k, self.count)
-
-    def copy(self, k):
-        return pltpu.make_async_remote_copy(
-            self.blocks.at[k],
-            self.inbox.at[k],
-            self.send.at[k],
-            self.recv.at[k],
-            device_id={CTX: self.peer(k)},
-            device_id_type=MESH,
-        )
-
-    def greet(self, bar):
-        for k in range(1, self.count):
-            pl.semaphore_signal(bar, inc=1, device_id={CTX: self.peer(k)}, device_id_type=MESH)
-        return self.count - 1
-
-    def start(self):
-        for k in reversed(range(1, self.count)):
-            self.copy(k).start()
-
-    def step(self, i, steps):
-        pass
-
-    def finish(self):
-        rows = 64
-
-        for k in range(1, self.count):
-            self.copy(k).wait_recv()
-
-        def add(j, _):
-            part = row_slice(j, rows)
-            total = self.blocks[0, part, :].astype(f32)
-            for k in range(1, self.count):
-                total += self.inbox[k, part, :].astype(f32)
-            self.out[part, :] = total.astype(bf16)
-            return 0
-
-        lax.fori_loop(0, self.out.shape[0] // rows, add, 0)
-        for k in range(1, self.count):
-            self.copy(k).wait_send()
-
-
 class Halving:
     cuts = 2
-    turns = (11, 20)
-
-    def __init__(self, streams, outs, scratch):
+
+    def __init__(self, streams, outs, scratch, turns):
+        self.turns = turns
         self.place, self.count = lax.axis_index(CTX), lax.axis_size(CTX)
         self.streams, self.outs = streams, outs
         self.orders = ctx_orders()
@@ -464,6 +415,8 @@
                 self.advance(0, cut)
 
     def finish(self):
+        for cut in range(len(self.turns), self.cuts):
+            self.advance(0, cut)
         for level in range(1, self.levels):
             for cut in range(self.cuts):
                 self.advance(level, cut)
@@ -501,9 +454,9 @@
             job.finish()
 
 
-def scatter_kernel(n, chunks, lag, p_ref, q_ref, d_ref, v_ref, gain_ref, blocks, *refs):
-    outs, out, scratch = refs[:4], refs[4], refs[5:]
-    job = Scatter(blocks, out, *scratch[9:])
+def scatter_kernel(n, chunks, lag, p_ref, q_ref, d_ref, v_ref, gain_ref, *refs):
+    streams, outs, totals, scratch = refs[:4], refs[4:8], refs[8:10], refs[10:]
+    job = Halving(streams, totals, scratch[9:], (7, 14))
     back_rows(n, chunks, lag, p_ref, d_ref, v_ref, gain_ref, *outs[:3], scratch[:9], job, q_ref, outs[3])
 
 
@@ -524,7 +477,8 @@
     cut = len(xs) + 2 * len(plan) + 2
     fill = Fill(plan, xs, ys, sums, refs[9 : 9 + cut])
     if ready:
-        fill = Together(fill, Halving(streams, totals, refs[9 + cut :]))
+        turns = (11, 20) if beside else (14,)
+        fill = Together(fill, Halving(streams, totals, refs[9 + cut :], turns))
     outs = out_ref, low_ref, gg_ref
     back_rows(n, chunks, lag, p_ref, d_ref, v_ref, gain_ref, *outs, refs[:9], fill, q_ref, q_out)
 
@@ -571,7 +525,7 @@
     line_sum(n, chunks, lag, p_rows, done, *scratch, fill=fill)
 
 
-def summed(kernel, collective, outs, *operands, extra=(), more=0, far=(0, 0)):
+def summed(kernel, collective, outs, *operands, extra=(), more=0, far=(0, 0), room=58):
     n = lax.axis_size(SHARD)
     length, width = operands[0].shape[0], operands[0].shape[1] + more
     box = pltpu.VMEM((CHUNKS, length // CHUNKS, width), bf16)
@@ -586,7 +540,7 @@
         + [pltpu.SemaphoreType.DMA((CHUNKS,))] * 4
         + [pltpu.VMEM((length // CHUNKS, width), f32), *extra],
         compiler_params=pltpu.CompilerParams(
-            collective_id=collective, has_side_effects=True, vmem_limit_bytes=58 << 20
+            collective_id=collective, has_side_effects=True, vmem_limit_bytes=room << 20
         ),
         cost_estimate=pl.CostEstimate(flops=0, bytes_accessed=20 << 20, transcendentals=0),
         name="line_sum"+str(collective),
@@ -623,6 +577,7 @@
         *other,
         extra=[*boxes, *[pltpu.SemaphoreType.DMA((2 * len(layers),))] * 2],
         far=(2 * len(layers), len(layers)),
+        room=26,
     )
     return first, low, chosen
 
@@ -654,17 +609,16 @@
     return out, low, jnp.sum(gg, axis=0), *sums
 
 
-def back_sum_scatter(collective, p, beside, d_out, values, gain, blocks):
+def back_sum_scatter(collective, p, beside, d_out, values, gain, streams):
     outs = [shaped(p, f32), shaped(p, bf16), jax.ShapeDtypeStruct((8, p.shape[1]), f32)]
-    outs += [shaped(beside, bf16), jax.ShapeDtypeStruct(blocks.shape[1:], bf16)]
-    sems = [pltpu.SemaphoreType.DMA((blocks.shape[0],))] * 2
-    extra = [pltpu.VMEM(blocks.shape, bf16), *sems]
-    operands = (p, beside, d_out, values, gain[None], blocks)
+    outs += [shaped(beside, bf16)]
+    outs += [jax.ShapeDtypeStruct(a.shape[1:], bf16) for a in streams[::2]]
+    operands = (p, beside, d_out, values, gain[None], *streams)
     more = beside.shape[1]
-    out, low, gg, whole, total = summed(
-        scatter_kernel, collective, outs, *operands, extra=extra, more=more
+    out, low, gg, whole, *totals = summed(
+        scatter_kernel, collective, outs, *operands, extra=halving_scratch(streams), more=more, room=36
     )
-    return out, low, jnp.sum(gg, axis=0), whole, total
+    return out, low, jnp.sum(gg, axis=0), whole, totals
 
 
 def dot(left, right, dims=((1,), (0,))):
@@ -1168,7 +1122,7 @@
     lax.fori_loop(1, count, drain, 0)
 
 
-def mixer_call(kernel, collective, outs, scratch, sems, widths, heads, operands):
+def mixer_call(kernel, collective, outs, scratch, sems, widths, heads, operands, room):
     count = lax.axis_size(CTX)
     whole = pl.BlockSpec(memory_space=pltpu.VMEM)
     return pl.pallas_call(
@@ -1179,7 +1133,9 @@
         scratch_shapes=[pltpu.VMEM(*s) for s in scratch]
         + [pltpu.SemaphoreType.DMA((count,))] * sems,
         compiler_params=pltpu.CompilerParams(
-            collective_id=collective, has_side_effects=True, vmem_limit_bytes=56 << 20
+            collective_id=collective,
+            has_side_effects=True,
+            vmem_limit_bytes=(room + 2 * count) << 20,
         ),
         cost_estimate=pl.CostEstimate(flops=0, bytes_accessed=20 << 20, transcendentals=0),
         name="mixer"+str(collective),
@@ -1216,7 +1172,7 @@
         ((inner, states), f32),
     ]
     operands = (proj, weights.head_rows, weights.skip_row, *layout)
-    return mixer_call(mix_forward_kernel, 5, outs, scratch, 6, widths, heads, operands)
+    return mixer_call(mix_forward_kernel, 5, outs, scratch, 6, widths, heads, operands, 18)
 
 
 def mix_backward(weights, saved, d_both, layout):
@@ -1265,7 +1221,7 @@
         saved.decays,
         d_both,
     )
-    return mixer_call(mix_backward_kernel, 6, outs, scratch, 4, widths, heads, operands)
+    return mixer_call(mix_backward_kernel, 6, outs, scratch, 4, widths, heads, operands, 24)
 
 
 def finish_kernel(
@@ -1274,7 +1230,7 @@
     widths,
     *refs,
 ):
-    arrays, refs = refs[: len(places[2])], refs[len(places[2]) :]
+    unsummed, arrays, refs = refs[:8], refs[8:14], refs[14:]
     (
         rows0,
         rows1,
@@ -1300,6 +1256,7 @@
         tiny_out,
         *refs,
     ) = refs
+    arrays, refs = (*refs[:4], *arrays), refs[4:]
     boxes, refs = refs[: len(widths)], refs[len(widths) :]
     (
         rows_box,
@@ -1368,6 +1325,8 @@
     early += [over(2 + l, columns[l], columns_boxes.at[l]) for l in range(2)]
     for copy in early:
         copy.start()
+    for i in range(4):
+        arrays[i][...] = (unsummed[2 * i][...].astype(f32) + unsummed[2 * i + 1][...].astype(f32)).astype(bf16)
     pairs = [(tiny0, tiny1, tiny_box)]
     pairs += [(part(0, i), part(1, i), box) for i, box in enumerate(boxes)]
     pairs += [(rows0, rows1, rows_box), (grad0, grad1, grad_box)]
@@ -1469,36 +1428,36 @@
 
 def finish(first, second, rows, d_rows, tinies, wides, columns):
     count = lax.axis_size(CTX)
-    arrays = (*first.ffn, first.proj, *first.out, *second.ffn, *second.mix)
-    up, down = first.ffn[0].shape[1] // 3 * 2, first.ffn[0].shape[1] // 3
-    out = first.out[0].shape[1]
+    pairs = [*first.ffn, *first.out]
+    arrays = (*first.proj, *second.ffn, *second.mix)
+    up, down = second.ffn[0].shape[1] // 3 * 2, second.ffn[0].shape[1] // 3
+    out = first.out[0][0].shape[1]
     step = 128
-    query = (first.proj.shape[1] - step) - 2 * (second.mix[1].shape[1] - step - out)
     most = second.mix[1].shape[1] - step - out
+    query = first.proj[0].shape[1] - most
 
     def ffn(a):
         return (a, 0, up), (a + 1, 0, up), (a, up, down), (a + 1, up, down)
 
     places = (
         (
-            (2, 0, query),
-            (2, query, most),
-            (2, query + most, most),
+            (4, 0, query),
+            (4, query, most),
+            (5, 0, most),
             *ffn(0),
+            (2, 0, out),
             (3, 0, out),
-            (4, 0, out),
         ),
         (
-            (7, 0, query),
-            (7, query, most),
-            (8, 0, most),
-            *ffn(5),
-            (7, query + most, out),
-            (8, most + step, out),
+            (8, 0, query),
+            (8, query, most),
+            (9, 0, most),
+            *ffn(6),
+            (8, query + most, out),
+            (9, most + step, out),
         ),
-        arrays,
     )
-    length, part = first.proj.shape[0], rows[0].shape[0]
+    length = first.proj[0].shape[0]
     widths = [piece[2] for piece in places[0]]
     half, block = wides[0].shape[1] // 2, columns[0].shape[1] // count
     shape = jax.ShapeDtypeStruct
@@ -1514,7 +1473,8 @@
         shape(tinies[0].shape, f32),
     ]
     tokens = columns[0].shape[0]
-    scratch = [pltpu.VMEM((length, w), bf16) for w in widths]
+    scratch = [pltpu.VMEM(kept.shape, bf16) for kept, _ in pairs]
+    scratch += [pltpu.VMEM((length, w), bf16) for w in widths]
     scratch += [
         pltpu.VMEM(rows[0].shape, bf16),
         pltpu.VMEM(d_rows[0].shape, f32),
@@ -1531,7 +1491,7 @@
     over = len(widths) + 8
     scratch += [pltpu.SemaphoreType.DMA((n,)) for n in (over, over, 3 * count, 3 * count)]
     whole = pl.BlockSpec(memory_space=pltpu.VMEM)
-    operands = (*arrays, *rows, *d_rows, *tinies, *wides, *columns)
+    operands = (*sum(pairs, ()), *arrays, *rows, *d_rows, *tinies, *wides, *columns)
     return pl.pallas_call(
         functools.partial(finish_kernel, count, places, widths),
         out_shape=outs,
@@ -1665,14 +1625,6 @@
     )
 
 
-def blocks_of(total):
-    place, count = lax.axis_index(CTX), lax.axis_size(CTX)
-    block = total.shape[0] // count
-    return jnp.stack(
-        [lax.dynamic_slice_in_dim(total, (place ^ k) * block, block, 0) for k in range(count)]
-    )
-
-
 def streams_of(total):
     place, count = lax.axis_index(CTX), lax.axis_size(CTX)
     block, half = total.shape[0] // count, total.shape[1] // 2
@@ -1701,9 +1653,7 @@
             rows = kept.shape[0] // 2
             sent = (kept[rows:].astype(f32) + got[rows:].astype(f32)).astype(bf16)
             kept = (kept[:rows].astype(f32) + got[:rows].astype(f32)).astype(bf16)
-        else:
-            kept = (kept.astype(f32) + got.astype(f32)).astype(bf16)
-    return kept
+    return kept, got
 
 
 def after(first, *later):
@@ -1767,10 +1717,10 @@
         sums_proj = weight_sums(
             normed, d_proj[:, : widths[0]], d_zx, jnp.concatenate([d_step, d_step], axis=1)
         )
-        blocks = blocks_of(sums_proj)
-        (blocks,), (d_normed,) = after((blocks,), d_normed)
+        streams = streams_of(sums_proj)
+        (streams,), (d_normed,) = after((streams,), d_normed)
         d_hidden, d_hidden_low, grads.gain_in, d_shared, grads.proj = back_sum_scatter(
-            7, d_normed, d_shared, d_middle, values_in, weights.gain_in, blocks
+            7, d_normed, d_shared, d_middle, values_in, weights.gain_in, streams
         )
     else:
         query, inner = widths[0] // 2, (d_proj.shape[1] - widths[3]) // 2
@@ -1888,21 +1838,26 @@
             block_cot = lax.all_gather(rows_cot, SHARD, axis=0, tiled=True)
         partial, saved = layer_forward(weights, normed, layout)
         first, second = layers
-        wanted = [(layer, own[i], other[i]) for i in (2, 3)]
+        wanted = [(1, own[i], other[i]) for i in (0, 1)]
+        if layer == 1:
+            wanted = [(0, own[i], other[i]) for i in (2, 3)]
         saved.middle, saved.ffn_in, chosen = copying_sum(
             middle_kernel, 1 + 8 * layer, f32, partial, hidden, weights.gain_ffn, wanted
         )
-        weights.gate_up, weights.down = chosen
+        if layer == 0:
+            second.proj, second.out = chosen
+        else:
+            first.gate_up, first.down = chosen
         partial, saved.gate_pre, saved.upward, saved.product = ffn_forward(
             weights, saved.ffn_in
         )
         saves.append(saved)
         if layer == 0:
-            wanted = [(1, own[i], other[i]) for i in (0, 1)]
+            wanted = [(1, own[i], other[i]) for i in (2, 3)]
             out_low, normed, chosen = copying_sum(
                 layer_end_kernel, 2, bf16, partial, saved.middle, second.gain_in, wanted
             )
-            second.proj, second.out = chosen
+            second.gate_up, second.down = chosen
             outs.append(own_rows(out_low))
             hidden = out_low.astype(f32)
         else:
@@ -1942,7 +1897,7 @@
     heads = tiny[2 * width :]
     step = jnp.where(
         leading,
-        first.proj[:, first.proj.shape[1] - 128 :],
+        first.proj[1][:, zx.shape[2] // 2 :],
         second.mix[1][:, zx.shape[2] // 2 : zx.shape[2] // 2 + 128],
     )
     io_width = w_state_io.shape[2]

time: 795 us -> 754 us (0.948)
  Pallas kernels: 520 us -> 481 us
  matrix products: 101 us -> 85.9 us
  local copies, waits for them, and re-layouts: 74.8 us -> 86.9 us
  other arithmetic: 50.6 us -> 39 us
  waiting for transfers between devices: 2.79 us -> 13.7 us
    pallas_call x7, Pallas kernels: 349 us -> 320 us  [summed(): pl.pallas_call(functools.partial(kernel, n, CHUNKS, LAG), out_shape=outs,...]
    unnamed x108 -> x174, local copies, waits for them, and re-layouts: 41.7 us -> 60.2 us
    ppermute x8, waiting for transfers between devices: 0.02 us -> 11.1 us  [flip(): lax.ppermute(values, CTX, [(i, i ^ bit) for i in range(lax.axis_size(CTX))])]
    dot_general x8, matrix products: 44 us -> 33 us  [matmul(): return jnp.dot(left, right, preferred_element_type=f32)]
    pallas_call x4, Pallas kernels: 144 us -> 133 us  [mixer_call(): pl.pallas_call(functools.partial(kernel, count, widths, heads), out_shape...]
    convert_element_type x4 -> x0, other arithmetic: 8.91 us -> none  [scatter_relative(): kept = (kept.astype(f32) + got.astype(f32)).astype(bf16)]
  transfers between devices with their start and end apart: 22 -> 22, of which waited for: 1 -> 3; matrix products, arithmetic and copies ran while one was open for 25% -> 22% of each run, Pallas kernels for 63% -> 61%
where the time goes in v2:
time: 754 us; the launch traced here: 742 us
  Pallas kernels  481 us (64%)
  local copies, waits for them, and re-layouts  86.9 us (12%)
  matrix products  85.9 us (11%)
  other arithmetic  39 us (5%)
  starting transfers between devices  18.2 us (2%)
  between operations  17.2 us (2%)
  waiting for transfers between devices  13.7 us (2%)
    pallas_call x7, Pallas kernels, summed(): pl.pallas_call(functools.partial(kernel, n, CHUNKS, LAG), out_shape=outs,...  320 us
    pallas_call x4, Pallas kernels, mixer_call(): pl.pallas_call(functools.partial(kernel, count, widths, heads), out_shape...  133 us
    unnamed x174, local copies, waits for them, and re-layouts  60.2 us
    dot_general x8, matrix products, matmul_nt(): lax.dot_general(left, right, (((1,), (1,)), ((), ())), preferred_element_...  46.3 us
    dot_general x8, matrix products, matmul(): return jnp.dot(left, right, preferred_element_type=f32)  33 us
    pallas_call x1, Pallas kernels, finish(): pl.pallas_call(functools.partial(finish_kernel, count, places, widths), o...  28.3 us
  transfers between devices with their start and end apart: 22, of which 3 were waited for; matrix products, arithmetic and copies ran while one was open for 22% of the time, Pallas kernels for 61%

profile of v2, /device:TPU:0, one launch (start us, length us, event | category | flops | bytes accessed | tf_op | source)
XLA Modules:
  0.0 741.9 jit_solution(9723319846457368120)
XLA Ops:
  9.1 5.0 collective-permute-start
  18.1 6.7 copy.55
  37.9 10.3 %copy.58 = bf16[256,8,2,1024]{3,1,2,0:T(8,128)(2,1)} copy(bf16[256,8,2,1024]{3,2,1,0:T(2,128)(2,1)} %bitcast.207) | data formatting | bytes 16777216
  48.8 4.5 pad_maximum_fusion.refs_1_
  63.3 7.8 %fusion.4.proj_ref = f32[256,2688]{1,0:T(8,128)S(1)} fusion(bf16[256,2048]{1,0:T(8,128)(2,1)} %multiply_convert_fusion, bf16[2048,2688]{1,0:T(8,128)(2,1)} %constant_dynamic-update-slice_fusion.refs_0_, bf16[2048,2688]{1,0:T(8,128)(2,1)} %collective-permute-done.4.refs_2_, pred[]{:T(512)S(6)} %eq.54), kind=kOutput, calls=%fused_computation.5 | convolution fusion | flops 2824077312 | bytes 25821184 | tf_op jit(solution)/shard_map/dot_general | solution.py:1514
  71.1 26.1 %mixer5.2 = (bf16[256,1024]{1,0:T(8,128)(2,1)S(1)}, f32[256,768]{1,0:T(8,128)S(1)}, bf16[768,256]{1,0:T(8,128)(2,1)S(1)}, bf16[1024,256]{1,0:T(8,128)(2,1)S(1)}, f32[4,16,256]{2,1,0:T(8,128)S(1)}) custom-call(f32[256,2688]{1,0:T(8,128)S(1)} %fusion.4.proj_ref, f32[8,128]{1,0:T(8,128)S(1)} %pad.23.vec_ref, f32[1,768]{1,0:T(1,128)S(1)} %broadcast_in_dim_reshape.13.skip_ref, ...), custom_call_target="tpu_custom_call" | custom-call | bytes 20971520 | tf_op jit(solution)/shard_map/mixer5/pallas_call | solution.py:1128
  99.0 34.0 %line_sum1.1 = (f32[256,2048]{1,0:T(8,128)S(1)}, bf16[256,2048]{1,0:T(8,128)(2,1)S(1)}, bf16[2048,2688]{1,0:T(8,128)(2,1)}, bf16[1024,2048]{1,0:T(8,128)(2,1)S(1)}) custom-call(f32[256,2048]{1,0:T(8,128)S(1)} %fusion.15.p_ref, f32[256,2048]{1,0:T(8,128)S(1)} %convert_element_type.251.h_ref.v_ref, f32[1,2048]{1,0:T(1,128)S(1)} %bitcast.193, ...), custom_call_target="tpu_custom_call" | custom-call | bytes 20971520 | tf_op jit(solution)/shard_map/line_sum1/pallas_call | solution.py:534
  137.8 4.1 fusion.5.p_ref
  141.9 31.9 %line_sum2.1 = (bf16[256,2048]{1,0:T(8,128)(2,1)S(1)}, bf16[256,2048]{1,0:T(8,128)(2,1)S(1)}, bf16[2048,2048]{1,0:T(8,128)(2,1)S(1)}, bf16[1024,2048]{1,0:T(8,128)(2,1)S(1)}) custom-call(f32[256,2048]{1,0:T(8,128)S(1)} %fusion.5.p_ref, f32[256,2048]{1,0:T(8,128)S(1)} %get-tuple-element.102.h_ref.refs_2_, f32[1,2048]{1,0:T(1,128)S(1)} %bitcast.196, ...), custom_call_target="tpu_custom_call" | custom-call | bytes 20971520 | tf_op jit(solution)/shard_map/line_sum2/pallas_call | solution.py:534
  186.6 6.7 fusion.50.proj_ref
  193.3 28.6 %mixer5.3 = (bf16[256,1024]{1,0:T(8,128)(2,1)S(1)}, f32[256,768]{1,0:T(8,128)S(1)}, bf16[768,256]{1,0:T(8,128)(2,1)S(1)}, bf16[1024,256]{1,0:T(8,128)(2,1)S(1)}, f32[4,16,256]{2,1,0:T(8,128)S(1)}) custom-call(f32[256,2688]{1,0:T(8,128)S(1)} %fusion.50.proj_ref, f32[8,128]{1,0:T(8,128)S(1)} %pad.25.vec_ref, f32[1,768]{1,0:T(1,128)S(1)} %broadcast_in_dim_reshape.14.skip_ref, ...), custom_call_target="tpu_custom_call" | custom-call | bytes 20971520 | tf_op jit(solution)/shard_map/mixer5/pallas_call | solution.py:1128
  225.5 32.8 %line_sum9.1 = (f32[256,2048]{1,0:T(8,128)S(1)}, bf16[256,2048]{1,0:T(8,128)(2,1)S(1)}, bf16[2048,2048]{1,0:T(8,128)(2,1)S(1)}, bf16[1024,2048]{1,0:T(8,128)(2,1)S(1)}) custom-call(f32[256,2048]{1,0:T(8,128)S(1)} %fusion.51.p_ref, f32[256,2048]{1,0:T(8,128)S(1)} %copy-done.2, f32[1,2048]{1,0:T(1,128)S(1)} %bitcast.198, bf16[2048,2048]{1,0:T(8,128)(2,1)} %bitcast.202, ...), custom_call_target="tpu_custom_call" | custom-call | bytes 20971520 | tf_op jit(solution)/shard_map/line_sum9/pallas_call | solution.py:534
  265.5 7.0 fusion.52
  272.5 4.8 multiply_convert_fusion.5
  278.5 7.2 fusion.47.refs_0_
  287.9 41.1 %line_sum3.1 = (f32[256,2048]{1,0:T(8,128)}, bf16[256,2048]{1,0:T(8,128)(2,1)}, f32[8,2048]{1,0:T(8,128)}, bf16[2,512,768]{2,1,0:T(8,128)(2,1)}, bf16[2,512,768]...) custom-call(f32[256,2048]{1,0:T(8,128)} %fusion.47.refs_0_, ...), custom_call_target="tpu_custom_call" | custom-call | bytes 20971520 | tf_op jit(solution)/shard_map/line_sum3/pallas_call | solution.py:534
  329.1 3.9 fusion.53.d_both_ref
  333.1 31.8 %mixer6.2 = (bf16[256,2688]{1,0:T(8,128)(2,1)S(1)}, f32[8,128]{1,0:T(8,128)S(1)}) custom-call(f32[256,2688]{1,0:T(8,128)S(1)} %copy-done.6, f32[8,128]{1,0:T(8,128)S(1)} %pad.25.vec_ref, f32[1,768]{1,0:T(1,128)S(1)} %broadcast_in_dim_reshape.14.skip_ref, f32[256,8]{1,0:T(8,128)S(1)} %pad.24.tok_ref, f32[2,1024]{1,0:T(2,128)S(1)} %pad_maximum_fusion.14.key_ref, ...), custom_call_target="tpu_custom_call" | custom-call | bytes 20971520 | tf_op jit(solution)/shard_map/mixer6/pallas_call | solution.py:1128
  364.9 9.1 %fusion.54.refs_0_ = f32[256,2048]{1,0:T(8,128)} fusion(bf16[256,2688]{1,0:T(8,128)(2,1)S(1)} %get-tuple-element.120.refs_7_, bf16[2048,2688]{1,0:T(8,128)(2,1)} %get-tuple-element.105), kind=kOutput, calls=%fused_computation.189 | convolution fusion | flops 2818572288 | bytes 14483456 | tf_op jit(solution)/shard_map/dot_general | solution.py:1518
  374.9 64.6 %line_sum4.1 = (f32[256,2048]{1,0:T(8,128)}, bf16[256,2048]{1,0:T(8,128)(2,1)}, f32[8,2048]{1,0:T(8,128)}, bf16[256,1024]{1,0:T(8,128)(2,1)}, bf16[2,512,768]{2,...) custom-call(f32[256,2048]{1,0:T(8,128)} %fusion.54.refs_0_, ...), custom_call_target="tpu_custom_call" | custom-call | bytes 20971520 | tf_op jit(solution)/shard_map/line_sum4/pallas_call | solution.py:534
  439.6 4.1 multiply_convert_fusion.2
  444.7 7.1 fusion.46.refs_0_
  451.8 63.6 %line_sum10.1 = (f32[256,2048]{1,0:T(8,128)}, bf16[256,2048]{1,0:T(8,128)(2,1)}, f32[8,2048]{1,0:T(8,128)}, bf16[2,512,768]{2,1,0:T(8,128)(2,1)}, bf16[2,512,768...) custom-call(f32[256,2048]{1,0:T(8,128)} %fusion.46.refs_0_, ...), custom_call_target="tpu_custom_call" | custom-call | bytes 20971520 | tf_op jit(solution)/shard_map/line_sum10/pallas_call | solution.py:534
  520.7 4.0 fusion.14.d_both_ref
  532.0 46.6 %mixer6.3 = (bf16[256,2688]{1,0:T(8,128)(2,1)S(1)}, f32[8,128]{1,0:T(8,128)S(1)}) custom-call(f32[256,2688]{1,0:T(8,128)S(1)} %copy-done.4, f32[8,128]{1,0:T(8,128)S(1)} %pad.23.vec_ref, f32[1,768]{1,0:T(1,128)S(1)} %broadcast_in_dim_reshape.13.skip_ref, f32[256,8]{1,0:T(8,128)S(1)} %pad.24.tok_ref, f32[2,1024]{1,0:T(2,128)S(1)} %pad_maximum_fusion.14.key_ref, ...), custom_call_target="tpu_custom_call" | custom-call | bytes 20971520 | tf_op jit(solution)/shard_map/mixer6/pallas_call | solution.py:1128
  581.6 6.1 fusion.3.p_ref
  587.8 4.1 convolution_convert_fusion
  593.9 51.6 %line_sum7.1 = (f32[256,2048]{1,0:T(8,128)S(1)}, bf16[256,2048]{1,0:T(8,128)(2,1)}, f32[8,2048]{1,0:T(8,128)S(1)}, bf16[256,1024]{1,0:T(8,128)(2,1)S(1)}, bf16[5...) custom-call(f32[256,2048]{1,0:T(8,128)S(1)} %fusion.3.p_ref, bf16[256,1024]{1,0:T(8,128)(2,1)S(1)} %get-tuple-element.271.q_ref, ...), custom_call_target="tpu_custom_call" | custom-call | bytes 20971520 | tf_op jit(solution)/shard_map/line_sum7/pallas_call | solution.py:534
  668.0 7.6 %collective-permute-done.11.refs_3_ = bf16[512,768]{1,0:T(8,128)(2,1)S(1)} collective-permute-done((bf16[512,768]{1,0:T(8,128)(2,1)}, bf16[512,768]{1,0:T(8,128)(2,1)S(1)}, u32[]{:S(2)}, u32[]{:S(2)}) %collective-permute-start.11) | collective-permute-done | bytes 786464 | tf_op jit(solution)/shard_map/ppermute | solution.py:1579
  679.9 28.3 %finish.1 = (bf16[512,256]{1,0:T(8,128)(2,1)}, f32[2,512,768]{2,1,0:T(8,128)}, f32[2,512,1024]{2,1,0:T(8,128)}, bf16[1024,512]{1,0:T(8,128)(2,1)}, bf16[1024,512...) custom-call(bf16[512,768]{1,0:T(8,128)(2,1)} %get-tuple-element.257., ...), custom_call_target="tpu_custom_call" | custom-call | bytes 20971520 | tf_op jit(solution)/shard_map/finish/pallas_call | solution.py:1495
  712.5 7.6 %copy.53 = f32[1,512,2,1024]{3,2,1,0:T(2,128)} copy(f32[1,512,2,1024]{3,1,2,0:T(8,128)} %bitcast.210) | data formatting | bytes 8388608
  720.1 4.1 copy.51
  (328 shorter events, 121.9 us)
Async XLA Ops:
  7.2 265.3 %all-gather.2.cloned.1.call-start = ((), (), s32[]{:S(2)}) async-start(), calls=%async_computation.1 | async-start | bytes 1310720 | tf_op jit(solution)/shard_map/all_gather | solution.py:1838
  9.1 24.1 %collective-permute-start = (bf16[64,2048]{1,0:T(8,128)(2,1)}, bf16[64,2048]{1,0:T(8,128)(2,1)}, u32[]{:S(2)}, u32[]{:S(2)}) collective-permute-start(bf16[64,2048]{1,0:T(8,128)(2,1)} %get-tuple-element.245), channel_id=1, source_target_pairs={{0,3},{1,2},{2,1},{3,0},{4,7},{5,6},{6,5},{7,4},{8,11},{9,10},{10,... | collective-permute-start | bytes 786440 | tf_op jit(solution)/shard_map/ppermute | solution.py:556
  14.1 22.6 %collective-permute-start.1 = (bf16[64,2048]{1,0:T(8,128)(2,1)}, bf16[64,2048]{1,0:T(8,128)(2,1)}, u32[]{:S(2)}, u32[]{:S(2)}) collective-permute-start(bf16[64,2048]{1,0:T(8,128)(2,1)} %get-tuple-element.245), channel_id=1, source_target_pairs={{0,2},{1,3},{2,0},{3,1},{4,6},{5,7},{6,4},{7,5},{8,10},{9,11},{10,... | collective-permute-start | bytes 786440 | tf_op jit(solution)/shard_map/ppermute | solution.py:556
  14.1 23.6 %collective-permute-start.2 = (bf16[64,2048]{1,0:T(8,128)(2,1)}, bf16[64,2048]{1,0:T(8,128)(2,1)S(1)}, u32[]{:S(2)}, u32[]{:S(2)}) collective-permute-start(bf16[64,2048]{1,0:T(8,128)(2,1)} %get-tuple-element.245), channel_id=1, source_target_pairs={{0,1},{1,0},{2,3},{3,2},{4,5},{5,4},{6,7},{7,6},{8,9},{9,8},{10,11... | collective-permute-start | bytes 786440 | tf_op jit(solution)/shard_map/ppermute | solution.py:556
  37.8 25.5 %collective-permute-start.4 = (bf16[2048,2688]{1,0:T(8,128)(2,1)}, bf16[2048,2688]{1,0:T(8,128)(2,1)}, u32[]{:S(2)}, u32[]{:S(2)}) collective-permute-start(bf16[2048,2688]{1,0:T(8,128)(2,1)} %constant_dynamic-update-slice_fusion.refs_0_), channel_id=1, source_target_pairs={{0,16},{16,0},{1,17},{17,1},{2,18},{18,2},{3,19},{19,3},{4,20},{20... | collective-permute-start | bytes 33030152 | tf_op jit(solution)/shard_map/ppermute | solution.py:1526
  48.2 86.8 %collective-permute-start.6 = (bf16[2048,2048]{1,0:T(8,128)(2,1)}, bf16[2048,2048]{1,0:T(8,128)(2,1)}, u32[]{:S(2)}, u32[]{:S(2)}) collective-permute-start(bf16[2048,2048]{1,0:T(8,128)(2,1)} %bitcast.200), channel_id=1, source_target_pairs={{0,16},{16,0},{1,17},{17,1},{2,18},{18,2},{3,19},{19,3},{4,20},{20... | collective-permute-start | bytes 25165832 | tf_op jit(solution)/shard_map/ppermute | solution.py:1526
  48.8 9.8 %collective-permute-start.3 = (f32[4132]{0:T(1024)S(1)}, f32[4132]{0:T(1024)S(1)}, u32[]{:S(2)}, u32[]{:S(2)}) collective-permute-start(f32[4132]{0:T(1024)S(1)} %concatenate.57), channel_id=1, source_target_pairs={{0,16},{16,0},{1,17},{17,1},{2,18},{18,2},{3,19},{19,3},{4,20},{20... | collective-permute-start | bytes 49592 | tf_op jit(solution)/shard_map/ppermute | solution.py:1526
  53.4 43.9 %collective-permute-start.5 = (bf16[1024,2048]{1,0:T(8,128)(2,1)}, bf16[1024,2048]{1,0:T(8,128)(2,1)}, u32[]{:S(2)}, u32[]{:S(2)}) collective-permute-start(bf16[1024,2048]{1,0:T(8,128)(2,1)} %pad_maximum_fusion.refs_1_), channel_id=1, source_target_pairs={{0,16},{16,0},{1,17},{17,1},{2,18},{18,2},{3,19},{19,3},{4,20},{20... | collective-permute-start | bytes 12582920 | tf_op jit(solution)/shard_map/ppermute | solution.py:1526
  53.9 83.9 %collective-permute-start.7 = (bf16[1024,2048]{1,0:T(8,128)(2,1)}, bf16[1024,2048]{1,0:T(8,128)(2,1)}, u32[]{:S(2)}, u32[]{:S(2)}) collective-permute-start(bf16[1024,2048]{1,0:T(8,128)(2,1)} %bitcast.19.refs_1_), channel_id=1, source_target_pairs={{0,16},{16,0},{1,17},{17,1},{2,18},{18,2},{3,19},{19,3},{4,20},{20... | collective-permute-start | bytes 12582920 | tf_op jit(solution)/shard_map/ppermute | solution.py:1526
  59.3 39.7 %copy-start.32 = (f32[2048]{0:T(1024)}, f32[2048]{0:T(1024)S(1)}, u32[]{:S(2)}) copy-start(f32[2048]{0:T(1024)S(1)} %get-tuple-element.319) | copy-start | bytes 24580
  59.3 82.5 %copy-start.33 = (f32[2048]{0:T(1024)}, f32[2048]{0:T(1024)S(1)}, u32[]{:S(2)}) copy-start(f32[2048]{0:T(1024)S(1)} %get-tuple-element.300) | copy-start | bytes 24580
  59.3 165.4 %copy-start.34 = (f32[2048]{0:T(1024)}, f32[2048]{0:T(1024)S(1)}, u32[]{:S(2)}) copy-start(f32[2048]{0:T(1024)S(1)} %get-tuple-element.299) | copy-start | bytes 24580
  61.1 526.6 %collective-permute-start.18 = (bf16[256,2048]{1,0:T(8,128)(2,1)}, bf16[256,2048]{1,0:T(8,128)(2,1)}, u32[]{:S(2)}, u32[]{:S(2)}) collective-permute-start(bf16[256,2048]{1,0:T(8,128)(2,1)} %multiply_convert_fusion), channel_id=1, source_target_pairs={{0,16},{16,0},{1,17},{17,1},{2,18},{18,2},{3,19},{19,3},{4,20},{20... | collective-permute-start | bytes 3145736 | tf_op jit(solution)/shard_map/ppermute | solution.py:1526
  97.3 37.7 %slice-start = ((s8[8388608]{0:T(1024)(128)(4,1)}), s8[4194304]{0:T(1024)(128)(4,1)S(1)}, s32[]{:S(2)}) async-start(s8[8388608]{0:T(1024)(128)(4,1)} %bitcast.203), calls=%async_computation.3 | async-start | bytes 8388608
  181.7 484.4 %reduce-scatter.2.cloned.1.call-start = ((), (), s32[]{:S(2)}) async-start(), calls=%async_computation.2 | async-start | bytes 1310720 | tf_op jit(solution)/shard_map/reduce_scatter | solution.py:1875
  183.6 343.1 %collective-permute-start.13 = (bf16[256,512]{1,0:T(8,128)(2,1)}, bf16[256,512]{1,0:T(8,128)(2,1)}, u32[]{:S(2)}, u32[]{:S(2)}) collective-permute-start(bf16[256,512]{1,0:T(8,128)(2,1)} %get-tuple-element.288), channel_id=1, source_target_pairs={{0,16},{16,0},{1,17},{17,1},{2,18},{18,2},{3,19},{19,3},{4,20},{20... | collective-permute-start | bytes 786440 | tf_op jit(solution)/shard_map/ppermute | solution.py:1526
  186.6 36.8 %copy-start.39 = (bf16[1024,2048]{1,0:T(8,128)(2,1)S(1)}, bf16[1024,2048]{1,0:T(8,128)(2,1)}, u32[]{:S(2)}) copy-start(bf16[1024,2048]{1,0:T(8,128)(2,1)} %copy-done.38) | copy-start | bytes 12582916
  374.9 64.7 %copy-start.47 = (f32[256,2048]{1,0:T(8,128)S(1)}, f32[256,2048]{1,0:T(8,128)}, u32[]{:S(2)}) copy-start(f32[256,2048]{1,0:T(8,128)} %copy-done.46) | copy-start | bytes 6291460
  451.8 65.2 %copy-start.69 = (f32[8,2048]{1,0:T(8,128)S(1)}, f32[8,2048]{1,0:T(8,128)}, u32[]{:S(2)}) copy-start(f32[8,2048]{1,0:T(8,128)} %get-tuple-element.166) | copy-start | bytes 196612
  451.8 65.3 %copy-start.68 = (f32[8,2048]{1,0:T(8,128)S(1)}, f32[8,2048]{1,0:T(8,128)}, u32[]{:S(2)}) copy-start(f32[8,2048]{1,0:T(8,128)} %get-tuple-element.167) | copy-start | bytes 196612
  451.8 68.9 %copy-start.56 = (bf16[1,256,2048]{2,1,0:T(8,128)(2,1)S(1)}, bf16[1,256,2048]{2,1,0:T(8,128)(2,1)}, u32[]{:S(2)}) copy-start(bf16[1,256,2048]{2,1,0:T(8,128)(2,1)} %param.23) | copy-start | bytes 3145732
  515.4 11.2 %collective-permute-start.12 = (bf16[256,2048]{1,0:T(8,128)(2,1)}, bf16[256,2048]{1,0:T(8,128)(2,1)}, u32[]{:S(2)}, u32[]{:S(2)}) collective-permute-start(bf16[256,2048]{1,0:T(8,128)(2,1)} %get-tuple-element.137), channel_id=1, source_target_pairs={{0,16},{16,0},{1,17},{17,1},{2,18},{18,2},{3,19},{19,3},{4,20},{20... | collective-permute-start | bytes 3145736 | tf_op jit(solution)/shard_map/ppermute | solution.py:1526
  518.0 136.6 %collective-permute-start.10 = (bf16[1024,768]{1,0:T(8,128)(2,1)}, bf16[1024,768]{1,0:T(8,128)(2,1)}, u32[]{:S(2)}, u32[]{:S(2)}) collective-permute-start(bf16[1024,768]{1,0:T(8,128)(2,1)} %bitcast.234), channel_id=1, source_target_pairs={{0,4},{4,0},{8,12},{12,8},{1,5},{5,1},{9,13},{13,9},{2,6},{6,2},{1... | collective-permute-start | bytes 4718600 | tf_op jit(solution)/shard_map/ppermute | solution.py:1579
  519.2 140.2 %collective-permute-start.8 = (bf16[1024,768]{1,0:T(8,128)(2,1)}, bf16[1024,768]{1,0:T(8,128)(2,1)}, u32[]{:S(2)}, u32[]{:S(2)}) collective-permute-start(bf16[1024,768]{1,0:T(8,128)(2,1)} %bitcast.233), channel_id=1, source_target_pairs={{0,8},{4,12},{8,0},{12,4},{1,9},{5,13},{9,1},{13,5},{2,10},{6,14},... | collective-permute-start | bytes 4718600 | tf_op jit(solution)/shard_map/ppermute | solution.py:1579
  579.9 7.9 %collective-permute-start.19 = (bf16[256,1024]{1,0:T(8,128)(2,1)S(1)}, bf16[256,1024]{1,0:T(8,128)(2,1)}, u32[]{:S(2)}, u32[]{:S(2)}) collective-permute-start(bf16[256,1024]{1,0:T(8,128)(2,1)S(1)} %pad_maximum_fusion.11), channel_id=1, source_target_pairs={{0,16},{16,0},{1,17},{17,1},{2,18},{18,2},{3,19},{19,3},{4,20},{20... | collective-permute-start | bytes 1572872 | tf_op jit(solution)/shard_map/ppermute | solution.py:1526
  580.0 69.3 %collective-permute-start.16 = (bf16[1024,256]{1,0:T(8,128)(2,1)}, bf16[1024,256]{1,0:T(8,128)(2,1)}, u32[]{:S(2)}, u32[]{:S(2)}) collective-permute-start(bf16[1024,256]{1,0:T(8,128)(2,1)} %bitcast.41), channel_id=1, source_target_pairs={{0,4},{4,0},{8,12},{12,8},{1,5},{5,1},{9,13},{13,9},{2,6},{6,2},{1... | collective-permute-start | bytes 1572872 | tf_op jit(solution)/shard_map/ppermute | solution.py:1579
  587.7 64.2 %collective-permute-start.14 = (bf16[1024,256]{1,0:T(8,128)(2,1)}, bf16[1024,256]{1,0:T(8,128)(2,1)}, u32[]{:S(2)}, u32[]{:S(2)}) collective-permute-start(bf16[1024,256]{1,0:T(8,128)(2,1)} %bitcast.38), channel_id=1, source_target_pairs={{0,8},{4,12},{8,0},{12,4},{1,9},{5,13},{9,1},{13,5},{2,10},{6,14},... | collective-permute-start | bytes 1572872 | tf_op jit(solution)/shard_map/ppermute | solution.py:1579
  593.9 54.5 %copy-start.60 = (bf16[512,128]{1,0:T(8,128)(2,1)S(1)}, bf16[512,128]{1,0:T(8,128)(2,1)}, u32[]{:S(2)}) copy-start(bf16[512,128]{1,0:T(8,128)(2,1)} %slice.240) | copy-start | bytes 393220
  651.3 16.7 %collective-permute-start.17 = (bf16[512,256]{1,0:T(8,128)(2,1)S(1)}, bf16[512,256]{1,0:T(8,128)(2,1)S(1)}, u32[]{:S(2)}, u32[]{:S(2)}) collective-permute-start(bf16[512,256]{1,0:T(8,128)(2,1)S(1)} %get-tuple-element.281), channel_id=1, source_target_pairs={{0,8},{4,12},{8,0},{12,4},{1,9},{5,13},{9,1},{13,5},{2,10},{6,14},... | collective-permute-start | bytes 786440 | tf_op jit(solution)/shard_map/ppermute | solution.py:1579
  653.8 14.1 %collective-permute-start.15 = (bf16[512,256]{1,0:T(8,128)(2,1)}, bf16[512,256]{1,0:T(8,128)(2,1)S(1)}, u32[]{:S(2)}, u32[]{:S(2)}) collective-permute-start(bf16[512,256]{1,0:T(8,128)(2,1)} %get-tuple-element.283), channel_id=1, source_target_pairs={{0,4},{4,0},{8,12},{12,8},{1,5},{5,1},{9,13},{13,9},{2,6},{6,2},{1... | collective-permute-start | bytes 786440 | tf_op jit(solution)/shard_map/ppermute | solution.py:1579
  658.0 17.6 %collective-permute-start.11 = (bf16[512,768]{1,0:T(8,128)(2,1)}, bf16[512,768]{1,0:T(8,128)(2,1)S(1)}, u32[]{:S(2)}, u32[]{:S(2)}) collective-permute-start(bf16[512,768]{1,0:T(8,128)(2,1)} %get-tuple-element.254), channel_id=1, source_target_pairs={{0,8},{4,12},{8,0},{12,4},{1,9},{5,13},{9,1},{13,5},{2,10},{6,14},... | collective-permute-start | bytes 2359304 | tf_op jit(solution)/shard_map/ppermute | solution.py:1579
  662.3 16.7 %collective-permute-start.9 = (bf16[512,768]{1,0:T(8,128)(2,1)}, bf16[512,768]{1,0:T(8,128)(2,1)S(1)}, u32[]{:S(2)}, u32[]{:S(2)}) collective-permute-start(bf16[512,768]{1,0:T(8,128)(2,1)} %get-tuple-element.256), channel_id=1, source_target_pairs={{0,4},{4,0},{8,12},{12,8},{1,5},{5,1},{9,13},{13,9},{2,6},{6,2},{1... | collective-permute-start | bytes 2359304 | tf_op jit(solution)/shard_map/ppermute | solution.py:1579
  (69 other events, 482.1 us)
Sparse Core Ops, SparseCore 0:
  181.8 32.2 all-gather.1
  518.1 24.8 reduce-scatter.1

commit v3 on v2

--- a/solution.py
+++ b/solution.py
@@ -290,6 +290,9 @@
                 own[:, at : at + width] = self.ys[y][:, pl.ds(start, width)]
                 at += width
 
+    def each(self, steps):
+        return -(-lax.axis_size(CTX) * len(self.plan) // (steps - self.first))
+
     def step(self, i, steps):
         place, count = lax.axis_index(CTX), lax.axis_size(CTX)
 
@@ -298,22 +301,23 @@
             for copy in self.copies():
                 copy.wait_recv()
 
-        each = -(-count * len(self.plan) // (steps - self.first))
+        each = self.each(steps)
         begin = (i - self.first) * each
 
         def piece(t, _):
-            at = [0, 0]
+            at = [0] * 4
             for f, (x, stream, _) in enumerate(self.plan):
                 k = t - f * count
                 width = self.own_y[f].shape[1]
                 where = slice(at[stream], at[stream] + width)
                 at[stream] += width
                 kept, sent = self.outs[2 * stream : 2 * stream + 2]
+                turned = stream % 2
 
                 @pl.when((k >= 0) & (k < count))
                 def _():
                     block = kept.shape[1]
-                    source = flipped(place, mirrored(k, count) if stream else k, count)
+                    source = flipped(place, mirrored(k, count) if turned else k, count)
                     cols = pl.ds(pl.multiple_of(source * block, block), block)
                     dims = (((0,), (0,)), ((), ()))
                     total = lax.dot_general(
@@ -348,8 +352,8 @@
 class Halving:
     cuts = 2
 
-    def __init__(self, streams, outs, scratch, turns):
-        self.turns = turns
+    def __init__(self, streams, outs, scratch, turns, begin=None, greets=True):
+        self.turns, self.begin, self.greets = turns, begin, greets
         self.place, self.count = lax.axis_index(CTX), lax.axis_size(CTX)
         self.streams, self.outs = streams, outs
         self.orders = ctx_orders()
@@ -360,6 +364,8 @@
         self.send, self.recv = rest[2 * (self.levels - 1) :]
 
     def greet(self, bar):
+        if not self.greets:
+            return 0
         for bit in self.orders[0]:
             peer = flipped(self.place, bit, self.count)
             pl.semaphore_signal(bar, inc=1, device_id={CTX: peer}, device_id_type=MESH)
@@ -403,11 +409,21 @@
                 self.copy(level + 1, stream, cut).start()
 
     def start(self):
+        if self.begin is None:
+            self.first_copies()
+
+    def first_copies(self):
         for cut in range(self.cuts):
             for stream in range(2):
                 self.copy(0, stream, cut).start()
 
     def step(self, i, steps):
+        if self.begin is not None:
+
+            @pl.when(i == self.begin)
+            def _():
+                self.first_copies()
+
         for cut, turn in enumerate(self.turns):
 
             @pl.when(i == turn)
@@ -460,7 +476,7 @@
     back_rows(n, chunks, lag, p_ref, d_ref, v_ref, gain_ref, *outs[:3], scratch[:9], job, q_ref, outs[3])
 
 
-def back_kernel(n, chunks, lag, plan, x_count, y_count, beside, ready, p_ref, *refs):
+def back_kernel(n, chunks, lag, plan, x_count, y_count, beside, ready, soon, p_ref, *refs):
     q_ref = q_out = None
     if beside:
         q_ref, refs = refs[0], refs[1:]
@@ -474,13 +490,24 @@
         q_out, refs = refs[0], refs[1:]
     sums, refs = refs[:4], refs[4:]
     totals, refs = refs[: ready // 2], refs[ready // 2 :]
+    soon_totals, refs = refs[: 2 * soon], refs[2 * soon :]
+    scratch, rest = refs[:9], refs[9:]
     cut = len(xs) + 2 * len(plan) + 2
-    fill = Fill(plan, xs, ys, sums, refs[9 : 9 + cut])
+    own, rest = rest[:cut], rest[cut:]
+    here, rest = rest[: 4 * soon], rest[4 * soon :]
+    fill = Fill(plan, xs, ys, (*sums, *here), own)
+    jobs = [fill]
+    boxes = 4 * len(ctx_bits())
     if ready:
-        turns = (11, 20) if beside else (14,)
-        fill = Together(fill, Halving(streams, totals, refs[9 + cut :], turns))
+        turns = (8, 14) if beside else (9,)
+        jobs.append(Halving(streams, totals, rest[:boxes], turns))
+        rest = rest[boxes:]
+    if soon:
+        begin = Fill.first + -(-2 * lax.axis_size(CTX) // fill.each(chunks + lag * (n - 1)))
+        jobs.append(Halving(here, soon_totals, rest, (), begin, not ready))
+    fill = Together(*jobs)
     outs = out_ref, low_ref, gg_ref
-    back_rows(n, chunks, lag, p_ref, d_ref, v_ref, gain_ref, *outs, refs[:9], fill, q_ref, q_out)
+    back_rows(n, chunks, lag, p_ref, d_ref, v_ref, gain_ref, *outs, scratch, fill, q_ref, q_out)
 
 
 def back_rows(
@@ -525,7 +552,7 @@
     line_sum(n, chunks, lag, p_rows, done, *scratch, fill=fill)
 
 
-def summed(kernel, collective, outs, *operands, extra=(), more=0, far=(0, 0), room=58):
+def summed(kernel, collective, outs, *operands, extra=(), more=0, far=(0, 0), room=50):
     n = lax.axis_size(SHARD)
     length, width = operands[0].shape[0], operands[0].shape[1] + more
     box = pltpu.VMEM((CHUNKS, length // CHUNKS, width), bf16)
@@ -582,30 +609,40 @@
     return first, low, chosen
 
 
-def back_sum(collective, p, d_out, values, gain, plan, xs, ys, beside=(), ready=()):
+def back_sum(collective, p, d_out, values, gain, plan, xs, ys, beside=(), ready=(), soon=False):
     count = lax.axis_size(CTX)
     length = p.shape[0]
     outs = [shaped(p, f32), shaped(p, bf16), jax.ShapeDtypeStruct((8, p.shape[1]), f32)]
     outs += [shaped(q, bf16) for q in beside]
     widths = [sum(part[3] for part in parts) for _, _, parts in plan]
-    for stream in range(2):
+    sums = []
+    for stream in range(4 if soon else 2):
         total = sum(w for (_, at, _), w in zip(plan, widths) if at == stream)
         shape = (count // 2, xs[0].shape[1] // count, total)
-        outs += [jax.ShapeDtypeStruct(shape, bf16)] * 2
+        sums += [jax.ShapeDtypeStruct(shape, bf16)] * 2
+    outs += sums[:4]
     extra = [pltpu.VMEM(x.shape, bf16) for x in xs]
     extra += [pltpu.VMEM((length, w), bf16) for w in widths] * 2
     copies = len(xs) + sum(len(parts) for _, _, parts in plan)
     extra += [pltpu.SemaphoreType.DMA((copies,))] * 2
+    outs += [jax.ShapeDtypeStruct(a.shape[1:], bf16) for a in ready[::2]]
+    if soon:
+        outs += [jax.ShapeDtypeStruct(sums[4].shape[1:], bf16)] * 2
+        extra += [pltpu.VMEM(a.shape, bf16) for a in sums[4:]]
     if ready:
-        outs += [jax.ShapeDtypeStruct(a.shape[1:], bf16) for a in ready[::2]]
         extra += halving_scratch(ready)
+    if soon:
+        extra += halving_scratch(sums[4:])
 
     def bound(n, chunks, lag, *refs):
-        back_kernel(n, chunks, lag, plan, len(xs), len(ys), bool(beside), len(ready), *refs)
+        back_kernel(n, chunks, lag, plan, len(xs), len(ys), bool(beside), len(ready), soon, *refs)
 
     operands = (p, *beside, d_out, values, gain[None], *xs, *ys, *ready)
     more = sum(q.shape[1] for q in beside)
-    out, low, gg, *sums = summed(bound, collective, outs, *operands, extra=extra, more=more)
+    room = 50 if ready else 38
+    out, low, gg, *sums = summed(
+        bound, collective, outs, *operands, extra=extra, more=more, room=room
+    )
     return out, low, jnp.sum(gg, axis=0), *sums
 
 
@@ -1230,7 +1267,7 @@
     widths,
     *refs,
 ):
-    unsummed, arrays, refs = refs[:8], refs[8:14], refs[14:]
+    unsummed, arrays, refs = refs[:8], refs[8:18], refs[18:]
     (
         rows0,
         rows1,
@@ -1429,32 +1466,35 @@
 def finish(first, second, rows, d_rows, tinies, wides, columns):
     count = lax.axis_size(CTX)
     pairs = [*first.ffn, *first.out]
-    arrays = (*first.proj, *second.ffn, *second.mix)
-    up, down = second.ffn[0].shape[1] // 3 * 2, second.ffn[0].shape[1] // 3
+    arrays = (*first.proj, *second.ffn, *second.down, *second.mix, *second.out)
+    up, down = second.ffn[0].shape[1], second.down[0].shape[1]
     out = first.out[0][0].shape[1]
     step = 128
-    most = second.mix[1].shape[1] - step - out
+    most = second.mix[1].shape[1] - step
     query = first.proj[0].shape[1] - most
-
-    def ffn(a):
-        return (a, 0, up), (a + 1, 0, up), (a, up, down), (a + 1, up, down)
 
     places = (
         (
             (4, 0, query),
             (4, query, most),
             (5, 0, most),
-            *ffn(0),
+            (0, 0, up),
+            (1, 0, up),
+            (0, up, down),
+            (1, up, down),
             (2, 0, out),
             (3, 0, out),
         ),
         (
-            (8, 0, query),
-            (8, query, most),
-            (9, 0, most),
-            *ffn(6),
-            (8, query + most, out),
-            (9, most + step, out),
+            (10, 0, query),
+            (10, query, most),
+            (11, 0, most),
+            (6, 0, up),
+            (7, 0, up),
+            (8, 0, down),
+            (9, 0, down),
+            (12, 0, out),
+            (13, 0, out),
         ),
     )
     length = first.proj[0].shape[0]
@@ -1677,6 +1717,11 @@
         for stream in range(2)
         for x, part in ((0, up), (1, down))
     )
+    if not last:
+        plan = tuple(
+            (x, 2 * x + stream, parts)
+            for x, stream, parts in sorted(plan, key=lambda entry: -entry[0])
+        )
     d_middle, d_mixed, grads.gain_ffn, *sums = back_sum(
         10 if last else 3,
         d_ffn_in,
@@ -1688,12 +1733,13 @@
         (d_gate_up, saved.product),
         (),
         before.sums_mix if last else (),
+        not last,
     )
     if last:
         sums, before.mix = sums[:4], sums[4:]
         grads.ffn = weight_scatter(sums)
     else:
-        sums_ffn = sums
+        sums_ffn, grads.down = sums[:4], sums[4:]
     d_both = matmul_nt(d_mixed, weights.out)
     if not last:
         (d_both,), (before.tail,) = after((d_both,), before.tail)
@@ -1727,10 +1773,10 @@
         step, zx = widths[3] - widths[2], widths[3]
         both, most = saved.both.shape[1] // 4, inner // 2
         plan = (
+            (1, 2, ((1, 0, 2 * both, both),)),
+            (1, 3, ((1, both, 3 * both, both),)),
             (0, 0, ((0, 0, query, query), (0, zx, zx + inner, most))),
-            (1, 0, ((1, 0, 2 * both, both),)),
             (0, 1, ((0, zx + most, zx + inner + most, most), (0, widths[2], widths[2], step))),
-            (1, 1, ((1, both, 3 * both, both),)),
         )
         d_hidden, d_hidden_low, grads.gain_in, d_shared, *sums = back_sum(
             4,
@@ -1743,8 +1789,9 @@
             (d_proj, saved.both),
             (d_shared,),
             sums_ffn,
+            True,
         )
-        sums, grads.ffn = sums[:4], sums[4:]
+        sums, grads.ffn, grads.out = sums[:4], sums[4:6], sums[6:]
         grads.sums_mix = sums
     grads.wide = d_shared
     return d_hidden, d_hidden_low, grads

time: 754 us -> 743 us (0.985)
  Pallas kernels: 481 us -> 462 us
  local copies, waits for them, and re-layouts: 86.9 us -> 99.2 us
    pallas_call x7, Pallas kernels: 320 us -> 304 us  [summed(): pl.pallas_call(functools.partial(kernel, n, CHUNKS, LAG), out_shape=outs,...]
    unnamed x174 -> x214, local copies, waits for them, and re-layouts: 60.2 us -> 74.2 us
  transfers between devices with their start and end apart: 22 -> 22, of which waited for: 3 -> 3; matrix products, arithmetic and copies ran while one was open for 22% -> 22% of each run, Pallas kernels for 61% -> 59%
where the time goes in v3:
time: 743 us; the launch traced here: 731 us
  Pallas kernels  462 us (62%)
  local copies, waits for them, and re-layouts  99.2 us (13%)
  matrix products  82.8 us (11%)
  other arithmetic  38.5 us (5%)
  starting transfers between devices  17.8 us (2%)
  between operations  17.3 us (2%)
  waiting for transfers between devices  13.6 us (2%)
    pallas_call x7, Pallas kernels, summed(): pl.pallas_call(functools.partial(kernel, n, CHUNKS, LAG), out_shape=outs,...  304 us
    pallas_call x4, Pallas kernels, mixer_call(): pl.pallas_call(functools.partial(kernel, count, widths, heads), out_shape...  130 us
    unnamed x214, local copies, waits for them, and re-layouts  74.2 us
    dot_general x8, matrix products, matmul_nt(): lax.dot_general(left, right, (((1,), (1,)), ((), ())), preferred_element_...  43.1 us
    dot_general x8, matrix products, matmul(): return jnp.dot(left, right, preferred_element_type=f32)  32.7 us
    pallas_call x1, Pallas kernels, finish(): pl.pallas_call(functools.partial(finish_kernel, count, places, widths), o...  28.6 us
  transfers between devices with their start and end apart: 22, of which 3 were waited for; matrix products, arithmetic and copies ran while one was open for 22% of the time, Pallas kernels for 59%

profile of v3, /device:TPU:0, one launch (start us, length us, event | category | flops | bytes accessed | tf_op | source)
XLA Modules:
  0.0 731.2 jit_solution(5359897631354515937)
XLA Ops:
  9.1 5.0 collective-permute-start
  18.1 6.7 copy.55
  37.9 10.3 %copy.58 = bf16[256,8,2,1024]{3,1,2,0:T(8,128)(2,1)} copy(bf16[256,8,2,1024]{3,2,1,0:T(2,128)(2,1)} %bitcast.207) | data formatting | bytes 16777216
  48.9 4.5 pad_maximum_fusion.refs_1_
  63.3 7.8 %fusion.4.proj_ref = f32[256,2688]{1,0:T(8,128)S(1)} fusion(bf16[256,2048]{1,0:T(8,128)(2,1)} %multiply_convert_fusion, bf16[2048,2688]{1,0:T(8,128)(2,1)} %constant_dynamic-update-slice_fusion.refs_0_, bf16[2048,2688]{1,0:T(8,128)(2,1)} %collective-permute-done.4.refs_2_, pred[]{:T(512)S(6)} %eq.54), kind=kOutput, calls=%fused_computation.5 | convolution fusion | flops 2824077312 | bytes 25821184 | tf_op jit(solution)/shard_map/dot_general | solution.py:1554
  71.1 26.1 %mixer5.2 = (bf16[256,1024]{1,0:T(8,128)(2,1)S(1)}, f32[256,768]{1,0:T(8,128)S(1)}, bf16[768,256]{1,0:T(8,128)(2,1)S(1)}, bf16[1024,256]{1,0:T(8,128)(2,1)S(1)}, f32[4,16,256]{2,1,0:T(8,128)S(1)}) custom-call(f32[256,2688]{1,0:T(8,128)S(1)} %fusion.4.proj_ref, f32[8,128]{1,0:T(8,128)S(1)} %pad.23.vec_ref, f32[1,768]{1,0:T(1,128)S(1)} %broadcast_in_dim_reshape.13.skip_ref, ...), custom_call_target="tpu_custom_call" | custom-call | bytes 20971520 | tf_op jit(solution)/shard_map/mixer5/pallas_call | solution.py:1165
  99.0 34.0 %line_sum1.1 = (f32[256,2048]{1,0:T(8,128)S(1)}, bf16[256,2048]{1,0:T(8,128)(2,1)S(1)}, bf16[2048,2688]{1,0:T(8,128)(2,1)}, bf16[1024,2048]{1,0:T(8,128)(2,1)S(1)}) custom-call(f32[256,2048]{1,0:T(8,128)S(1)} %fusion.15.p_ref, f32[256,2048]{1,0:T(8,128)S(1)} %convert_element_type.251.h_ref.v_ref, f32[1,2048]{1,0:T(1,128)S(1)} %bitcast.194, ...), custom_call_target="tpu_custom_call" | custom-call | bytes 20971520 | tf_op jit(solution)/shard_map/line_sum1/pallas_call | solution.py:561
  137.8 4.1 fusion.5.p_ref
  141.9 31.9 %line_sum2.1 = (bf16[256,2048]{1,0:T(8,128)(2,1)S(1)}, bf16[256,2048]{1,0:T(8,128)(2,1)S(1)}, bf16[2048,2048]{1,0:T(8,128)(2,1)S(1)}, bf16[1024,2048]{1,0:T(8,128)(2,1)S(1)}) custom-call(f32[256,2048]{1,0:T(8,128)S(1)} %fusion.5.p_ref, f32[256,2048]{1,0:T(8,128)S(1)} %get-tuple-element.106.h_ref.refs_2_, f32[1,2048]{1,0:T(1,128)S(1)} %bitcast.196, ...), custom_call_target="tpu_custom_call" | custom-call | bytes 20971520 | tf_op jit(solution)/shard_map/line_sum2/pallas_call | solution.py:561
  186.6 6.4 fusion.50.proj_ref
  193.0 28.6 %mixer5.3 = (bf16[256,1024]{1,0:T(8,128)(2,1)S(1)}, f32[256,768]{1,0:T(8,128)S(1)}, bf16[768,256]{1,0:T(8,128)(2,1)S(1)}, bf16[1024,256]{1,0:T(8,128)(2,1)S(1)}, f32[4,16,256]{2,1,0:T(8,128)S(1)}) custom-call(f32[256,2688]{1,0:T(8,128)S(1)} %fusion.50.proj_ref, f32[8,128]{1,0:T(8,128)S(1)} %pad.25.vec_ref, f32[1,768]{1,0:T(1,128)S(1)} %broadcast_in_dim_reshape.14.skip_ref, ...), custom_call_target="tpu_custom_call" | custom-call | bytes 20971520 | tf_op jit(solution)/shard_map/mixer5/pallas_call | solution.py:1165
  224.6 32.8 %line_sum9.1 = (f32[256,2048]{1,0:T(8,128)S(1)}, bf16[256,2048]{1,0:T(8,128)(2,1)S(1)}, bf16[2048,2048]{1,0:T(8,128)(2,1)S(1)}, bf16[1024,2048]{1,0:T(8,128)(2,1)S(1)}) custom-call(f32[256,2048]{1,0:T(8,128)S(1)} %fusion.51.p_ref, f32[256,2048]{1,0:T(8,128)S(1)} %copy-done.2, f32[1,2048]{1,0:T(1,128)S(1)} %bitcast.198, bf16[2048,2048]{1,0:T(8,128)(2,1)} %bitcast.202, ...), custom_call_target="tpu_custom_call" | custom-call | bytes 20971520 | tf_op jit(solution)/shard_map/line_sum9/pallas_call | solution.py:561
  266.5 7.0 fusion.52
  273.5 4.8 multiply_convert_fusion.5
  279.4 7.2 fusion.47.refs_0_
  295.6 43.2 %line_sum3.1 = (f32[256,2048]{1,0:T(8,128)S(1)}, bf16[256,2048]{1,0:T(8,128)(2,1)S(1)}, f32[8,2048]{1,0:T(8,128)S(1)}, bf16[2,512,512]{2,1,0:T(8,128)(2,1)S(1)},...) custom-call(f32[256,2048]{1,0:T(8,128)S(1)} %copy-done.15, ...), custom_call_target="tpu_custom_call" | custom-call | bytes 20971520 | tf_op jit(solution)/shard_map/line_sum3/pallas_call | solution.py:561
  344.9 28.4 %mixer6.2 = (bf16[256,2688]{1,0:T(8,128)(2,1)S(1)}, f32[8,128]{1,0:T(8,128)S(1)}) custom-call(f32[256,2688]{1,0:T(8,128)S(1)} %copy-done.6, f32[8,128]{1,0:T(8,128)S(1)} %pad.25.vec_ref, f32[1,768]{1,0:T(1,128)S(1)} %broadcast_in_dim_reshape.14.skip_ref, f32[256,8]{1,0:T(8,128)S(1)} %pad.24.tok_ref, f32[2,1024]{1,0:T(2,128)S(1)} %pad_maximum_fusion.14.key_ref, ...), custom_call_target="tpu_custom_call" | custom-call | bytes 20971520 | tf_op jit(solution)/shard_map/mixer6/pallas_call | solution.py:1165
  373.3 9.1 %fusion.54.refs_0_ = f32[256,2048]{1,0:T(8,128)} fusion(bf16[256,2688]{1,0:T(8,128)(2,1)S(1)} %get-tuple-element.124.refs_7_, bf16[2048,2688]{1,0:T(8,128)(2,1)} %get-tuple-element.109), kind=kOutput, calls=%fused_computation.189 | convolution fusion | flops 2818572288 | bytes 14483456 | tf_op jit(solution)/shard_map/dot_general | solution.py:1558
  382.6 63.9 %line_sum4.1 = (f32[256,2048]{1,0:T(8,128)}, bf16[256,2048]{1,0:T(8,128)(2,1)}, f32[8,2048]{1,0:T(8,128)S(1)}, bf16[256,1024]{1,0:T(8,128)(2,1)S(1)}, bf16[2,512...) custom-call(f32[256,2048]{1,0:T(8,128)} %fusion.54.refs_0_, ...), custom_call_target="tpu_custom_call" | custom-call | bytes 20971520 | tf_op jit(solution)/shard_map/line_sum4/pallas_call | solution.py:561
  446.6 3.5 multiply_convert_fusion.2
  451.2 7.2 fusion.46.refs_0_
  458.4 47.7 %line_sum10.1 = (f32[256,2048]{1,0:T(8,128)}, bf16[256,2048]{1,0:T(8,128)(2,1)}, f32[8,2048]{1,0:T(8,128)S(1)}, bf16[2,512,768]{2,1,0:T(8,128)(2,1)}, bf16[2,512...) custom-call(f32[256,2048]{1,0:T(8,128)} %fusion.46.refs_0_, ...), custom_call_target="tpu_custom_call" | custom-call | bytes 20971520 | tf_op jit(solution)/shard_map/line_sum10/pallas_call | solution.py:561
  511.2 4.0 fusion.14.d_both_ref
  522.9 46.6 %mixer6.3 = (bf16[256,2688]{1,0:T(8,128)(2,1)S(1)}, f32[8,128]{1,0:T(8,128)S(1)}) custom-call(f32[256,2688]{1,0:T(8,128)S(1)} %copy-done.4, f32[8,128]{1,0:T(8,128)S(1)} %pad.23.vec_ref, f32[1,768]{1,0:T(1,128)S(1)} %broadcast_in_dim_reshape.13.skip_ref, f32[256,8]{1,0:T(8,128)S(1)} %pad.24.tok_ref, f32[2,1024]{1,0:T(2,128)S(1)} %pad_maximum_fusion.14.key_ref, ...), custom_call_target="tpu_custom_call" | custom-call | bytes 20971520 | tf_op jit(solution)/shard_map/mixer6/pallas_call | solution.py:1165
  572.1 6.1 fusion.3.p_ref
  578.3 4.1 convolution_convert_fusion
  584.3 50.3 %line_sum7.1 = (f32[256,2048]{1,0:T(8,128)S(1)}, bf16[256,2048]{1,0:T(8,128)(2,1)}, f32[8,2048]{1,0:T(8,128)S(1)}, bf16[256,1024]{1,0:T(8,128)(2,1)S(1)}, bf16[5...) custom-call(f32[256,2048]{1,0:T(8,128)S(1)} %fusion.3.p_ref, bf16[256,1024]{1,0:T(8,128)(2,1)S(1)} %get-tuple-element.279.q_ref, ...), custom_call_target="tpu_custom_call" | custom-call | bytes 20971520 | tf_op jit(solution)/shard_map/line_sum7/pallas_call | solution.py:561
  644.1 3.4 fusion.16
  657.2 7.8 %collective-permute-done.11.refs_3_ = bf16[512,768]{1,0:T(8,128)(2,1)S(1)} collective-permute-done((bf16[512,768]{1,0:T(8,128)(2,1)}, bf16[512,768]{1,0:T(8,128)(2,1)S(1)}, u32[]{:S(2)}, u32[]{:S(2)}) %collective-permute-start.11) | collective-permute-done | bytes 786464 | tf_op jit(solution)/shard_map/ppermute | solution.py:1619
  668.9 28.6 %finish.1 = (bf16[512,256]{1,0:T(8,128)(2,1)}, f32[2,512,768]{2,1,0:T(8,128)}, f32[2,512,1024]{2,1,0:T(8,128)}, bf16[1024,512]{1,0:T(8,128)(2,1)}, bf16[1024,512...) custom-call(bf16[512,768]{1,0:T(8,128)(2,1)} %get-tuple-element.265., ...), custom_call_target="tpu_custom_call" | custom-call | bytes 20971520 | tf_op jit(solution)/shard_map/finish/pallas_call | solution.py:1535
  701.8 7.6 %copy.53 = f32[1,512,2,1024]{3,2,1,0:T(2,128)} copy(f32[1,512,2,1024]{3,1,2,0:T(8,128)} %bitcast.210) | data formatting | bytes 8388608
  709.4 4.1 copy.51
  (368 shorter events, 131.2 us)
Async XLA Ops:
  7.2 266.3 %all-gather.2.cloned.1.call-start = ((), (), s32[]{:S(2)}) async-start(), calls=%async_computation.1 | async-start | bytes 1310720 | tf_op jit(solution)/shard_map/all_gather | solution.py:1885
  9.1 24.0 %collective-permute-start = (bf16[64,2048]{1,0:T(8,128)(2,1)}, bf16[64,2048]{1,0:T(8,128)(2,1)}, u32[]{:S(2)}, u32[]{:S(2)}) collective-permute-start(bf16[64,2048]{1,0:T(8,128)(2,1)} %get-tuple-element.253), channel_id=1, source_target_pairs={{0,3},{1,2},{2,1},{3,0},{4,7},{5,6},{6,5},{7,4},{8,11},{9,10},{10,... | collective-permute-start | bytes 786440 | tf_op jit(solution)/shard_map/ppermute | solution.py:583
  14.1 22.6 %collective-permute-start.1 = (bf16[64,2048]{1,0:T(8,128)(2,1)}, bf16[64,2048]{1,0:T(8,128)(2,1)}, u32[]{:S(2)}, u32[]{:S(2)}) collective-permute-start(bf16[64,2048]{1,0:T(8,128)(2,1)} %get-tuple-element.253), channel_id=1, source_target_pairs={{0,2},{1,3},{2,0},{3,1},{4,6},{5,7},{6,4},{7,5},{8,10},{9,11},{10,... | collective-permute-start | bytes 786440 | tf_op jit(solution)/shard_map/ppermute | solution.py:583
  14.1 23.6 %collective-permute-start.2 = (bf16[64,2048]{1,0:T(8,128)(2,1)}, bf16[64,2048]{1,0:T(8,128)(2,1)S(1)}, u32[]{:S(2)}, u32[]{:S(2)}) collective-permute-start(bf16[64,2048]{1,0:T(8,128)(2,1)} %get-tuple-element.253), channel_id=1, source_target_pairs={{0,1},{1,0},{2,3},{3,2},{4,5},{5,4},{6,7},{7,6},{8,9},{9,8},{10,11... | collective-permute-start | bytes 786440 | tf_op jit(solution)/shard_map/ppermute | solution.py:583
  37.8 25.5 %collective-permute-start.4 = (bf16[2048,2688]{1,0:T(8,128)(2,1)}, bf16[2048,2688]{1,0:T(8,128)(2,1)}, u32[]{:S(2)}, u32[]{:S(2)}) collective-permute-start(bf16[2048,2688]{1,0:T(8,128)(2,1)} %constant_dynamic-update-slice_fusion.refs_0_), channel_id=1, source_target_pairs={{0,16},{16,0},{1,17},{17,1},{2,18},{18,2},{3,19},{19,3},{4,20},{20... | collective-permute-start | bytes 33030152 | tf_op jit(solution)/shard_map/ppermute | solution.py:1566
  48.2 86.8 %collective-permute-start.6 = (bf16[2048,2048]{1,0:T(8,128)(2,1)}, bf16[2048,2048]{1,0:T(8,128)(2,1)}, u32[]{:S(2)}, u32[]{:S(2)}) collective-permute-start(bf16[2048,2048]{1,0:T(8,128)(2,1)} %bitcast.200), channel_id=1, source_target_pairs={{0,16},{16,0},{1,17},{17,1},{2,18},{18,2},{3,19},{19,3},{4,20},{20... | collective-permute-start | bytes 25165832 | tf_op jit(solution)/shard_map/ppermute | solution.py:1566
  48.8 9.8 %collective-permute-start.3 = (f32[4132]{0:T(1024)S(1)}, f32[4132]{0:T(1024)S(1)}, u32[]{:S(2)}, u32[]{:S(2)}) collective-permute-start(f32[4132]{0:T(1024)S(1)} %concatenate.57), channel_id=1, source_target_pairs={{0,16},{16,0},{1,17},{17,1},{2,18},{18,2},{3,19},{19,3},{4,20},{20... | collective-permute-start | bytes 49592 | tf_op jit(solution)/shard_map/ppermute | solution.py:1566
  53.4 43.8 %collective-permute-start.5 = (bf16[1024,2048]{1,0:T(8,128)(2,1)}, bf16[1024,2048]{1,0:T(8,128)(2,1)}, u32[]{:S(2)}, u32[]{:S(2)}) collective-permute-start(bf16[1024,2048]{1,0:T(8,128)(2,1)} %pad_maximum_fusion.refs_1_), channel_id=1, source_target_pairs={{0,16},{16,0},{1,17},{17,1},{2,18},{18,2},{3,19},{19,3},{4,20},{20... | collective-permute-start | bytes 12582920 | tf_op jit(solution)/shard_map/ppermute | solution.py:1566
  53.9 83.9 %collective-permute-start.7 = (bf16[1024,2048]{1,0:T(8,128)(2,1)}, bf16[1024,2048]{1,0:T(8,128)(2,1)}, u32[]{:S(2)}, u32[]{:S(2)}) collective-permute-start(bf16[1024,2048]{1,0:T(8,128)(2,1)} %bitcast.19.refs_1_), channel_id=1, source_target_pairs={{0,16},{16,0},{1,17},{17,1},{2,18},{18,2},{3,19},{19,3},{4,20},{20... | collective-permute-start | bytes 12582920 | tf_op jit(solution)/shard_map/ppermute | solution.py:1566
  61.1 517.0 %collective-permute-start.18 = (bf16[256,2048]{1,0:T(8,128)(2,1)}, bf16[256,2048]{1,0:T(8,128)(2,1)}, u32[]{:S(2)}, u32[]{:S(2)}) collective-permute-start(bf16[256,2048]{1,0:T(8,128)(2,1)} %multiply_convert_fusion), channel_id=1, source_target_pairs={{0,16},{16,0},{1,17},{17,1},{2,18},{18,2},{3,19},{19,3},{4,20},{20... | collective-permute-start | bytes 3145736 | tf_op jit(solution)/shard_map/ppermute | solution.py:1566
  63.3 34.0 %copy-start.71 = (bf16[1,768,2048]{2,1,0:T(8,128)(2,1)S(1)}, bf16[1,768,2048]{2,1,0:T(8,128)(2,1)}, u32[]{:S(2)}) copy-start(bf16[1,768,2048]{2,1,0:T(8,128)(2,1)} %param.30) | copy-start | bytes 9437188
  63.3 34.0 %copy-start.80 = (bf16[1,256,2048]{2,1,0:T(8,128)(2,1)S(1)}, bf16[1,256,2048]{2,1,0:T(8,128)(2,1)}, u32[]{:S(2)}) copy-start(bf16[1,256,2048]{2,1,0:T(8,128)(2,1)} %param.23) | copy-start | bytes 3145732
  97.3 37.7 %slice-start = ((s8[8388608]{0:T(1024)(128)(4,1)}), s8[4194304]{0:T(1024)(128)(4,1)S(1)}, s32[]{:S(2)}) async-start(s8[8388608]{0:T(1024)(128)(4,1)} %bitcast.203), calls=%async_computation.3 | async-start | bytes 8388608
  98.9 36.1 %slice-start.1 = ((s8[8388608]{0:T(1024)(128)(4,1)}), s8[4194304]{0:T(1024)(128)(4,1)S(1)}, s32[]{:S(2)}) async-start(s8[8388608]{0:T(1024)(128)(4,1)} %bitcast.203), calls=%async_computation.4 | async-start | bytes 8388608
  179.1 78.3 %copy-start.19 = (bf16[256,2048]{1,0:T(8,128)(2,1)}, bf16[256,2048]{1,0:T(8,128)(2,1)S(1)}, u32[]{:S(2)}) copy-start(bf16[256,2048]{1,0:T(8,128)(2,1)S(1)} %get-tuple-element.108.refs_5_) | copy-start | bytes 3145732
  181.7 473.6 %reduce-scatter.2.cloned.1.call-start = ((), (), s32[]{:S(2)}) async-start(), calls=%async_computation.2 | async-start | bytes 1310720 | tf_op jit(solution)/shard_map/reduce_scatter | solution.py:1922
  183.6 333.6 %collective-permute-start.13 = (bf16[256,512]{1,0:T(8,128)(2,1)}, bf16[256,512]{1,0:T(8,128)(2,1)}, u32[]{:S(2)}, u32[]{:S(2)}) collective-permute-start(bf16[256,512]{1,0:T(8,128)(2,1)} %get-tuple-element.296), channel_id=1, source_target_pairs={{0,16},{16,0},{1,17},{17,1},{2,18},{18,2},{3,19},{19,3},{4,20},{20... | collective-permute-start | bytes 786440 | tf_op jit(solution)/shard_map/ppermute | solution.py:1566
  186.6 35.8 %copy-start.65 = (bf16[1024,2048]{1,0:T(8,128)(2,1)S(1)}, bf16[1024,2048]{1,0:T(8,128)(2,1)}, u32[]{:S(2)}) copy-start(bf16[1024,2048]{1,0:T(8,128)(2,1)} %copy-done.64) | copy-start | bytes 12582916
  295.5 44.6 %copy-start.66 = (bf16[1024,2048]{1,0:T(8,128)(2,1)S(1)}, bf16[1024,2048]{1,0:T(8,128)(2,1)}, u32[]{:S(2)}) copy-start(bf16[1024,2048]{1,0:T(8,128)(2,1)} %copy-done.64) | copy-start | bytes 12582916
  382.6 64.0 %copy-start.63 = (bf16[1024,2048]{1,0:T(8,128)(2,1)S(1)}, bf16[1024,2048]{1,0:T(8,128)(2,1)}, u32[]{:S(2)}) copy-start(bf16[1024,2048]{1,0:T(8,128)(2,1)} %copy-done.62) | copy-start | bytes 12582916
  382.6 64.0 %copy-start.73 = (f32[256,2048]{1,0:T(8,128)S(1)}, f32[256,2048]{1,0:T(8,128)}, u32[]{:S(2)}) copy-start(f32[256,2048]{1,0:T(8,128)} %copy-done.72) | copy-start | bytes 6291460
  506.8 10.4 %collective-permute-start.12 = (bf16[256,2048]{1,0:T(8,128)(2,1)}, bf16[256,2048]{1,0:T(8,128)(2,1)}, u32[]{:S(2)}, u32[]{:S(2)}) collective-permute-start(bf16[256,2048]{1,0:T(8,128)(2,1)} %get-tuple-element.141), channel_id=1, source_target_pairs={{0,16},{16,0},{1,17},{17,1},{2,18},{18,2},{3,19},{19,3},{4,20},{20... | collective-permute-start | bytes 3145736 | tf_op jit(solution)/shard_map/ppermute | solution.py:1566
  508.5 135.6 %collective-permute-start.10 = (bf16[1024,768]{1,0:T(8,128)(2,1)}, bf16[1024,768]{1,0:T(8,128)(2,1)}, u32[]{:S(2)}, u32[]{:S(2)}) collective-permute-start(bf16[1024,768]{1,0:T(8,128)(2,1)} %bitcast.234), channel_id=1, source_target_pairs={{0,4},{4,0},{8,12},{12,8},{1,5},{5,1},{9,13},{13,9},{2,6},{6,2},{1... | collective-permute-start | bytes 4718600 | tf_op jit(solution)/shard_map/ppermute | solution.py:1619
  510.2 138.6 %collective-permute-start.8 = (bf16[1024,768]{1,0:T(8,128)(2,1)}, bf16[1024,768]{1,0:T(8,128)(2,1)}, u32[]{:S(2)}, u32[]{:S(2)}) collective-permute-start(bf16[1024,768]{1,0:T(8,128)(2,1)} %bitcast.233), channel_id=1, source_target_pairs={{0,8},{4,12},{8,0},{12,4},{1,9},{5,13},{9,1},{13,5},{2,10},{6,14},... | collective-permute-start | bytes 4718600 | tf_op jit(solution)/shard_map/ppermute | solution.py:1619
  570.8 7.5 %collective-permute-start.19 = (bf16[256,1024]{1,0:T(8,128)(2,1)S(1)}, bf16[256,1024]{1,0:T(8,128)(2,1)}, u32[]{:S(2)}, u32[]{:S(2)}) collective-permute-start(bf16[256,1024]{1,0:T(8,128)(2,1)S(1)} %pad_maximum_fusion.11), channel_id=1, source_target_pairs={{0,16},{16,0},{1,17},{17,1},{2,18},{18,2},{3,19},{19,3},{4,20},{20... | collective-permute-start | bytes 1572872 | tf_op jit(solution)/shard_map/ppermute | solution.py:1566
  570.9 67.6 %collective-permute-start.16 = (bf16[1024,256]{1,0:T(8,128)(2,1)}, bf16[1024,256]{1,0:T(8,128)(2,1)}, u32[]{:S(2)}, u32[]{:S(2)}) collective-permute-start(bf16[1024,256]{1,0:T(8,128)(2,1)} %bitcast.41), channel_id=1, source_target_pairs={{0,4},{4,0},{8,12},{12,8},{1,5},{5,1},{9,13},{13,9},{2,6},{6,2},{1... | collective-permute-start | bytes 1572872 | tf_op jit(solution)/shard_map/ppermute | solution.py:1619
  578.2 63.1 %collective-permute-start.14 = (bf16[1024,256]{1,0:T(8,128)(2,1)}, bf16[1024,256]{1,0:T(8,128)(2,1)}, u32[]{:S(2)}, u32[]{:S(2)}) collective-permute-start(bf16[1024,256]{1,0:T(8,128)(2,1)} %bitcast.38), channel_id=1, source_target_pairs={{0,8},{4,12},{8,0},{12,4},{1,9},{5,13},{9,1},{13,5},{2,10},{6,14},... | collective-permute-start | bytes 1572872 | tf_op jit(solution)/shard_map/ppermute | solution.py:1619
  584.3 53.3 %copy-start.83 = (bf16[512,128]{1,0:T(8,128)(2,1)S(1)}, bf16[512,128]{1,0:T(8,128)(2,1)}, u32[]{:S(2)}) copy-start(bf16[512,128]{1,0:T(8,128)(2,1)} %slice.240) | copy-start | bytes 393220
  640.5 16.7 %collective-permute-start.17 = (bf16[512,256]{1,0:T(8,128)(2,1)S(1)}, bf16[512,256]{1,0:T(8,128)(2,1)S(1)}, u32[]{:S(2)}, u32[]{:S(2)}) collective-permute-start(bf16[512,256]{1,0:T(8,128)(2,1)S(1)} %get-tuple-element.289), channel_id=1, source_target_pairs={{0,8},{4,12},{8,0},{12,4},{1,9},{5,13},{9,1},{13,5},{2,10},{6,14},... | collective-permute-start | bytes 786440 | tf_op jit(solution)/shard_map/ppermute | solution.py:1619
  643.2 14.0 %collective-permute-start.15 = (bf16[512,256]{1,0:T(8,128)(2,1)}, bf16[512,256]{1,0:T(8,128)(2,1)S(1)}, u32[]{:S(2)}, u32[]{:S(2)}) collective-permute-start(bf16[512,256]{1,0:T(8,128)(2,1)} %get-tuple-element.291), channel_id=1, source_target_pairs={{0,4},{4,0},{8,12},{12,8},{1,5},{5,1},{9,13},{13,9},{2,6},{6,2},{1... | collective-permute-start | bytes 786440 | tf_op jit(solution)/shard_map/ppermute | solution.py:1619
  647.5 17.6 %collective-permute-start.11 = (bf16[512,768]{1,0:T(8,128)(2,1)}, bf16[512,768]{1,0:T(8,128)(2,1)S(1)}, u32[]{:S(2)}, u32[]{:S(2)}) collective-permute-start(bf16[512,768]{1,0:T(8,128)(2,1)} %get-tuple-element.262), channel_id=1, source_target_pairs={{0,8},{4,12},{8,0},{12,4},{1,9},{5,13},{9,1},{13,5},{2,10},{6,14},... | collective-permute-start | bytes 2359304 | tf_op jit(solution)/shard_map/ppermute | solution.py:1619
  651.6 16.4 %collective-permute-start.9 = (bf16[512,768]{1,0:T(8,128)(2,1)}, bf16[512,768]{1,0:T(8,128)(2,1)S(1)}, u32[]{:S(2)}, u32[]{:S(2)}) collective-permute-start(bf16[512,768]{1,0:T(8,128)(2,1)} %get-tuple-element.264), channel_id=1, source_target_pairs={{0,4},{4,0},{8,12},{12,8},{1,5},{5,1},{9,13},{13,9},{2,6},{6,2},{1... | collective-permute-start | bytes 2359304 | tf_op jit(solution)/shard_map/ppermute | solution.py:1619
  (89 other events, 448.2 us)
Sparse Core Ops, SparseCore 0:
  181.8 32.2 all-gather.1
  508.6 25.1 reduce-scatter.1

commit v4 on v3

--- a/solution.py
+++ b/solution.py
@@ -130,7 +130,7 @@
         return p_ref[row_slice(j, rows), :]
 
     def done(j, total):
-        v = h_ref[row_slice(j, rows), :] + total
+        v = h_ref[row_slice(j, rows), :].astype(f32) + total
         r = lax.rsqrt(jnp.mean(v * v, axis=-1, keepdims=True) + eps)
         mid_ref[row_slice(j, rows), :] = v
         low_ref[row_slice(j, rows), :] = (v * r * gain_ref[...]).astype(bf16)
@@ -499,7 +499,7 @@
     jobs = [fill]
     boxes = 4 * len(ctx_bits())
     if ready:
-        turns = (8, 14) if beside else (9,)
+        turns = (9, 17) if beside else (9,)
         jobs.append(Halving(streams, totals, rest[:boxes], turns))
         rest = rest[boxes:]
     if soon:
@@ -1874,8 +1874,8 @@
     def own_rows(values):
         return lax.dynamic_slice_in_dim(values, shard * part, part, 0)
 
-    hidden = block_in.astype(f32)
-    normed = norm_apply(hidden, layers[0].gain_in).astype(bf16)
+    hidden = block_in
+    normed = norm_apply(hidden.astype(f32), layers[0].gain_in).astype(bf16)
     hiddens, outs, saves = [], [], []
     for layer in range(2):
         weights = layers[layer]
@@ -1906,7 +1906,7 @@
             )
             second.gate_up, second.down = chosen
             outs.append(own_rows(out_low))
-            hidden = out_low.astype(f32)
+            hidden = out_low
         else:
             held = types.SimpleNamespace(tail=partial.astype(bf16))
 

time: 743 us -> 726 us (0.977)
    unnamed x214 -> x212, local copies, waits for them, and re-layouts: 74.2 us -> 69 us
  transfers between devices with their start and end apart: 22 -> 22, of which waited for: 3 -> 3; matrix products, arithmetic and copies ran while one was open for 22% -> 20% of each run, Pallas kernels for 59% -> 60%
where the time goes in v4:
time: 726 us; the launch traced here: 714 us
  Pallas kernels  460 us (63%)
  local copies, waits for them, and re-layouts  94.4 us (13%)
  matrix products  76.1 us (10%)
  other arithmetic  33.6 us (5%)
  starting transfers between devices  19.1 us (3%)
  between operations  17.4 us (2%)
  waiting for transfers between devices  13.3 us (2%)
    pallas_call x7, Pallas kernels, summed(): pl.pallas_call(functools.partial(kernel, n, CHUNKS, LAG), out_shape=outs,...  303 us
    pallas_call x4, Pallas kernels, mixer_call(): pl.pallas_call(functools.partial(kernel, count, widths, heads), out_shape...  128 us
    unnamed x212, local copies, waits for them, and re-layouts  69 us
    dot_general x8, matrix products, matmul_nt(): lax.dot_general(left, right, (((1,), (1,)), ((), ())), preferred_element_...  40.9 us
    dot_general x8, matrix products, matmul(): return jnp.dot(left, right, preferred_element_type=f32)  28.4 us
    pallas_call x1, Pallas kernels, finish(): pl.pallas_call(functools.partial(finish_kernel, count, places, widths), o...  28.3 us
  transfers between devices with their start and end apart: 22, of which 3 were waited for; matrix products, arithmetic and copies ran while one was open for 20% of the time, Pallas kernels for 60%

profile of v4, /device:TPU:0, one launch (start us, length us, event | category | flops | bytes accessed | tf_op | source)
XLA Modules:
  0.0 713.9 jit_solution(10787232993012900246)
XLA Ops:
  9.1 5.0 collective-permute-start
  18.1 6.7 copy.55
  37.9 10.3 %copy.58 = bf16[256,8,2,1024]{3,1,2,0:T(8,128)(2,1)} copy(bf16[256,8,2,1024]{3,2,1,0:T(2,128)(2,1)} %bitcast.211) | data formatting | bytes 16777216
  48.8 4.5 pad_maximum_fusion.refs_1_
  63.0 7.8 %fusion.4.proj_ref = f32[256,2688]{1,0:T(8,128)S(1)} fusion(bf16[256,2048]{1,0:T(8,128)(2,1)} %fusion.10, bf16[2048,2688]{1,0:T(8,128)(2,1)} %constant_dynamic-update-slice_fusion.refs_0_, bf16[2048,2688]{1,0:T(8,128)(2,1)} %collective-permute-done.4.refs_2_, pred[]{:T(512)S(6)} %eq.54), kind=kOutput, calls=%fused_computation.5 | convolution fusion | flops 2824077312 | bytes 25821184 | tf_op jit(solution)/shard_map/dot_general | solution.py:1554
  70.8 26.1 %mixer5.2 = (bf16[256,1024]{1,0:T(8,128)(2,1)S(1)}, f32[256,768]{1,0:T(8,128)S(1)}, bf16[768,256]{1,0:T(8,128)(2,1)S(1)}, bf16[1024,256]{1,0:T(8,128)(2,1)S(1)}, f32[4,16,256]{2,1,0:T(8,128)S(1)}) custom-call(f32[256,2688]{1,0:T(8,128)S(1)} %fusion.4.proj_ref, f32[8,128]{1,0:T(8,128)S(1)} %pad.23.vec_ref, f32[1,768]{1,0:T(1,128)S(1)} %broadcast_in_dim_reshape.13.skip_ref, ...), custom_call_target="tpu_custom_call" | custom-call | bytes 20971520 | tf_op jit(solution)/shard_map/mixer5/pallas_call | solution.py:1165
  98.7 34.0 %line_sum1.1 = (f32[256,2048]{1,0:T(8,128)S(1)}, bf16[256,2048]{1,0:T(8,128)(2,1)S(1)}, bf16[2048,2688]{1,0:T(8,128)(2,1)}, bf16[1024,2048]{1,0:T(8,128)(2,1)S(1)}) custom-call(f32[256,2048]{1,0:T(8,128)S(1)} %fusion.18.p_ref, bf16[256,2048]{1,0:T(8,128)(2,1)S(1)} %constant_dynamic-update-slice_fusion.1.h_ref.v_ref, f32[1,2048]{1,0:T(1,128)S(1)} %bitcast.194, ...), custom_call_target="tpu_custom_call" | custom-call | bytes 20971520 | tf_op jit(solution)/shard_map/line_sum1/pallas_call | solution.py:561
  135.6 4.0 fusion.5.p_ref
  139.6 31.6 %line_sum2.1 = (bf16[256,2048]{1,0:T(8,128)(2,1)S(1)}, bf16[256,2048]{1,0:T(8,128)(2,1)S(1)}, bf16[2048,2048]{1,0:T(8,128)(2,1)S(1)}, bf16[1024,2048]{1,0:T(8,128)(2,1)S(1)}) custom-call(f32[256,2048]{1,0:T(8,128)S(1)} %fusion.5.p_ref, f32[256,2048]{1,0:T(8,128)S(1)} %get-tuple-element.106.h_ref.refs_2_, f32[1,2048]{1,0:T(1,128)S(1)} %bitcast.196, ...), custom_call_target="tpu_custom_call" | custom-call | bytes 20971520 | tf_op jit(solution)/shard_map/line_sum2/pallas_call | solution.py:561
  180.5 4.0 collective-permute-start.13
  184.5 6.7 fusion.53.proj_ref
  191.2 28.7 %mixer5.3 = (bf16[256,1024]{1,0:T(8,128)(2,1)S(1)}, f32[256,768]{1,0:T(8,128)S(1)}, bf16[768,256]{1,0:T(8,128)(2,1)S(1)}, bf16[1024,256]{1,0:T(8,128)(2,1)S(1)}, f32[4,16,256]{2,1,0:T(8,128)S(1)}) custom-call(f32[256,2688]{1,0:T(8,128)S(1)} %fusion.53.proj_ref, f32[8,128]{1,0:T(8,128)S(1)} %pad.25.vec_ref, f32[1,768]{1,0:T(1,128)S(1)} %broadcast_in_dim_reshape.14.skip_ref, ...), custom_call_target="tpu_custom_call" | custom-call | bytes 20971520 | tf_op jit(solution)/shard_map/mixer5/pallas_call | solution.py:1165
  221.9 32.9 %line_sum9.1 = (f32[256,2048]{1,0:T(8,128)S(1)}, bf16[256,2048]{1,0:T(8,128)(2,1)S(1)}, bf16[2048,2048]{1,0:T(8,128)(2,1)S(1)}, bf16[1024,2048]{1,0:T(8,128)(2,1)S(1)}) custom-call(f32[256,2048]{1,0:T(8,128)S(1)} %fusion.54.p_ref, bf16[256,2048]{1,0:T(8,128)(2,1)S(1)} %copy-done.8, f32[1,2048]{1,0:T(1,128)S(1)} %bitcast.198, bf16[2048,2048]{1,0:T(8,128)(2,1)} %bitcast.206, ...), custom_call_target="tpu_custom_call" | custom-call | bytes 20971520 | tf_op jit(solution)/shard_map/line_sum9/pallas_call | solution.py:561
  256.1 3.3 copy-done.58
  265.0 4.2 multiply_convert_fusion.4
  269.2 7.2 %fusion.50.refs_0_ = f32[256,2048]{1,0:T(8,128)} fusion(bf16[2048,2048]{1,0:T(8,128)(2,1)} %copy-done.59, bf16[256,1024]{1,0:T(8,128)(2,1)S(1)} %get-tuple-element.269, bf16[256,1024]{1,0:T(8,128)(2,1)S(1)} %get-tuple-element.268), kind=kOutput, calls=%fused_computation.185 | convolution fusion | flops 2149580800 | bytes 11534336 | tf_op jit(solution)/shard_map/dot_general | solution.py:1558
  284.1 43.6 %line_sum3.1 = (f32[256,2048]{1,0:T(8,128)S(1)}, bf16[256,2048]{1,0:T(8,128)(2,1)S(1)}, f32[8,2048]{1,0:T(8,128)S(1)}, bf16[2,512,512]{2,1,0:T(8,128)(2,1)S(1)},...) custom-call(f32[256,2048]{1,0:T(8,128)S(1)} %copy-done.14, ...), custom_call_target="tpu_custom_call" | custom-call | bytes 20971520 | tf_op jit(solution)/shard_map/line_sum3/pallas_call | solution.py:561
  334.0 27.1 %mixer6.2 = (bf16[256,2688]{1,0:T(8,128)(2,1)S(1)}, f32[8,128]{1,0:T(8,128)S(1)}) custom-call(f32[256,2688]{1,0:T(8,128)S(1)} %copy-done.5, f32[8,128]{1,0:T(8,128)S(1)} %pad.25.vec_ref, f32[1,768]{1,0:T(1,128)S(1)} %broadcast_in_dim_reshape.14.skip_ref, f32[256,8]{1,0:T(8,128)S(1)} %pad.24.tok_ref, f32[2,1024]{1,0:T(2,128)S(1)} %pad_maximum_fusion.14.key_ref, ...), custom_call_target="tpu_custom_call" | custom-call | bytes 20971520 | tf_op jit(solution)/shard_map/mixer6/pallas_call | solution.py:1165
  361.2 9.1 %fusion.57.refs_0_ = f32[256,2048]{1,0:T(8,128)} fusion(bf16[256,2688]{1,0:T(8,128)(2,1)S(1)} %get-tuple-element.124.refs_7_, bf16[2048,2688]{1,0:T(8,128)(2,1)} %get-tuple-element.109), kind=kOutput, calls=%fused_computation.192 | convolution fusion | flops 2818572288 | bytes 14483456 | tf_op jit(solution)/shard_map/dot_general | solution.py:1558
  370.4 63.0 %line_sum4.1 = (f32[256,2048]{1,0:T(8,128)}, bf16[256,2048]{1,0:T(8,128)(2,1)}, f32[8,2048]{1,0:T(8,128)S(1)}, bf16[256,1024]{1,0:T(8,128)(2,1)S(1)}, bf16[2,512...) custom-call(f32[256,2048]{1,0:T(8,128)} %fusion.57.refs_0_, ...), custom_call_target="tpu_custom_call" | custom-call | bytes 20971520 | tf_op jit(solution)/shard_map/line_sum4/pallas_call | solution.py:561
  433.5 5.4 multiply_convert_fusion.1
  440.0 3.7 fusion.49.refs_0_
  443.7 47.8 %line_sum10.1 = (f32[256,2048]{1,0:T(8,128)}, bf16[256,2048]{1,0:T(8,128)(2,1)}, f32[8,2048]{1,0:T(8,128)S(1)}, bf16[2,512,768]{2,1,0:T(8,128)(2,1)}, bf16[2,512...) custom-call(f32[256,2048]{1,0:T(8,128)} %fusion.49.refs_0_, ...), custom_call_target="tpu_custom_call" | custom-call | bytes 20971520 | tf_op jit(solution)/shard_map/line_sum10/pallas_call | solution.py:561
  495.4 3.9 fusion.17.d_both_ref
  506.9 46.4 %mixer6.3 = (bf16[256,2688]{1,0:T(8,128)(2,1)S(1)}, f32[8,128]{1,0:T(8,128)S(1)}) custom-call(f32[256,2688]{1,0:T(8,128)S(1)} %copy-done.3, f32[8,128]{1,0:T(8,128)S(1)} %pad.23.vec_ref, f32[1,768]{1,0:T(1,128)S(1)} %broadcast_in_dim_reshape.13.skip_ref, f32[256,8]{1,0:T(8,128)S(1)} %pad.24.tok_ref, f32[2,1024]{1,0:T(2,128)S(1)} %pad_maximum_fusion.14.key_ref, ...), custom_call_target="tpu_custom_call" | custom-call | bytes 20971520 | tf_op jit(solution)/shard_map/mixer6/pallas_call | solution.py:1165
  556.2 6.1 fusion.3.p_ref
  562.4 3.9 convolution_convert_fusion
  568.4 50.5 %line_sum7.1 = (f32[256,2048]{1,0:T(8,128)S(1)}, bf16[256,2048]{1,0:T(8,128)(2,1)}, f32[8,2048]{1,0:T(8,128)S(1)}, bf16[256,1024]{1,0:T(8,128)(2,1)S(1)}, bf16[5...) custom-call(f32[256,2048]{1,0:T(8,128)S(1)} %fusion.3.p_ref, bf16[256,1024]{1,0:T(8,128)(2,1)S(1)} %get-tuple-element.279.q_ref, ...), custom_call_target="tpu_custom_call" | custom-call | bytes 20971520 | tf_op jit(solution)/shard_map/line_sum7/pallas_call | solution.py:561
  640.6 7.9 %collective-permute-done.11.refs_3_ = bf16[512,768]{1,0:T(8,128)(2,1)S(1)} collective-permute-done((bf16[512,768]{1,0:T(8,128)(2,1)}, bf16[512,768]{1,0:T(8,128)(2,1)S(1)}, u32[]{:S(2)}, u32[]{:S(2)}) %collective-permute-start.11) | collective-permute-done | bytes 786464 | tf_op jit(solution)/shard_map/ppermute | solution.py:1619
  651.9 28.3 %finish.1 = (bf16[512,256]{1,0:T(8,128)(2,1)}, f32[2,512,768]{2,1,0:T(8,128)}, f32[2,512,1024]{2,1,0:T(8,128)}, bf16[1024,512]{1,0:T(8,128)(2,1)}, bf16[1024,512...) custom-call(bf16[512,768]{1,0:T(8,128)(2,1)} %get-tuple-element.265., ...), custom_call_target="tpu_custom_call" | custom-call | bytes 20971520 | tf_op jit(solution)/shard_map/finish/pallas_call | solution.py:1535
  684.5 7.6 %copy.53 = f32[1,512,2,1024]{3,2,1,0:T(2,128)} copy(f32[1,512,2,1024]{3,1,2,0:T(8,128)} %bitcast.214) | data formatting | bytes 8388608
  692.1 4.1 copy.51
  (366 shorter events, 121.1 us)
Async XLA Ops:
  7.2 257.7 %all-gather.2.cloned.1.call-start = ((), (), s32[]{:S(2)}) async-start(), calls=%async_computation.1 | async-start | bytes 1310720 | tf_op jit(solution)/shard_map/all_gather | solution.py:1885
  9.1 24.0 %collective-permute-start = (bf16[64,2048]{1,0:T(8,128)(2,1)}, bf16[64,2048]{1,0:T(8,128)(2,1)}, u32[]{:S(2)}, u32[]{:S(2)}) collective-permute-start(bf16[64,2048]{1,0:T(8,128)(2,1)} %get-tuple-element.253), channel_id=1, source_target_pairs={{0,3},{1,2},{2,1},{3,0},{4,7},{5,6},{6,5},{7,4},{8,11},{9,10},{10,... | collective-permute-start | bytes 786440 | tf_op jit(solution)/shard_map/ppermute | solution.py:583
  14.1 22.6 %collective-permute-start.1 = (bf16[64,2048]{1,0:T(8,128)(2,1)}, bf16[64,2048]{1,0:T(8,128)(2,1)}, u32[]{:S(2)}, u32[]{:S(2)}) collective-permute-start(bf16[64,2048]{1,0:T(8,128)(2,1)} %get-tuple-element.253), channel_id=1, source_target_pairs={{0,2},{1,3},{2,0},{3,1},{4,6},{5,7},{6,4},{7,5},{8,10},{9,11},{10,... | collective-permute-start | bytes 786440 | tf_op jit(solution)/shard_map/ppermute | solution.py:583
  14.1 23.6 %collective-permute-start.2 = (bf16[64,2048]{1,0:T(8,128)(2,1)}, bf16[64,2048]{1,0:T(8,128)(2,1)S(1)}, u32[]{:S(2)}, u32[]{:S(2)}) collective-permute-start(bf16[64,2048]{1,0:T(8,128)(2,1)} %get-tuple-element.253), channel_id=1, source_target_pairs={{0,1},{1,0},{2,3},{3,2},{4,5},{5,4},{6,7},{7,6},{8,9},{9,8},{10,11... | collective-permute-start | bytes 786440 | tf_op jit(solution)/shard_map/ppermute | solution.py:583
  37.8 25.2 %collective-permute-start.4 = (bf16[2048,2688]{1,0:T(8,128)(2,1)}, bf16[2048,2688]{1,0:T(8,128)(2,1)}, u32[]{:S(2)}, u32[]{:S(2)}) collective-permute-start(bf16[2048,2688]{1,0:T(8,128)(2,1)} %constant_dynamic-update-slice_fusion.refs_0_), channel_id=1, source_target_pairs={{0,16},{16,0},{1,17},{17,1},{2,18},{18,2},{3,19},{19,3},{4,20},{20... | collective-permute-start | bytes 33030152 | tf_op jit(solution)/shard_map/ppermute | solution.py:1566
  48.2 84.6 %collective-permute-start.6 = (bf16[2048,2048]{1,0:T(8,128)(2,1)}, bf16[2048,2048]{1,0:T(8,128)(2,1)}, u32[]{:S(2)}, u32[]{:S(2)}) collective-permute-start(bf16[2048,2048]{1,0:T(8,128)(2,1)} %bitcast.204), channel_id=1, source_target_pairs={{0,16},{16,0},{1,17},{17,1},{2,18},{18,2},{3,19},{19,3},{4,20},{20... | collective-permute-start | bytes 25165832 | tf_op jit(solution)/shard_map/ppermute | solution.py:1566
  48.8 9.8 %collective-permute-start.3 = (f32[4132]{0:T(1024)S(1)}, f32[4132]{0:T(1024)S(1)}, u32[]{:S(2)}, u32[]{:S(2)}) collective-permute-start(f32[4132]{0:T(1024)S(1)} %concatenate.57), channel_id=1, source_target_pairs={{0,16},{16,0},{1,17},{17,1},{2,18},{18,2},{3,19},{19,3},{4,20},{20... | collective-permute-start | bytes 49592 | tf_op jit(solution)/shard_map/ppermute | solution.py:1566
  53.4 43.6 %collective-permute-start.5 = (bf16[1024,2048]{1,0:T(8,128)(2,1)}, bf16[1024,2048]{1,0:T(8,128)(2,1)}, u32[]{:S(2)}, u32[]{:S(2)}) collective-permute-start(bf16[1024,2048]{1,0:T(8,128)(2,1)} %pad_maximum_fusion.refs_1_), channel_id=1, source_target_pairs={{0,16},{16,0},{1,17},{17,1},{2,18},{18,2},{3,19},{19,3},{4,20},{20... | collective-permute-start | bytes 12582920 | tf_op jit(solution)/shard_map/ppermute | solution.py:1566
  53.8 81.7 %collective-permute-start.7 = (bf16[1024,2048]{1,0:T(8,128)(2,1)}, bf16[1024,2048]{1,0:T(8,128)(2,1)}, u32[]{:S(2)}, u32[]{:S(2)}) collective-permute-start(bf16[1024,2048]{1,0:T(8,128)(2,1)} %bitcast.19.refs_1_), channel_id=1, source_target_pairs={{0,16},{16,0},{1,17},{17,1},{2,18},{18,2},{3,19},{19,3},{4,20},{20... | collective-permute-start | bytes 12582920 | tf_op jit(solution)/shard_map/ppermute | solution.py:1566
  60.9 501.5 %collective-permute-start.18 = (bf16[256,2048]{1,0:T(8,128)(2,1)}, bf16[256,2048]{1,0:T(8,128)(2,1)}, u32[]{:S(2)}, u32[]{:S(2)}) collective-permute-start(bf16[256,2048]{1,0:T(8,128)(2,1)} %fusion.10), channel_id=1, source_target_pairs={{0,16},{16,0},{1,17},{17,1},{2,18},{18,2},{3,19},{19,3},{4,20},{20... | collective-permute-start | bytes 3145736 | tf_op jit(solution)/shard_map/ppermute | solution.py:1566
  63.0 34.0 %copy-start.68 = (bf16[1,768,2048]{2,1,0:T(8,128)(2,1)S(1)}, bf16[1,768,2048]{2,1,0:T(8,128)(2,1)}, u32[]{:S(2)}) copy-start(bf16[1,768,2048]{2,1,0:T(8,128)(2,1)} %param.30) | copy-start | bytes 9437188
  97.0 35.8 %slice-start.4 = ((s8[8388608]{0:T(1024)(128)(4,1)}), s8[4194304]{0:T(1024)(128)(4,1)S(1)}, s32[]{:S(2)}) async-start(s8[8388608]{0:T(1024)(128)(4,1)} %bitcast.207), calls=%async_computation.7 | async-start | bytes 8388608
  98.7 34.1 %slice-start.5 = ((s8[8388608]{0:T(1024)(128)(4,1)}), s8[4194304]{0:T(1024)(128)(4,1)S(1)}, s32[]{:S(2)}) async-start(s8[8388608]{0:T(1024)(128)(4,1)} %bitcast.207), calls=%async_computation.8 | async-start | bytes 8388608
  178.6 460.1 %reduce-scatter.2.cloned.1.call-start = ((), (), s32[]{:S(2)}) async-start(), calls=%async_computation.2 | async-start | bytes 1310720 | tf_op jit(solution)/shard_map/reduce_scatter | solution.py:1922
  180.5 320.8 %collective-permute-start.13 = (bf16[256,512]{1,0:T(8,128)(2,1)}, bf16[256,512]{1,0:T(8,128)(2,1)}, u32[]{:S(2)}, u32[]{:S(2)}) collective-permute-start(bf16[256,512]{1,0:T(8,128)(2,1)} %get-tuple-element.296), channel_id=1, source_target_pairs={{0,16},{16,0},{1,17},{17,1},{2,18},{18,2},{3,19},{19,3},{4,20},{20... | collective-permute-start | bytes 786440 | tf_op jit(solution)/shard_map/ppermute | solution.py:1566
  184.5 35.4 %copy-start.62 = (bf16[1024,2048]{1,0:T(8,128)(2,1)S(1)}, bf16[1024,2048]{1,0:T(8,128)(2,1)}, u32[]{:S(2)}) copy-start(bf16[1024,2048]{1,0:T(8,128)(2,1)} %copy-done.61) | copy-start | bytes 12582916
  191.2 30.0 %copy-start.4 = (f32[256,2688]{1,0:T(8,128)}, f32[256,2688]{1,0:T(8,128)S(1)}, u32[]{:S(2)}) copy-start(f32[256,2688]{1,0:T(8,128)S(1)} %fusion.53.proj_ref) | copy-start | bytes 8257540
  219.9 42.6 %slice-start.2 = ((s8[8388608]{0:T(1024)(128)(4,1)}), s8[4194304]{0:T(1024)(128)(4,1)S(1)}, s32[]{:S(2)}) async-start(s8[8388608]{0:T(1024)(128)(4,1)} %bitcast.202), calls=%async_computation.5 | async-start | bytes 8388608
  221.9 40.6 %slice-start.3 = ((s8[8388608]{0:T(1024)(128)(4,1)}), s8[4194304]{0:T(1024)(128)(4,1)S(1)}, s32[]{:S(2)}) async-start(s8[8388608]{0:T(1024)(128)(4,1)} %bitcast.202), calls=%async_computation.6 | async-start | bytes 8388608
  284.1 45.1 %copy-start.63 = (bf16[1024,2048]{1,0:T(8,128)(2,1)S(1)}, bf16[1024,2048]{1,0:T(8,128)(2,1)}, u32[]{:S(2)}) copy-start(bf16[1024,2048]{1,0:T(8,128)(2,1)} %copy-done.61) | copy-start | bytes 12582916
  370.4 69.6 %slice-start = ((s8[8388608]{0:T(1024)(128)(4,1)}), s8[4194304]{0:T(1024)(128)(4,1)S(1)}, s32[]{:S(2)}) async-start(s8[8388608]{0:T(1024)(128)(4,1)} %bitcast.200), calls=%async_computation.3 | async-start | bytes 8388608
  491.6 9.7 %collective-permute-start.12 = (bf16[256,2048]{1,0:T(8,128)(2,1)}, bf16[256,2048]{1,0:T(8,128)(2,1)}, u32[]{:S(2)}, u32[]{:S(2)}) collective-permute-start(bf16[256,2048]{1,0:T(8,128)(2,1)} %get-tuple-element.141), channel_id=1, source_target_pairs={{0,16},{16,0},{1,17},{17,1},{2,18},{18,2},{3,19},{19,3},{4,20},{20... | collective-permute-start | bytes 3145736 | tf_op jit(solution)/shard_map/ppermute | solution.py:1566
  492.6 135.4 %collective-permute-start.10 = (bf16[1024,768]{1,0:T(8,128)(2,1)}, bf16[1024,768]{1,0:T(8,128)(2,1)}, u32[]{:S(2)}, u32[]{:S(2)}) collective-permute-start(bf16[1024,768]{1,0:T(8,128)(2,1)} %bitcast.238), channel_id=1, source_target_pairs={{0,4},{4,0},{8,12},{12,8},{1,5},{5,1},{9,13},{13,9},{2,6},{6,2},{1... | collective-permute-start | bytes 4718600 | tf_op jit(solution)/shard_map/ppermute | solution.py:1619
  494.1 137.9 %collective-permute-start.8 = (bf16[1024,768]{1,0:T(8,128)(2,1)}, bf16[1024,768]{1,0:T(8,128)(2,1)}, u32[]{:S(2)}, u32[]{:S(2)}) collective-permute-start(bf16[1024,768]{1,0:T(8,128)(2,1)} %bitcast.237), channel_id=1, source_target_pairs={{0,8},{4,12},{8,0},{12,4},{1,9},{5,13},{9,1},{13,5},{2,10},{6,14},... | collective-permute-start | bytes 4718600 | tf_op jit(solution)/shard_map/ppermute | solution.py:1619
  554.6 7.8 %collective-permute-start.19 = (bf16[256,1024]{1,0:T(8,128)(2,1)S(1)}, bf16[256,1024]{1,0:T(8,128)(2,1)S(1)}, u32[]{:S(2)}, u32[]{:S(2)}) collective-permute-start(bf16[256,1024]{1,0:T(8,128)(2,1)S(1)} %pad_maximum_fusion.11), channel_id=1, source_target_pairs={{0,16},{16,0},{1,17},{17,1},{2,18},{18,2},{3,19},{19,3},{4,20},{20... | collective-permute-start | bytes 1572872 | tf_op jit(solution)/shard_map/ppermute | solution.py:1566
  554.7 67.9 %collective-permute-start.16 = (bf16[1024,256]{1,0:T(8,128)(2,1)}, bf16[1024,256]{1,0:T(8,128)(2,1)}, u32[]{:S(2)}, u32[]{:S(2)}) collective-permute-start(bf16[1024,256]{1,0:T(8,128)(2,1)} %bitcast.41), channel_id=1, source_target_pairs={{0,4},{4,0},{8,12},{12,8},{1,5},{5,1},{9,13},{13,9},{2,6},{6,2},{1... | collective-permute-start | bytes 1572872 | tf_op jit(solution)/shard_map/ppermute | solution.py:1619
  562.3 62.9 %collective-permute-start.14 = (bf16[1024,256]{1,0:T(8,128)(2,1)}, bf16[1024,256]{1,0:T(8,128)(2,1)}, u32[]{:S(2)}, u32[]{:S(2)}) collective-permute-start(bf16[1024,256]{1,0:T(8,128)(2,1)} %bitcast.38), channel_id=1, source_target_pairs={{0,8},{4,12},{8,0},{12,4},{1,9},{5,13},{9,1},{13,5},{2,10},{6,14},... | collective-permute-start | bytes 1572872 | tf_op jit(solution)/shard_map/ppermute | solution.py:1619
  568.4 53.4 %copy-start.79 = (bf16[512,128]{1,0:T(8,128)(2,1)S(1)}, bf16[512,128]{1,0:T(8,128)(2,1)}, u32[]{:S(2)}) copy-start(bf16[512,128]{1,0:T(8,128)(2,1)} %slice.240) | copy-start | bytes 393220
  624.5 16.0 %collective-permute-start.17 = (bf16[512,256]{1,0:T(8,128)(2,1)}, bf16[512,256]{1,0:T(8,128)(2,1)S(1)}, u32[]{:S(2)}, u32[]{:S(2)}) collective-permute-start(bf16[512,256]{1,0:T(8,128)(2,1)} %get-tuple-element.289), channel_id=1, source_target_pairs={{0,8},{4,12},{8,0},{12,4},{1,9},{5,13},{9,1},{13,5},{2,10},{6,14},... | collective-permute-start | bytes 786440 | tf_op jit(solution)/shard_map/ppermute | solution.py:1619
  627.2 13.3 %collective-permute-start.15 = (bf16[512,256]{1,0:T(8,128)(2,1)}, bf16[512,256]{1,0:T(8,128)(2,1)}, u32[]{:S(2)}, u32[]{:S(2)}) collective-permute-start(bf16[512,256]{1,0:T(8,128)(2,1)} %get-tuple-element.291), channel_id=1, source_target_pairs={{0,4},{4,0},{8,12},{12,8},{1,5},{5,1},{9,13},{13,9},{2,6},{6,2},{1... | collective-permute-start | bytes 786440 | tf_op jit(solution)/shard_map/ppermute | solution.py:1619
  630.9 17.6 %collective-permute-start.11 = (bf16[512,768]{1,0:T(8,128)(2,1)}, bf16[512,768]{1,0:T(8,128)(2,1)S(1)}, u32[]{:S(2)}, u32[]{:S(2)}) collective-permute-start(bf16[512,768]{1,0:T(8,128)(2,1)} %get-tuple-element.262), channel_id=1, source_target_pairs={{0,8},{4,12},{8,0},{12,4},{1,9},{5,13},{9,1},{13,5},{2,10},{6,14},... | collective-permute-start | bytes 2359304 | tf_op jit(solution)/shard_map/ppermute | solution.py:1619
  634.6 16.4 %collective-permute-start.9 = (bf16[512,768]{1,0:T(8,128)(2,1)S(1)}, bf16[512,768]{1,0:T(8,128)(2,1)S(1)}, u32[]{:S(2)}, u32[]{:S(2)}) collective-permute-start(bf16[512,768]{1,0:T(8,128)(2,1)S(1)} %get-tuple-element.264), channel_id=1, source_target_pairs={{0,4},{4,0},{8,12},{12,8},{1,5},{5,1},{9,13},{13,9},{2,6},{6,2},{1... | collective-permute-start | bytes 2359304 | tf_op jit(solution)/shard_map/ppermute | solution.py:1619
  (88 other events, 423.5 us)
Sparse Core Ops, SparseCore 0:
  178.7 32.9 all-gather.1
  492.7 24.4 reduce-scatter.1

commit v5 on v4

--- a/solution.py
+++ b/solution.py
@@ -1608,7 +1608,7 @@
     width = gate_up.shape[1] // 2
     gate_pre, upward = gate_up[:, :width], gate_up[:, width:]
     product = (jax.nn.silu(gate_pre) * upward).astype(bf16)
-    return matmul(product, weights.down), gate_pre, upward, product
+    return matmul(product, weights.down), gate_pre.astype(bf16), upward.astype(bf16), product
 
 
 def ctx_bits():
@@ -1704,7 +1704,7 @@
 def layer_backward(weights, saved, d_out, d_low, values_in, layout, last, before):
     grads = types.SimpleNamespace()
     d_product = matmul_nt(d_low, weights.down)
-    gate_pre, upward = saved.gate_pre, saved.upward
+    gate_pre, upward = saved.gate_pre.astype(f32), saved.upward.astype(f32)
     gate_sig = jax.nn.sigmoid(gate_pre)
     d_gate = d_product * upward * gate_sig * (1.0 + gate_pre * (1.0 - gate_sig))
     d_upward = d_product * gate_pre * gate_sig

time: 726 us -> 726 us (level)
  no operation moved by 1% of the time
where the time goes in v5:
time: 726 us; the launch traced here: 715 us
  Pallas kernels  459 us (63%)
  local copies, waits for them, and re-layouts  94.4 us (13%)
  matrix products  76.1 us (10%)
  other arithmetic  33.6 us (5%)
  starting transfers between devices  20 us (3%)
  between operations  17.4 us (2%)
  waiting for transfers between devices  14.3 us (2%)
    pallas_call x7, Pallas kernels, summed(): pl.pallas_call(functools.partial(kernel, n, CHUNKS, LAG), out_shape=outs,...  304 us
    pallas_call x4, Pallas kernels, mixer_call(): pl.pallas_call(functools.partial(kernel, count, widths, heads), out_shape...  127 us
    unnamed x212, local copies, waits for them, and re-layouts  69 us
    dot_general x8, matrix products, matmul_nt(): lax.dot_general(left, right, (((1,), (1,)), ((), ())), preferred_element_...  40.9 us
    dot_general x8, matrix products, matmul(): return jnp.dot(left, right, preferred_element_type=f32)  28.4 us
    pallas_call x1, Pallas kernels, finish(): pl.pallas_call(functools.partial(finish_kernel, count, places, widths), o...  27.5 us
  transfers between devices with their start and end apart: 22, of which 3 were waited for; matrix products, arithmetic and copies ran while one was open for 20% of the time, Pallas kernels for 60%

profile of v5, /device:TPU:0, one launch (start us, length us, event | category | flops | bytes accessed | tf_op | source)
XLA Modules:
  0.0 714.7 jit_solution(11144634103109150412)
XLA Ops:
  9.1 5.0 collective-permute-start
  18.1 6.7 copy.55
  37.9 10.3 %copy.58 = bf16[256,8,2,1024]{3,1,2,0:T(8,128)(2,1)} copy(bf16[256,8,2,1024]{3,2,1,0:T(2,128)(2,1)} %bitcast.211) | data formatting | bytes 16777216
  48.8 4.5 pad_maximum_fusion.refs_1_
  63.0 7.8 %fusion.4.proj_ref = f32[256,2688]{1,0:T(8,128)S(1)} fusion(bf16[256,2048]{1,0:T(8,128)(2,1)} %fusion.10, bf16[2048,2688]{1,0:T(8,128)(2,1)} %constant_dynamic-update-slice_fusion.refs_0_, bf16[2048,2688]{1,0:T(8,128)(2,1)} %collective-permute-done.4.refs_2_, pred[]{:T(512)S(6)} %eq.54), kind=kOutput, calls=%fused_computation.5 | convolution fusion | flops 2824077312 | bytes 25821184 | tf_op jit(solution)/shard_map/dot_general | solution.py:1554
  70.8 26.1 %mixer5.2 = (bf16[256,1024]{1,0:T(8,128)(2,1)S(1)}, f32[256,768]{1,0:T(8,128)S(1)}, bf16[768,256]{1,0:T(8,128)(2,1)S(1)}, bf16[1024,256]{1,0:T(8,128)(2,1)S(1)}, f32[4,16,256]{2,1,0:T(8,128)S(1)}) custom-call(f32[256,2688]{1,0:T(8,128)S(1)} %fusion.4.proj_ref, f32[8,128]{1,0:T(8,128)S(1)} %pad.23.vec_ref, f32[1,768]{1,0:T(1,128)S(1)} %broadcast_in_dim_reshape.13.skip_ref, ...), custom_call_target="tpu_custom_call" | custom-call | bytes 20971520 | tf_op jit(solution)/shard_map/mixer5/pallas_call | solution.py:1165
  98.7 34.0 %line_sum1.1 = (f32[256,2048]{1,0:T(8,128)S(1)}, bf16[256,2048]{1,0:T(8,128)(2,1)S(1)}, bf16[2048,2688]{1,0:T(8,128)(2,1)}, bf16[1024,2048]{1,0:T(8,128)(2,1)S(1)}) custom-call(f32[256,2048]{1,0:T(8,128)S(1)} %fusion.18.p_ref, bf16[256,2048]{1,0:T(8,128)(2,1)S(1)} %constant_dynamic-update-slice_fusion.1.h_ref.v_ref, f32[1,2048]{1,0:T(1,128)S(1)} %bitcast.194, ...), custom_call_target="tpu_custom_call" | custom-call | bytes 20971520 | tf_op jit(solution)/shard_map/line_sum1/pallas_call | solution.py:561
  135.6 4.0 fusion.5.p_ref
  139.6 31.6 %line_sum2.1 = (bf16[256,2048]{1,0:T(8,128)(2,1)S(1)}, bf16[256,2048]{1,0:T(8,128)(2,1)S(1)}, bf16[2048,2048]{1,0:T(8,128)(2,1)S(1)}, bf16[1024,2048]{1,0:T(8,128)(2,1)S(1)}) custom-call(f32[256,2048]{1,0:T(8,128)S(1)} %fusion.5.p_ref, f32[256,2048]{1,0:T(8,128)S(1)} %get-tuple-element.106.h_ref.refs_2_, f32[1,2048]{1,0:T(1,128)S(1)} %bitcast.196, ...), custom_call_target="tpu_custom_call" | custom-call | bytes 20971520 | tf_op jit(solution)/shard_map/line_sum2/pallas_call | solution.py:561
  180.5 4.0 collective-permute-start.13
  184.5 6.7 fusion.69.proj_ref
  191.2 28.7 %mixer5.3 = (bf16[256,1024]{1,0:T(8,128)(2,1)S(1)}, f32[256,768]{1,0:T(8,128)S(1)}, bf16[768,256]{1,0:T(8,128)(2,1)S(1)}, bf16[1024,256]{1,0:T(8,128)(2,1)S(1)}, f32[4,16,256]{2,1,0:T(8,128)S(1)}) custom-call(f32[256,2688]{1,0:T(8,128)S(1)} %fusion.69.proj_ref, f32[8,128]{1,0:T(8,128)S(1)} %pad.25.vec_ref, f32[1,768]{1,0:T(1,128)S(1)} %broadcast_in_dim_reshape.14.skip_ref, ...), custom_call_target="tpu_custom_call" | custom-call | bytes 20971520 | tf_op jit(solution)/shard_map/mixer5/pallas_call | solution.py:1165
  221.9 32.9 %line_sum9.1 = (f32[256,2048]{1,0:T(8,128)S(1)}, bf16[256,2048]{1,0:T(8,128)(2,1)S(1)}, bf16[2048,2048]{1,0:T(8,128)(2,1)S(1)}, bf16[1024,2048]{1,0:T(8,128)(2,1)S(1)}) custom-call(f32[256,2048]{1,0:T(8,128)S(1)} %fusion.70.p_ref, bf16[256,2048]{1,0:T(8,128)(2,1)S(1)} %copy-done.8, f32[1,2048]{1,0:T(1,128)S(1)} %bitcast.198, bf16[2048,2048]{1,0:T(8,128)(2,1)} %bitcast.206, ...), custom_call_target="tpu_custom_call" | custom-call | bytes 20971520 | tf_op jit(solution)/shard_map/line_sum9/pallas_call | solution.py:561
  256.1 3.3 copy-done.58
  265.0 4.2 fusion.28
  269.3 7.2 %fusion.66.refs_0_ = f32[256,2048]{1,0:T(8,128)} fusion(bf16[2048,2048]{1,0:T(8,128)(2,1)} %copy-done.59, bf16[256,1024]{1,0:T(8,128)(2,1)S(1)} %get-tuple-element.269, bf16[256,1024]{1,0:T(8,128)(2,1)S(1)} %get-tuple-element.268), kind=kOutput, calls=%fused_computation.205 | convolution fusion | flops 2149580800 | bytes 11534336 | tf_op jit(solution)/shard_map/dot_general | solution.py:1558
  284.2 43.6 %line_sum3.1 = (f32[256,2048]{1,0:T(8,128)S(1)}, bf16[256,2048]{1,0:T(8,128)(2,1)S(1)}, f32[8,2048]{1,0:T(8,128)S(1)}, bf16[2,512,512]{2,1,0:T(8,128)(2,1)S(1)},...) custom-call(f32[256,2048]{1,0:T(8,128)S(1)} %copy-done.14, ...), custom_call_target="tpu_custom_call" | custom-call | bytes 20971520 | tf_op jit(solution)/shard_map/line_sum3/pallas_call | solution.py:561
  334.0 27.1 %mixer6.2 = (bf16[256,2688]{1,0:T(8,128)(2,1)S(1)}, f32[8,128]{1,0:T(8,128)S(1)}) custom-call(f32[256,2688]{1,0:T(8,128)S(1)} %copy-done.5, f32[8,128]{1,0:T(8,128)S(1)} %pad.25.vec_ref, f32[1,768]{1,0:T(1,128)S(1)} %broadcast_in_dim_reshape.14.skip_ref, f32[256,8]{1,0:T(8,128)S(1)} %pad.24.tok_ref, f32[2,1024]{1,0:T(2,128)S(1)} %pad_maximum_fusion.14.key_ref, ...), custom_call_target="tpu_custom_call" | custom-call | bytes 20971520 | tf_op jit(solution)/shard_map/mixer6/pallas_call | solution.py:1165
  361.2 9.1 %fusion.73.refs_0_ = f32[256,2048]{1,0:T(8,128)} fusion(bf16[256,2688]{1,0:T(8,128)(2,1)S(1)} %get-tuple-element.124.refs_7_, bf16[2048,2688]{1,0:T(8,128)(2,1)} %get-tuple-element.109), kind=kOutput, calls=%fused_computation.212 | convolution fusion | flops 2818572288 | bytes 14483456 | tf_op jit(solution)/shard_map/dot_general | solution.py:1558
  370.4 63.0 %line_sum4.1 = (f32[256,2048]{1,0:T(8,128)}, bf16[256,2048]{1,0:T(8,128)(2,1)}, f32[8,2048]{1,0:T(8,128)S(1)}, bf16[256,1024]{1,0:T(8,128)(2,1)S(1)}, bf16[2,512...) custom-call(f32[256,2048]{1,0:T(8,128)} %fusion.73.refs_0_, ...), custom_call_target="tpu_custom_call" | custom-call | bytes 20971520 | tf_op jit(solution)/shard_map/line_sum4/pallas_call | solution.py:561
  433.5 5.4 fusion.36
  440.0 3.7 fusion.65.refs_0_
  443.7 48.4 %line_sum10.1 = (f32[256,2048]{1,0:T(8,128)}, bf16[256,2048]{1,0:T(8,128)(2,1)}, f32[8,2048]{1,0:T(8,128)S(1)}, bf16[2,512,768]{2,1,0:T(8,128)(2,1)}, bf16[2,512...) custom-call(f32[256,2048]{1,0:T(8,128)} %fusion.65.refs_0_, ...), custom_call_target="tpu_custom_call" | custom-call | bytes 20971520 | tf_op jit(solution)/shard_map/line_sum10/pallas_call | solution.py:561
  495.9 3.9 fusion.17.d_both_ref
  507.3 45.6 %mixer6.3 = (bf16[256,2688]{1,0:T(8,128)(2,1)S(1)}, f32[8,128]{1,0:T(8,128)S(1)}) custom-call(f32[256,2688]{1,0:T(8,128)S(1)} %copy-done.3, f32[8,128]{1,0:T(8,128)S(1)} %pad.23.vec_ref, f32[1,768]{1,0:T(1,128)S(1)} %broadcast_in_dim_reshape.13.skip_ref, f32[256,8]{1,0:T(8,128)S(1)} %pad.24.tok_ref, f32[2,1024]{1,0:T(2,128)S(1)} %pad_maximum_fusion.14.key_ref, ...), custom_call_target="tpu_custom_call" | custom-call | bytes 20971520 | tf_op jit(solution)/shard_map/mixer6/pallas_call | solution.py:1165
  556.7 6.1 fusion.3.p_ref
  563.0 3.9 convolution_convert_fusion
  568.9 50.5 %line_sum7.1 = (f32[256,2048]{1,0:T(8,128)S(1)}, bf16[256,2048]{1,0:T(8,128)(2,1)}, f32[8,2048]{1,0:T(8,128)S(1)}, bf16[256,1024]{1,0:T(8,128)(2,1)S(1)}, bf16[5...) custom-call(f32[256,2048]{1,0:T(8,128)S(1)} %fusion.3.p_ref, bf16[256,1024]{1,0:T(8,128)(2,1)S(1)} %get-tuple-element.279.q_ref, ...), custom_call_target="tpu_custom_call" | custom-call | bytes 20971520 | tf_op jit(solution)/shard_map/line_sum7/pallas_call | solution.py:561
  641.1 8.6 %collective-permute-done.11.refs_3_ = bf16[512,768]{1,0:T(8,128)(2,1)S(1)} collective-permute-done((bf16[512,768]{1,0:T(8,128)(2,1)}, bf16[512,768]{1,0:T(8,128)(2,1)S(1)}, u32[]{:S(2)}, u32[]{:S(2)}) %collective-permute-start.11) | collective-permute-done | bytes 786464 | tf_op jit(solution)/shard_map/ppermute | solution.py:1619
  653.5 27.5 %finish.1 = (bf16[512,256]{1,0:T(8,128)(2,1)}, f32[2,512,768]{2,1,0:T(8,128)}, f32[2,512,1024]{2,1,0:T(8,128)}, bf16[1024,512]{1,0:T(8,128)(2,1)}, bf16[1024,512...) custom-call(bf16[512,768]{1,0:T(8,128)(2,1)} %get-tuple-element.265., ...), custom_call_target="tpu_custom_call" | custom-call | bytes 20971520 | tf_op jit(solution)/shard_map/finish/pallas_call | solution.py:1535
  685.3 7.6 %copy.53 = f32[1,512,2,1024]{3,2,1,0:T(2,128)} copy(f32[1,512,2,1024]{3,1,2,0:T(8,128)} %bitcast.214) | data formatting | bytes 8388608
  692.9 4.1 copy.51
  (366 shorter events, 122.3 us)
Async XLA Ops:
  7.2 257.7 %all-gather.2.cloned.1.call-start = ((), (), s32[]{:S(2)}) async-start(), calls=%async_computation.1 | async-start | bytes 1310720 | tf_op jit(solution)/shard_map/all_gather | solution.py:1885
  9.1 24.0 %collective-permute-start = (bf16[64,2048]{1,0:T(8,128)(2,1)}, bf16[64,2048]{1,0:T(8,128)(2,1)}, u32[]{:S(2)}, u32[]{:S(2)}) collective-permute-start(bf16[64,2048]{1,0:T(8,128)(2,1)} %get-tuple-element.253), channel_id=1, source_target_pairs={{0,3},{1,2},{2,1},{3,0},{4,7},{5,6},{6,5},{7,4},{8,11},{9,10},{10,... | collective-permute-start | bytes 786440 | tf_op jit(solution)/shard_map/ppermute | solution.py:583
  14.1 22.6 %collective-permute-start.1 = (bf16[64,2048]{1,0:T(8,128)(2,1)}, bf16[64,2048]{1,0:T(8,128)(2,1)}, u32[]{:S(2)}, u32[]{:S(2)}) collective-permute-start(bf16[64,2048]{1,0:T(8,128)(2,1)} %get-tuple-element.253), channel_id=1, source_target_pairs={{0,2},{1,3},{2,0},{3,1},{4,6},{5,7},{6,4},{7,5},{8,10},{9,11},{10,... | collective-permute-start | bytes 786440 | tf_op jit(solution)/shard_map/ppermute | solution.py:583
  14.1 23.6 %collective-permute-start.2 = (bf16[64,2048]{1,0:T(8,128)(2,1)}, bf16[64,2048]{1,0:T(8,128)(2,1)S(1)}, u32[]{:S(2)}, u32[]{:S(2)}) collective-permute-start(bf16[64,2048]{1,0:T(8,128)(2,1)} %get-tuple-element.253), channel_id=1, source_target_pairs={{0,1},{1,0},{2,3},{3,2},{4,5},{5,4},{6,7},{7,6},{8,9},{9,8},{10,11... | collective-permute-start | bytes 786440 | tf_op jit(solution)/shard_map/ppermute | solution.py:583
  37.8 25.2 %collective-permute-start.4 = (bf16[2048,2688]{1,0:T(8,128)(2,1)}, bf16[2048,2688]{1,0:T(8,128)(2,1)}, u32[]{:S(2)}, u32[]{:S(2)}) collective-permute-start(bf16[2048,2688]{1,0:T(8,128)(2,1)} %constant_dynamic-update-slice_fusion.refs_0_), channel_id=1, source_target_pairs={{0,16},{16,0},{1,17},{17,1},{2,18},{18,2},{3,19},{19,3},{4,20},{20... | collective-permute-start | bytes 33030152 | tf_op jit(solution)/shard_map/ppermute | solution.py:1566
  48.2 84.6 %collective-permute-start.6 = (bf16[2048,2048]{1,0:T(8,128)(2,1)}, bf16[2048,2048]{1,0:T(8,128)(2,1)}, u32[]{:S(2)}, u32[]{:S(2)}) collective-permute-start(bf16[2048,2048]{1,0:T(8,128)(2,1)} %bitcast.204), channel_id=1, source_target_pairs={{0,16},{16,0},{1,17},{17,1},{2,18},{18,2},{3,19},{19,3},{4,20},{20... | collective-permute-start | bytes 25165832 | tf_op jit(solution)/shard_map/ppermute | solution.py:1566
  48.8 9.8 %collective-permute-start.3 = (f32[4132]{0:T(1024)S(1)}, f32[4132]{0:T(1024)S(1)}, u32[]{:S(2)}, u32[]{:S(2)}) collective-permute-start(f32[4132]{0:T(1024)S(1)} %concatenate.57), channel_id=1, source_target_pairs={{0,16},{16,0},{1,17},{17,1},{2,18},{18,2},{3,19},{19,3},{4,20},{20... | collective-permute-start | bytes 49592 | tf_op jit(solution)/shard_map/ppermute | solution.py:1566
  53.4 43.6 %collective-permute-start.5 = (bf16[1024,2048]{1,0:T(8,128)(2,1)}, bf16[1024,2048]{1,0:T(8,128)(2,1)}, u32[]{:S(2)}, u32[]{:S(2)}) collective-permute-start(bf16[1024,2048]{1,0:T(8,128)(2,1)} %pad_maximum_fusion.refs_1_), channel_id=1, source_target_pairs={{0,16},{16,0},{1,17},{17,1},{2,18},{18,2},{3,19},{19,3},{4,20},{20... | collective-permute-start | bytes 12582920 | tf_op jit(solution)/shard_map/ppermute | solution.py:1566
  53.8 81.7 %collective-permute-start.7 = (bf16[1024,2048]{1,0:T(8,128)(2,1)}, bf16[1024,2048]{1,0:T(8,128)(2,1)}, u32[]{:S(2)}, u32[]{:S(2)}) collective-permute-start(bf16[1024,2048]{1,0:T(8,128)(2,1)} %bitcast.19.refs_1_), channel_id=1, source_target_pairs={{0,16},{16,0},{1,17},{17,1},{2,18},{18,2},{3,19},{19,3},{4,20},{20... | collective-permute-start | bytes 12582920 | tf_op jit(solution)/shard_map/ppermute | solution.py:1566
  60.9 502.0 %collective-permute-start.18 = (bf16[256,2048]{1,0:T(8,128)(2,1)}, bf16[256,2048]{1,0:T(8,128)(2,1)}, u32[]{:S(2)}, u32[]{:S(2)}) collective-permute-start(bf16[256,2048]{1,0:T(8,128)(2,1)} %fusion.10), channel_id=1, source_target_pairs={{0,16},{16,0},{1,17},{17,1},{2,18},{18,2},{3,19},{19,3},{4,20},{20... | collective-permute-start | bytes 3145736 | tf_op jit(solution)/shard_map/ppermute | solution.py:1566
  63.0 34.0 %copy-start.68 = (bf16[1,768,2048]{2,1,0:T(8,128)(2,1)S(1)}, bf16[1,768,2048]{2,1,0:T(8,128)(2,1)}, u32[]{:S(2)}) copy-start(bf16[1,768,2048]{2,1,0:T(8,128)(2,1)} %param.30) | copy-start | bytes 9437188
  97.0 35.8 %slice-start.4 = ((s8[8388608]{0:T(1024)(128)(4,1)}), s8[4194304]{0:T(1024)(128)(4,1)S(1)}, s32[]{:S(2)}) async-start(s8[8388608]{0:T(1024)(128)(4,1)} %bitcast.207), calls=%async_computation.7 | async-start | bytes 8388608
  98.7 34.1 %slice-start.5 = ((s8[8388608]{0:T(1024)(128)(4,1)}), s8[4194304]{0:T(1024)(128)(4,1)S(1)}, s32[]{:S(2)}) async-start(s8[8388608]{0:T(1024)(128)(4,1)} %bitcast.207), calls=%async_computation.8 | async-start | bytes 8388608
  178.6 460.6 %reduce-scatter.2.cloned.1.call-start = ((), (), s32[]{:S(2)}) async-start(), calls=%async_computation.2 | async-start | bytes 1310720 | tf_op jit(solution)/shard_map/reduce_scatter | solution.py:1922
  180.5 321.2 %collective-permute-start.13 = (bf16[256,512]{1,0:T(8,128)(2,1)}, bf16[256,512]{1,0:T(8,128)(2,1)}, u32[]{:S(2)}, u32[]{:S(2)}) collective-permute-start(bf16[256,512]{1,0:T(8,128)(2,1)} %get-tuple-element.296), channel_id=1, source_target_pairs={{0,16},{16,0},{1,17},{17,1},{2,18},{18,2},{3,19},{19,3},{4,20},{20... | collective-permute-start | bytes 786440 | tf_op jit(solution)/shard_map/ppermute | solution.py:1566
  184.5 35.4 %copy-start.62 = (bf16[1024,2048]{1,0:T(8,128)(2,1)S(1)}, bf16[1024,2048]{1,0:T(8,128)(2,1)}, u32[]{:S(2)}) copy-start(bf16[1024,2048]{1,0:T(8,128)(2,1)} %copy-done.61) | copy-start | bytes 12582916
  191.2 30.0 %copy-start.4 = (f32[256,2688]{1,0:T(8,128)}, f32[256,2688]{1,0:T(8,128)S(1)}, u32[]{:S(2)}) copy-start(f32[256,2688]{1,0:T(8,128)S(1)} %fusion.69.proj_ref) | copy-start | bytes 8257540
  219.9 42.6 %slice-start.2 = ((s8[8388608]{0:T(1024)(128)(4,1)}), s8[4194304]{0:T(1024)(128)(4,1)S(1)}, s32[]{:S(2)}) async-start(s8[8388608]{0:T(1024)(128)(4,1)} %bitcast.202), calls=%async_computation.5 | async-start | bytes 8388608
  221.9 40.6 %slice-start.3 = ((s8[8388608]{0:T(1024)(128)(4,1)}), s8[4194304]{0:T(1024)(128)(4,1)S(1)}, s32[]{:S(2)}) async-start(s8[8388608]{0:T(1024)(128)(4,1)} %bitcast.202), calls=%async_computation.6 | async-start | bytes 8388608
  284.2 45.1 %copy-start.63 = (bf16[1024,2048]{1,0:T(8,128)(2,1)S(1)}, bf16[1024,2048]{1,0:T(8,128)(2,1)}, u32[]{:S(2)}) copy-start(bf16[1024,2048]{1,0:T(8,128)(2,1)} %copy-done.61) | copy-start | bytes 12582916
  370.4 69.5 %slice-start = ((s8[8388608]{0:T(1024)(128)(4,1)}), s8[4194304]{0:T(1024)(128)(4,1)S(1)}, s32[]{:S(2)}) async-start(s8[8388608]{0:T(1024)(128)(4,1)} %bitcast.200), calls=%async_computation.3 | async-start | bytes 8388608
  492.1 9.6 %collective-permute-start.12 = (bf16[256,2048]{1,0:T(8,128)(2,1)}, bf16[256,2048]{1,0:T(8,128)(2,1)}, u32[]{:S(2)}, u32[]{:S(2)}) collective-permute-start(bf16[256,2048]{1,0:T(8,128)(2,1)} %get-tuple-element.141), channel_id=1, source_target_pairs={{0,16},{16,0},{1,17},{17,1},{2,18},{18,2},{3,19},{19,3},{4,20},{20... | collective-permute-start | bytes 3145736 | tf_op jit(solution)/shard_map/ppermute | solution.py:1566
  493.1 135.6 %collective-permute-start.10 = (bf16[1024,768]{1,0:T(8,128)(2,1)}, bf16[1024,768]{1,0:T(8,128)(2,1)}, u32[]{:S(2)}, u32[]{:S(2)}) collective-permute-start(bf16[1024,768]{1,0:T(8,128)(2,1)} %bitcast.238), channel_id=1, source_target_pairs={{0,4},{4,0},{8,12},{12,8},{1,5},{5,1},{9,13},{13,9},{2,6},{6,2},{1... | collective-permute-start | bytes 4718600 | tf_op jit(solution)/shard_map/ppermute | solution.py:1619
  493.7 139.0 %collective-permute-start.8 = (bf16[1024,768]{1,0:T(8,128)(2,1)}, bf16[1024,768]{1,0:T(8,128)(2,1)}, u32[]{:S(2)}, u32[]{:S(2)}) collective-permute-start(bf16[1024,768]{1,0:T(8,128)(2,1)} %bitcast.237), channel_id=1, source_target_pairs={{0,8},{4,12},{8,0},{12,4},{1,9},{5,13},{9,1},{13,5},{2,10},{6,14},... | collective-permute-start | bytes 4718600 | tf_op jit(solution)/shard_map/ppermute | solution.py:1619
  554.2 8.7 %collective-permute-start.19 = (bf16[256,1024]{1,0:T(8,128)(2,1)S(1)}, bf16[256,1024]{1,0:T(8,128)(2,1)S(1)}, u32[]{:S(2)}, u32[]{:S(2)}) collective-permute-start(bf16[256,1024]{1,0:T(8,128)(2,1)S(1)} %pad_maximum_fusion.11), channel_id=1, source_target_pairs={{0,16},{16,0},{1,17},{17,1},{2,18},{18,2},{3,19},{19,3},{4,20},{20... | collective-permute-start | bytes 1572872 | tf_op jit(solution)/shard_map/ppermute | solution.py:1566
  554.3 68.8 %collective-permute-start.16 = (bf16[1024,256]{1,0:T(8,128)(2,1)}, bf16[1024,256]{1,0:T(8,128)(2,1)}, u32[]{:S(2)}, u32[]{:S(2)}) collective-permute-start(bf16[1024,256]{1,0:T(8,128)(2,1)} %bitcast.41), channel_id=1, source_target_pairs={{0,4},{4,0},{8,12},{12,8},{1,5},{5,1},{9,13},{13,9},{2,6},{6,2},{1... | collective-permute-start | bytes 1572872 | tf_op jit(solution)/shard_map/ppermute | solution.py:1619
  562.9 62.9 %collective-permute-start.14 = (bf16[1024,256]{1,0:T(8,128)(2,1)}, bf16[1024,256]{1,0:T(8,128)(2,1)}, u32[]{:S(2)}, u32[]{:S(2)}) collective-permute-start(bf16[1024,256]{1,0:T(8,128)(2,1)} %bitcast.38), channel_id=1, source_target_pairs={{0,8},{4,12},{8,0},{12,4},{1,9},{5,13},{9,1},{13,5},{2,10},{6,14},... | collective-permute-start | bytes 1572872 | tf_op jit(solution)/shard_map/ppermute | solution.py:1619
  568.9 53.4 %copy-start.79 = (bf16[512,128]{1,0:T(8,128)(2,1)S(1)}, bf16[512,128]{1,0:T(8,128)(2,1)}, u32[]{:S(2)}) copy-start(bf16[512,128]{1,0:T(8,128)(2,1)} %slice.240) | copy-start | bytes 393220
  625.0 16.0 %collective-permute-start.17 = (bf16[512,256]{1,0:T(8,128)(2,1)}, bf16[512,256]{1,0:T(8,128)(2,1)S(1)}, u32[]{:S(2)}, u32[]{:S(2)}) collective-permute-start(bf16[512,256]{1,0:T(8,128)(2,1)} %get-tuple-element.289), channel_id=1, source_target_pairs={{0,8},{4,12},{8,0},{12,4},{1,9},{5,13},{9,1},{13,5},{2,10},{6,14},... | collective-permute-start | bytes 786440 | tf_op jit(solution)/shard_map/ppermute | solution.py:1619
  627.8 13.3 %collective-permute-start.15 = (bf16[512,256]{1,0:T(8,128)(2,1)}, bf16[512,256]{1,0:T(8,128)(2,1)}, u32[]{:S(2)}, u32[]{:S(2)}) collective-permute-start(bf16[512,256]{1,0:T(8,128)(2,1)} %get-tuple-element.291), channel_id=1, source_target_pairs={{0,4},{4,0},{8,12},{12,8},{1,5},{5,1},{9,13},{13,9},{2,6},{6,2},{1... | collective-permute-start | bytes 786440 | tf_op jit(solution)/shard_map/ppermute | solution.py:1619
  631.7 18.0 %collective-permute-start.11 = (bf16[512,768]{1,0:T(8,128)(2,1)}, bf16[512,768]{1,0:T(8,128)(2,1)S(1)}, u32[]{:S(2)}, u32[]{:S(2)}) collective-permute-start(bf16[512,768]{1,0:T(8,128)(2,1)} %get-tuple-element.262), channel_id=1, source_target_pairs={{0,8},{4,12},{8,0},{12,4},{1,9},{5,13},{9,1},{13,5},{2,10},{6,14},... | collective-permute-start | bytes 2359304 | tf_op jit(solution)/shard_map/ppermute | solution.py:1619
  635.4 17.2 %collective-permute-start.9 = (bf16[512,768]{1,0:T(8,128)(2,1)S(1)}, bf16[512,768]{1,0:T(8,128)(2,1)S(1)}, u32[]{:S(2)}, u32[]{:S(2)}) collective-permute-start(bf16[512,768]{1,0:T(8,128)(2,1)S(1)} %get-tuple-element.264), channel_id=1, source_target_pairs={{0,4},{4,0},{8,12},{12,8},{1,5},{5,1},{9,13},{13,9},{2,6},{6,2},{1... | collective-permute-start | bytes 2359304 | tf_op jit(solution)/shard_map/ppermute | solution.py:1619
  (88 other events, 426.4 us)
Sparse Core Ops, SparseCore 0:
  178.7 32.9 all-gather.1
  493.3 24.3 reduce-scatter.1
